TPU v7x, 128 devices: a whole 4x4x4 slice. The times are simulated.
128 devices in a mesh: tile: 64 (over z, x, y_lo, core), chan: 2 (over y_hi).
Axes of the slice: x: 4, y: 4 (y_hi: 2, y_lo: 2; y = y_hi * 2 + y_lo), z: 4, core: 2. Of those that a mesh axis runs over, the one named last changes fastest.
Arguments:
- inputs: bfloat16 [128, 64, 4096], P('tile', 'chan'), may hold values from -6 to 6
- gluing: int32 [128, 4, 3], P('tile'), may hold values from 0 to 127, as said below
- conv_weight: bfloat16 [64, 64, 3, 3], replicated, may hold values from -0.25 to 0.25
- level_weight: bfloat16 [128, 64, 2, 2], replicated, may hold values from -0.375 to 0.375
- cotangent: bfloat16 [128, 128, 1024], P('tile', 'chan'), may hold values from -6 to 6
Outputs:
- level: bfloat16 [128, 128, 1024], P('tile', 'chan')
- grad_inputs: bfloat16 [128, 64, 4096], P('tile', 'chan')
- grad_conv: float32 [64, 64, 3, 3], P(None, 'chan')
- grad_level: float32 [128, 64, 2, 2], P(None, 'chan')
Inputs may be any that keep to these rules, and one draw needn't show every extreme that they name: Entry [t, s] = (u, r, f) with r in 0..3 and f in 0..1 says that side s of tile t is glued to side r of tile u; the gluing is symmetric: entry [u, r] is (t, s, f), and no side is glued to itself.
All inputs are finite; a program needn't handle non-finite values.
Results may differ from a plain program's by a relative error of at most 0.005.
Values may be sent and summed in bfloat16 or wider, within the bound.
No kernel may reach another device: no remote copies, remote signals or barrier semaphores. Data moves between devices by JAX's collectives and lax.ppermute only.
A program may use at most 128 MiB of HBM per device.

v0:
```python
import jax
import jax.numpy as jnp
from jax import lax
from jax.sharding import PartitionSpec as P

S = 64


def edge_strips(source):
    return jnp.stack(
        [source[:, :, 0, :], source[:, :, -1, :], source[:, :, :, 0], source[:, :, :, -1]], axis=1
    )


def border_strips(padded):
    return jnp.stack(
        [
            padded[:, :, 0, 1:-1],
            padded[:, :, -1, 1:-1],
            padded[:, :, 1:-1, 0],
            padded[:, :, 1:-1, -1],
        ],
        axis=1,
    )


def orient(strips, gluing):
    return jnp.where(gluing[:, :, 2][:, :, None, None] == 1, strips[..., ::-1], strips)


def make_picker(gluing):
    target = gluing[:, :, 0] * 4 + gluing[:, :, 1]

    def picker(current, received, first_row):
        strip_count = received.shape[0] * 4
        received_rows = received.reshape((strip_count,) + received.shape[2:])
        inside = (target >= 0) & (target < strip_count)
        chosen = jnp.take(received_rows, jnp.clip(target, 0, strip_count - 1), axis=0)
        return jnp.where(inside[:, :, None, None], chosen, current)

    return picker


def assemble(source, halo_cells):
    tile_count, chan_count = (source.shape[0], source.shape[1])
    corner = jnp.zeros((tile_count, chan_count, 1), source.dtype)
    top_row = jnp.concatenate([corner, halo_cells[:, 0], corner], axis=2)[:, :, None, :]
    low_row = jnp.concatenate([corner, halo_cells[:, 1], corner], axis=2)[:, :, None, :]
    middle = jnp.concatenate(
        [halo_cells[:, 2][:, :, :, None], source, halo_cells[:, 3][:, :, :, None]], axis=3
    )
    return jnp.concatenate([top_row, middle, low_row], axis=2)


def conv_three(padded, weight):
    extent = padded.shape[2] - 2
    summed = None
    for row_tap in range(3):
        for col_tap in range(3):
            product_term = jnp.einsum(
                "oc,ncxy->noxy",
                weight[:, :, row_tap, col_tap],
                padded[:, :, row_tap : row_tap + extent, col_tap : col_tap + extent],
                preferred_element_type=jnp.float32,
            )
            summed = product_term if summed is None else summed + product_term
    return summed


def conv_two(hidden, weight):
    tile_count, chan_count, extent = (hidden.shape[0], hidden.shape[1], hidden.shape[2])
    summed = None
    for row_tap in range(2):
        for col_tap in range(2):
            sampled = hidden[:, :, row_tap::2, col_tap::2].reshape(tile_count, chan_count, -1)
            product_term = jnp.einsum(
                "oc,ncp->nop",
                weight[:, :, row_tap, col_tap],
                sampled,
                preferred_element_type=jnp.float32,
            )
            summed = product_term if summed is None else summed + product_term
    return summed.reshape(tile_count, weight.shape[0], extent // 2, extent // 2)


def level_grads(hidden, cot_full, weight):
    tile_count, chan_count, extent = (hidden.shape[0], hidden.shape[1], hidden.shape[2])
    half = extent // 2
    cot_rows = cot_full.reshape(tile_count, cot_full.shape[1], -1)
    weight_rows = []
    spread_rows = []
    for row_tap in range(2):
        weight_cols = []
        spread_cols = []
        for col_tap in range(2):
            sampled = hidden[:, :, row_tap::2, col_tap::2].reshape(tile_count, chan_count, -1)
            weight_cols.append(
                jnp.einsum("nop,ncp->oc", cot_rows, sampled, preferred_element_type=jnp.float32)
            )
            spread = jnp.einsum(
                "oc,nop->ncp",
                weight[:, :, row_tap, col_tap],
                cot_rows,
                preferred_element_type=jnp.float32,
            )
            spread_cols.append(spread.reshape(tile_count, chan_count, half, half))
        weight_rows.append(jnp.stack(weight_cols, axis=-1))
        spread_rows.append(jnp.stack(spread_cols, axis=-1))
    grad_weight = jnp.stack(weight_rows, axis=2)
    grad_hidden = jnp.stack(spread_rows, axis=3).reshape(tile_count, chan_count, extent, extent)
    return (grad_weight, grad_hidden)


def conv_grads(padded, grad_full, weight):
    extent = padded.shape[2] - 2
    grad_padded = jnp.zeros(padded.shape, jnp.float32)
    weight_rows = []
    for row_tap in range(3):
        weight_cols = []
        for col_tap in range(3):
            window = padded[:, :, row_tap : row_tap + extent, col_tap : col_tap + extent]
            weight_cols.append(
                jnp.einsum("noxy,ncxy->oc", grad_full, window, preferred_element_type=jnp.float32)
            )
            spread = jnp.einsum(
                "oc,noxy->ncxy",
                weight[:, :, row_tap, col_tap],
                grad_full,
                preferred_element_type=jnp.float32,
            )
            grad_padded = grad_padded.at[
                :, :, row_tap : row_tap + extent, col_tap : col_tap + extent
            ].add(spread)
        weight_rows.append(jnp.stack(weight_cols, axis=-1))
    return (jnp.stack(weight_rows, axis=2), grad_padded)


def add_returned(grad_padded, returned):
    interior = grad_padded[:, :, 1:-1, 1:-1]
    interior = interior.at[:, :, 0, :].add(returned[:, 0])
    interior = interior.at[:, :, -1, :].add(returned[:, 1])
    interior = interior.at[:, :, :, 0].add(returned[:, 2])
    interior = interior.at[:, :, :, -1].add(returned[:, 3])
    return interior.astype(jnp.bfloat16)


def flatten_pixels(field):
    return field.reshape(field.shape[0], field.shape[1], -1)


def on_device(inputs, gluing, conv_weight, level_weight, cotangent):
    inputs = inputs.reshape(inputs.shape[0], inputs.shape[1], S, S)
    cotangent = cotangent.reshape(cotangent.shape[0], cotangent.shape[1], S // 2, S // 2)
    chan_width = inputs.shape[1]
    chan_first = lax.axis_index("chan") * chan_width
    picker = make_picker(gluing)
    conv_in = lax.dynamic_slice_in_dim(conv_weight, chan_first, chan_width, 1)
    level_in = lax.dynamic_slice_in_dim(level_weight, chan_first, chan_width, 1)
    strips = edge_strips(inputs)
    halo_cells = picker(
        jnp.zeros_like(strips), lax.all_gather(strips, "tile", axis=0, tiled=True), jnp.int32(0)
    )
    padded_own = assemble(inputs, orient(halo_cells, gluing))
    partial_pre = conv_three(padded_own, conv_in)
    pre_act = lax.psum_scatter(partial_pre, "chan", scatter_dimension=1, tiled=True)
    hidden = jax.nn.gelu(pre_act).astype(jnp.bfloat16)
    level_part = conv_two(hidden, level_in)
    level = lax.psum_scatter(level_part, "chan", scatter_dimension=1, tiled=True).astype(
        jnp.bfloat16
    )
    cot_full = lax.all_gather(cotangent, "chan", axis=1, tiled=True)
    grad_level, grad_hidden = level_grads(hidden, cot_full, level_in)
    unused, pullback = jax.vjp(jax.nn.gelu, pre_act)
    grad_pre = pullback(grad_hidden)[0].astype(jnp.bfloat16)
    grad_full = lax.all_gather(grad_pre, "chan", axis=1, tiled=True)
    grad_conv, grad_padded = conv_grads(padded_own, grad_full, conv_in)
    grad_conv, grad_level = lax.psum((grad_conv, grad_level), "tile")
    rims = border_strips(grad_padded).astype(jnp.bfloat16)
    returned = picker(
        jnp.zeros_like(rims), lax.all_gather(rims, "tile", axis=0, tiled=True), jnp.int32(0)
    )
    returned = orient(returned, gluing).astype(jnp.float32)
    grad_inputs = add_returned(grad_padded, returned)
    return (flatten_pixels(level), flatten_pixels(grad_inputs), grad_conv, grad_level)


def solution(mesh):
    return jax.shard_map(
        on_device,
        mesh=mesh,
        in_specs=(
            P("tile", "chan", None),
            P("tile", None, None),
            P(),
            P(),
            P("tile", "chan", None),
        ),
        out_specs=(
            P("tile", "chan", None),
            P("tile", "chan", None),
            P(None, "chan", None, None),
            P(None, "chan", None, None),
        ),
        check_vma=False,
    )
```

profile of v0, /device:TPU:1, one launch (start us, length us, event | category | flops | bytes accessed | tf_op | source)
XLA Modules:
  0.0 1141.6 jit_solution(13108972950838934719)
XLA Ops:
  16.2 104.5 %all-gather.4.cloned.1.call-done = bf16[128,4,32,64]{3,2,0,1:T(8,128)(2,1)} async-done(((bf16[2,4,32,64]{3,2,0,1:T(8,128)(2,1)}), bf16[128,4,32,64]{3,2,0,1:T(8,128)(2,1)}) %all-gather.4.cloned.1.call-update) | async-done | bytes 2097168 | tf_op jit(solution)/shard_map/all_gather | solution.py:161
  120.7 5.6 copy.407
  134.6 4.2 maximum_maximum_fusion
  140.8 3.3 fusion.16
  146.9 3.2 fusion.10
  150.2 15.4 %fusion.25 = f32[2,64,64,64]{3,2,1,0:T(8,128)} fusion(bf16[2,32,64,1]{3,1,2,0:T(8,128)(2,1)S(1)} %copy-done.12, bf16[2,32,64,64]{3,1,2,0:T(8,128)(2,1)S(1)} %copy.410, bf16[64,64,3,3]{1,0,3,2:T(8,128)(2,1)S(1)} %copy-done, s32[]{:T(128)S(6)} %select_n.26, s32[]{:T(128)S(6)} %add.205, s32[]{:T(128)S(6)} %add.206), kind=kOutput, calls=%fused_computation.75 | convolution fusion | flops 34603008 | bytes 4210700 | tf_op jit(solution)/shard_map/oc,ncxy->noxy/dot_general | solution.py:60
  165.6 3.3 fusion.24
  168.9 10.7 bitcast_add_fusion
  179.6 5.7 copy.420
  189.8 47.9 %all_gather.13 = bf16[2,128,32,32]{3,2,0,1:T(8,128)(2,1)} all-gather(bf16[2,64,32,32]{3,2,0,1:T(8,128)(2,1)S(1)} %copy.432), channel_id=1, replica_groups=mesh['tile'=64,'chan'=2] {'chan'}, dimensions={1}, use_global_device_ids=true | all-gather | bytes 786432 | tf_op jit(solution)/shard_map/all_gather | solution.py:171
  237.7 3.3 copy.433
  247.6 6.4 maximum_bitcast_fusion
  253.9 4.3 pad_maximum_fusion
  258.2 3.9 copy.442
  264.1 5.7 fusion.6
  269.7 32.0 %slice.621 = bf16[2,32,32,32]{3,1,2,0:T(8,128)(2,1)} slice(bf16[2,32,64,64]{3,1,2,0:T(8,128)(2,1)} %get-tuple-element.198), slice={[0:2:1], [0:32:1], [0:64:2], [1:64:2]} | slice | bytes 262144 | tf_op jit(solution)/shard_map/slice | solution.py:75
  301.7 32.0 %slice.619 = bf16[2,32,32,32]{3,1,2,0:T(8,128)(2,1)} slice(bf16[2,32,64,64]{3,1,2,0:T(8,128)(2,1)} %get-tuple-element.198), slice={[0:2:1], [0:32:1], [0:64:2], [0:64:2]} | slice | bytes 262144 | tf_op jit(solution)/shard_map/slice | solution.py:75
  333.8 27.9 %slice.625 = bf16[2,32,32,32]{3,1,2,0:T(8,128)(2,1)S(1)} slice(bf16[2,32,64,64]{3,1,2,0:T(8,128)(2,1)} %get-tuple-element.198), slice={[0:2:1], [0:32:1], [1:64:2], [1:64:2]} | slice | bytes 262144 | tf_op jit(solution)/shard_map/slice | solution.py:75
  361.7 32.0 %slice.623 = bf16[2,32,32,32]{3,1,2,0:T(8,128)(2,1)} slice(bf16[2,32,64,64]{3,1,2,0:T(8,128)(2,1)} %get-tuple-element.198), slice={[0:2:1], [0:32:1], [1:64:2], [0:64:2]} | slice | bytes 262144 | tf_op jit(solution)/shard_map/slice | solution.py:75
  414.9 21.4 %all-gather.6.cloned.1.call-done = bf16[2,64,64,64]{3,2,0,1:T(8,128)(2,1)} async-done(((bf16[2,32,64,64]{3,2,0,1:T(8,128)(2,1)}), bf16[2,64,64,64]{3,2,0,1:T(8,128)(2,1)}) %all-gather.6.cloned.1.call-update) | async-done | bytes 1048592 | tf_op jit(solution)/shard_map/all_gather | solution.py:175
  436.3 3.8 convolution_bitcast_fusion.15
  457.8 4.5 copy.510
  462.3 4.4 reshape.665
  467.2 3.7 copy.446
  474.4 3.4 bitcast_add_fusion.5
  477.8 11.3 scatter-add.45
  489.1 5.5 add_select_fusion
  494.6 11.3 scatter-add.46
  506.0 3.6 slice_add_fusion.7
  509.6 23.8 %scatter-add.49 = f32[2,32,66,66]{2,1,0,3:T(8,128)S(1)} dynamic-update-slice(f32[2,32,66,66]{2,1,0,3:T(8,128)S(1)} %scatter-add.46, f32[2,32,64,64]{2,1,0,3:T(8,128)} %slice_add_fusion.7, s32[]{:T(128)} %constant.397.clone.1, s32[]{:T(128)} %constant.397.clone.1, s32[]{:T(128)} %constant.395.clone.1, s32[]{:T(128)} %constant.397.clone.1) | dynamic-update-slice | bytes 2097156 | tf_op jit(solution)/shard_map/scatter-add | solution.py:133
  533.4 3.6 slice_add_fusion.6
  537.0 23.8 %scatter-add.50 = f32[2,32,66,66]{2,1,0,3:T(8,128)S(1)} dynamic-update-slice(f32[2,32,66,66]{2,1,0,3:T(8,128)S(1)} %scatter-add.49, f32[2,32,64,64]{2,1,0,3:T(8,128)} %slice_add_fusion.6, s32[]{:T(128)} %constant.397.clone.1, s32[]{:T(128)} %constant.397.clone.1, s32[]{:T(128)} %constant.395.clone.1, s32[]{:T(128)} %constant.395.clone.1) | dynamic-update-slice | bytes 2097156 | tf_op jit(solution)/shard_map/scatter-add | solution.py:133
  560.8 3.6 slice_add_fusion.5
  564.4 23.8 %scatter-add.51 = f32[2,32,66,66]{2,1,0,3:T(8,128)S(1)} dynamic-update-slice(f32[2,32,66,66]{2,1,0,3:T(8,128)S(1)} %scatter-add.50, f32[2,32,64,64]{2,1,0,3:T(8,128)} %slice_add_fusion.5, s32[]{:T(128)} %constant.397.clone.1, s32[]{:T(128)} %constant.397.clone.1, s32[]{:T(128)} %constant.395.clone.1, s32[]{:T(128)} %constant.411.clone.1) | dynamic-update-slice | bytes 2097156 | tf_op jit(solution)/shard_map/scatter-add | solution.py:133
  588.2 3.6 slice_add_fusion.4
  591.8 23.8 %scatter-add.54 = f32[2,32,66,66]{2,1,0,3:T(8,128)S(1)} dynamic-update-slice(f32[2,32,66,66]{2,1,0,3:T(8,128)S(1)} %scatter-add.51, f32[2,32,64,64]{2,1,0,3:T(8,128)} %slice_add_fusion.4, s32[]{:T(128)} %constant.397.clone.1, s32[]{:T(128)} %constant.397.clone.1, s32[]{:T(128)} %constant.411.clone.1, s32[]{:T(128)} %constant.397.clone.1) | dynamic-update-slice | bytes 2097156 | tf_op jit(solution)/shard_map/scatter-add | solution.py:133
  615.6 3.6 slice_add_fusion.3
  619.2 23.8 %scatter-add.55 = f32[2,32,66,66]{2,1,0,3:T(8,128)S(1)} dynamic-update-slice(f32[2,32,66,66]{2,1,0,3:T(8,128)S(1)} %scatter-add.54, f32[2,32,64,64]{2,1,0,3:T(8,128)} %slice_add_fusion.3, s32[]{:T(128)} %constant.397.clone.1, s32[]{:T(128)} %constant.397.clone.1, s32[]{:T(128)} %constant.411.clone.1, s32[]{:T(128)} %constant.395.clone.1) | dynamic-update-slice | bytes 2097156 | tf_op jit(solution)/shard_map/scatter-add | solution.py:133
  643.0 3.6 slice_add_fusion.2
  646.6 23.9 %scatter-add.56 = f32[2,32,66,66]{2,1,0,3:T(8,128)S(1)} dynamic-update-slice(f32[2,32,66,66]{2,1,0,3:T(8,128)S(1)} %scatter-add.55, f32[2,32,64,64]{2,1,0,3:T(8,128)} %slice_add_fusion.2, s32[]{:T(128)} %constant.397.clone.1, s32[]{:T(128)} %constant.397.clone.1, s32[]{:T(128)} %constant.411.clone.1, s32[]{:T(128)} %constant.411.clone.1) | dynamic-update-slice | bytes 2097156 | tf_op jit(solution)/shard_map/scatter-add | solution.py:133
  679.3 278.6 %all-reduce.4.cloned.1.call-done = (f32[64,32,3,3]{0,1,3,2:T(8,128)}, f32[128,32,2,2]{0,1,3,2:T(8,128)}) async-done(((f32[64,32,3,3]{0,1,3,2:T(8,128)}, f32[128,32,2,2]{0,1,3,2:T(8,128)}), (f32[64,32,3,3]{0,1,3,2:T(8,128)}, f32[128,32,2,2]{0,1,3,2:T(8,128)})) %all-reduce.4.cloned.1.call-update) | async-done | bytes 139280 | tf_op jit(solution)/shard_map/psum | solution.py:177
  959.4 24.5 %reduce-scatter.7.cloned.1.call-done = f32[64,2048]{1,0:T(8,128)} async-done(((f32[128,2048]{1,0:T(8,128)}), f32[64,2048]{1,0:T(8,128)}) %reduce-scatter.7.cloned.1.call-update) | async-done | bytes 524304
  989.7 101.2 %all-gather.8.cloned.1.call-done = bf16[128,4,32,64]{3,2,0,1:T(8,128)(2,1)} async-done(((bf16[2,4,32,64]{3,2,0,1:T(8,128)(2,1)}), bf16[128,4,32,64]{3,2,0,1:T(8,128)(2,1)}) %all-gather.8.cloned.1.call-update) | async-done | bytes 2097168 | tf_op jit(solution)/shard_map/all_gather | solution.py:180
  1090.9 5.5 copy.458
  1102.6 3.6 slice_add_fusion.1
  1109.2 5.2 scatter-add.59
  1114.4 3.6 slice_add_fusion
  1118.0 12.7 %scatter-add.60 = f32[2,32,64,64]{2,1,0,3:T(8,128)S(1)} dynamic-update-slice(f32[2,32,64,64]{2,1,0,3:T(8,128)S(1)} %scatter-add.59, f32[2,32,1,64]{2,1,0,3:T(8,128)} %slice_add_fusion, s32[]{:T(128)} %constant.397.clone.1, s32[]{:T(128)} %constant.397.clone.1, s32[]{:T(128)} %constant.414.clone.1, s32[]{:T(128)} %constant.397.clone.1) | dynamic-update-slice | bytes 32772 | tf_op jit(solution)/shard_map/scatter-add | solution.py:141
  (185 shorter events, 106.5 us)
Async XLA Ops:
  7.2 6.0 copy-start
  7.2 113.5 %all-gather.4.cloned.1.call-start = ((), (), s32[]{:S(2)}) async-start(), calls=%async_computation.2 | async-start | bytes 4259840 | tf_op jit(solution)/shard_map/all_gather | solution.py:161
  9.4 3.3 copy-start.28
  11.6 252.5 %reduce-scatter.5.cloned.1.call-start = ((), (), s32[]{:S(2)}) async-start(), calls=%async_computation.3 | async-start | bytes 6291456 | tf_op jit(solution)/shard_map/reduce_scatter | solution.py:165
  12.9 116.4 %copy-start.29 = (pred[2,4]{0,1:T(4,128)(4,1)}, pred[2,4]{0,1:T(4,128)(4,1)S(1)}, u32[]{:S(2)}) copy-start(pred[2,4]{0,1:T(4,128)(4,1)S(1)} %copy.406) | copy-start | bytes 28
  13.0 116.3 %copy-start.31 = (pred[2,4]{0,1:T(4,128)(4,1)}, pred[2,4]{0,1:T(4,128)(4,1)S(1)}, u32[]{:S(2)}) copy-start(pred[2,4]{0,1:T(4,128)(4,1)S(1)} %copy.405) | copy-start | bytes 28
  13.1 116.2 %copy-start.33 = (pred[2,4]{0,1:T(4,128)(4,1)}, pred[2,4]{0,1:T(4,128)(4,1)S(1)}, u32[]{:S(2)}) copy-start(pred[2,4]{0,1:T(4,128)(4,1)S(1)} %copy.404) | copy-start | bytes 28
  13.1 113.2 %copy-start.27 = (s32[1024]{0:T(1024)}, s32[1024]{0:T(1024)S(1)}, u32[]{:S(2)}) copy-start(s32[1024]{0:T(1024)S(1)} %pad_clamp_fusion) | copy-start | bytes 12292
  138.8 2.1 copy-start.5
  138.8 30.1 %copy-start.7 = (bf16[2,32,65,66]{3,1,2,0:T(8,128)(2,1)}, bf16[2,32,65,66]{3,1,2,0:T(8,128)(2,1)S(1)}, u32[]{:S(2)}) copy-start(bf16[2,32,65,66]{3,1,2,0:T(8,128)(2,1)S(1)} %get-tuple-element.196) | copy-start | bytes 1647364
  146.9 3.3 copy-start.12
  150.2 15.4 %copy-start.10 = (bf16[2,32,64,1]{3,1,2,0:T(8,128)(2,1)S(1)}, bf16[2,32,64,1]{3,1,2,0:T(8,128)(2,1)}, u32[]{:S(2)}) copy-start(bf16[2,32,64,1]{3,1,2,0:T(8,128)(2,1)} %copy.409) | copy-start | bytes 24580
  165.6 3.3 copy-start.4
  185.3 0.9 copy-start.24
  185.3 251.1 %all-gather.6.cloned.1.call-start = ((), (), s32[]{:S(2)}) async-start(), calls=%async_computation.4 | async-start | bytes 3145728 | tf_op jit(solution)/shard_map/all_gather | solution.py:175
  237.7 3.3 copy-start.26
  258.2 5.2 copy-start.35
  393.6 3.7 copy-start.15
  393.6 4.2 copy-start.18
  397.8 4.0 copy-start.14
  399.3 558.6 %all-reduce.4.cloned.1.call-start = ((), (), s32[]{:S(2)}) async-start(), calls=%async_computation.7 | async-start | bytes 425984 | tf_op jit(solution)/shard_map/psum | solution.py:177
  399.7 3.1 copy-start.16
  402.9 2.0 copy-start.19
  404.9 5.8 copy-start.20
  406.1 5.9 copy-start.23
  411.2 2.4 copy-start.22
  412.3 24.1 %copy-start.6 = (bf16[2,32,65,66]{3,1,2,0:T(8,128)(2,1)S(1)}, bf16[2,32,65,66]{3,1,2,0:T(8,128)(2,1)}, u32[]{:S(2)}) copy-start(bf16[2,32,65,66]{3,1,2,0:T(8,128)(2,1)} %copy-done.5) | copy-start | bytes 1647364
  436.3 3.8 copy-start.21
  442.3 1.9 copy-start.13
  444.3 1.8 copy-start.11
  448.4 2.2 copy-start.8
  454.5 2.9 copy-start.17
  457.4 526.6 %reduce-scatter.7.cloned.1.call-start = ((), (), s32[]{:S(2)}) async-start(), calls=%async_computation.6 | async-start | bytes 1572864
  466.7 624.2 %all-gather.8.cloned.1.call-start = ((), (), s32[]{:S(2)}) async-start(), calls=%async_computation.5 | async-start | bytes 4259840 | tf_op jit(solution)/shard_map/all_gather | solution.py:180
  470.9 1.3 copy-start.1
  472.8 1.6 copy-start.2
  670.8 1.5 copy-start.9
  989.7 109.6 %copy-start.30 = (pred[2,4]{0,1:T(4,128)(4,1)S(1)}, pred[2,4]{0,1:T(4,128)(4,1)}, u32[]{:S(2)}) copy-start(pred[2,4]{0,1:T(4,128)(4,1)} %copy-done.29) | copy-start | bytes 28
  989.7 109.6 %copy-start.32 = (pred[2,4]{0,1:T(4,128)(4,1)S(1)}, pred[2,4]{0,1:T(4,128)(4,1)}, u32[]{:S(2)}) copy-start(pred[2,4]{0,1:T(4,128)(4,1)} %copy-done.31) | copy-start | bytes 28
  989.7 109.8 %copy-start.34 = (pred[2,4]{0,1:T(4,128)(4,1)S(1)}, pred[2,4]{0,1:T(4,128)(4,1)}, u32[]{:S(2)}) copy-start(pred[2,4]{0,1:T(4,128)(4,1)} %copy-done.33) | copy-start | bytes 28
  1106.3 2.9 copy-start.3
  1131.0 2.9 copy-start.25
Sparse Core Ops, SparseCore 0:
  11.7 109.0 all-gather.3
  185.4 78.0 reduce-scatter.4
  399.4 36.9 all-gather.5
  457.5 500.3 all-reduce.3
  960.1 23.8 reduce-scatter.6
  985.5 105.3 all-gather.7
where the time goes:
time: 1160 us; the launch traced here: 1140 us
  waiting for transfers between devices  530 us (46%)
  local copies, waits for them, and re-layouts  411 us (35%)
  matrix products  104 us (9%)
  blocking collectives  47.9 us (4%)
  other arithmetic  32.2 us (3%)
  between operations  15 us (1%)
    psum x1, waiting for transfers between devices, on_device(): grad_conv, grad_level = lax.psum((grad_conv, grad_level), 'tile')  279 us
    scatter-add x9, local copies, waits for them, and re-layouts, conv_grads(): grad_padded = grad_padded.at[:, :, row_tap:row_tap + extent, col_tap:col_...  166 us
    slice x8, local copies, waits for them, and re-layouts, conv_two(): hidden[:, :, row_tap::2, col_tap::2].reshape(tile_count, chan_count, -1)  129 us
    all_gather x1, waiting for transfers between devices, on_device(): lax.all_gather(strips, 'tile', axis=0, tiled=True)  105 us
    all_gather x1, waiting for transfers between devices, on_device(): lax.all_gather(rims, 'tile', axis=0, tiled=True)  101 us
    all_gather x1, blocking collectives, on_device(): cot_full = lax.all_gather(cotangent, 'chan', axis=1, tiled=True)  47.9 us
    dot_general x9, matrix products, conv_three(): jnp.einsum('oc,ncxy->noxy', weight[:, :, row_tap, col_tap], padded[:, :,...  43.8 us
    dot_general x9, matrix products, conv_grads(): jnp.einsum('oc,noxy->ncxy', weight[:, :, row_tap, col_tap], grad_full, pr...  31.3 us
  transfers between devices with their start and end apart: 6, of which 5 were waited for; matrix products, arithmetic and copies ran while one was open for 24% of the time, Pallas kernels for 0%

commit v1 on v0

v1 whole, which is shorter than its diff:
```python
import functools

import jax
import jax.numpy as jnp
import numpy as np
from jax import lax
from jax.experimental import pallas as pl
from jax.experimental.pallas import tpu as pltpu
from jax.sharding import Mesh
from jax.sharding import PartitionSpec as P

BF = jnp.bfloat16
F32 = jnp.float32
NT = (((1,), (1,)), ((), ()))
SQ = float(np.sqrt(2.0 / np.pi))


def constants():
    perm = np.zeros((512, 512), np.float32)
    for i in range(8):
        for j in range(64):
            perm[i * 64 + j, ((i % 2) * 2 + j % 2) * 128 + (i // 2) * 32 + j // 2] = 1
    edge = np.zeros((128, 2048), np.float32)
    for side in range(2):
        for a in range(2):
            for x in range(32):
                edge[side * 64 + a * 32 + x, a * 1024 + x * 32 + 31 * side] = 1
    rev = np.zeros((128, 128), np.float32)
    for half in range(2):
        for i in range(64):
            rev[half * 64 + i, half * 64 + 63 - i] = 1
    spread = np.zeros((256, 4096), np.float32)
    for b in range(2):
        for y in range(32):
            k = b * 32 + y
            spread[k, 2 * y + b] = 1
            spread[64 + k, 63 * 64 + 2 * y + b] = 1
            spread[128 + k, (2 * y + b) * 64] = 1
            spread[192 + k, (2 * y + b) * 64 + 63] = 1
    return [jnp.asarray(m, BF) for m in (perm, edge, rev, spread)]


def dot(a, b):
    return jnp.dot(a, b, preferred_element_type=F32)


def dot_nt(a, b):
    return lax.dot_general(a, b, NT, preferred_element_type=F32)


def al(v, m):
    return pl.multiple_of(v, m)


def split(v):
    hi = v.astype(BF)
    return hi, (v - hi.astype(F32)).astype(BF)


def strips_kernel(meta, inp, spread, out):
    both = inp[...].reshape(64, 4096)
    s = dot_nt(both, spread[...]).astype(BF)
    for tile in range(2):
        for pair in range(2):
            row = (tile * 2 + pair) * 32
            out[row : row + 32, :] = s[tile * 32 : tile * 32 + 32, pair * 128 : pair * 128 + 128]
    lane = lax.broadcasted_iota(jnp.int32, (16, 128), 1)
    codes = jnp.zeros((16, 128), jnp.int32)
    for k in range(24):
        codes = jnp.where(lane == k, meta[k], codes)
    out[128:144, :] = codes.astype(F32).astype(BF)


def send_kernel(meta, inp, cot, out_in, out_cot):
    o = 1 - meta[24]
    out_in[...] = inp[o]
    out_cot[...] = cot[o]


def weight_kernel(w, wt, wb, wbt):
    wb[...] = jnp.zeros((256, 1024), BF)
    wbt[...] = jnp.zeros((1024, 256), BF)
    for a in range(2):
        for b in range(2):
            ab = (a * 2 + b) * 64
            for i in range(3):
                for j in range(3):
                    rs = ((a + i) * 4 + b + j) * 64
                    wb[ab : ab + 64, rs : rs + 64] = w[i, j]
                    wbt[rs : rs + 64, ab : ab + 64] = wt[i, j]


def place(acc, row, v, src_side, dst_side, half):
    v = pltpu.roll(v, ((src_side ^ dst_side) & 1) * 64, 1)
    acc[pl.ds(row, 32), :] = jnp.where(half == (dst_side & 1), v, acc[pl.ds(row, 32), :])


def route_strips_kernel(meta, codes, b0, b1, b2, b3, *rest):
    outs, acc = rest[:8], rest[8]
    acc[...] = jnp.zeros((512, 128), F32)
    half = lax.broadcasted_iota(jnp.int32, (32, 128), 1) // 64
    lch, zx = meta[25], meta[27]
    for bi, bundle in enumerate((b0, b1, b2, b3)):

        @pl.loop(0, 32)
        def _(m, bi=bi, bundle=bundle):
            base = (bi * 32 + m) * 3
            t = codes[base]
            s = codes[base + 1]
            r = m & 3

            @pl.when((t >> 3) == zx)
            def _():
                k = (t & 7) ^ lch
                row = al((m >> 3) * 144 + ((m >> 2) & 1) * 64 + (r >> 1) * 32, 16)
                v = bundle[pl.ds(row, 32), :].astype(F32)
                place(acc, al(k * 64 + (s >> 1) * 32, 32), v, r, s, half)

    for k in range(8):
        outs[k][...] = acc[k * 64 : k * 64 + 64, :].astype(BF)


def flip(strips, rev, first, second):
    n = strips.shape[0]
    turned = dot(strips.astype(BF), rev)
    lane = lax.broadcasted_iota(jnp.int32, (n, 128), 1)
    flag = jnp.where(lane < 64, first, second)
    return jnp.where(flag == 1, turned, strips)


def main_kernel(
    meta, inp, rin, cot, rcot, h0, h1, h2, h3, h4, h5, h6, h7, wb, wbt, lw, lwt, perm, edge, rev,
    gxk, gxs, lvk, lvs, rim, wown, p1, p2, p3,
    xs, pt, ct, tb_s, lr_s, pre_s, gh_s, hd, gp, wh, lv_s,
):
    h, xi = meta[24], meta[26]
    mine, other = h * 32, 32 - h * 32
    for g in range(8):
        xs[pl.ds(al(g * 64 + mine, 32), 32), :] = inp[h, :, g * 512 : g * 512 + 512]
        xs[pl.ds(al(g * 64 + other, 32), 32), :] = rin[:, g * 512 : g * 512 + 512]
    ct[pl.ds(al(h * 64, 64), 64), :] = cot[h]
    ct[pl.ds(al(64 - h * 64, 64), 64), :] = rcot[...]
    nat = dot(xs[...], perm[...])
    ph = [
        [
            jnp.concatenate(
                [nat[g * 64 : g * 64 + 64, (a * 2 + b) * 128 : (a * 2 + b) * 128 + 128] for g in range(8)],
                axis=1,
            )
            for b in range(2)
        ]
        for a in range(2)
    ]
    own = (h0[...].astype(F32) + h2[...].astype(F32)) + (h4[...].astype(F32) + h6[...].astype(F32))
    far = (h1[...].astype(F32) + h3[...].astype(F32)) + (h5[...].astype(F32) + h7[...].astype(F32))
    for ref, k in ((tb_s, 0), (lr_s, 32)):
        ref[pl.ds(al(mine, 32), 32), :] = own[k : k + 32]
        ref[pl.ds(al(other, 32), 32), :] = far[k : k + 32]
    fl = [meta[(h * 4 + s) * 3 + 2] for s in range(4)]
    tb = flip(tb_s[...], rev[...], fl[0], fl[1])
    lr = flip(lr_s[...], rev[...], fl[2], fl[3])
    sp = dot(lr.astype(BF), edge[...])
    lane = lax.broadcasted_iota(jnp.int32, (64, 1024), 1)
    y = lane & 31
    l1 = lax.broadcasted_iota(jnp.int32, (64, 128), 1)
    cols = [[None] * 4 for _ in range(2)]
    for a in range(2):
        spa = sp[:, a * 1024 : a * 1024 + 1024]
        cols[a][0] = jnp.where(y == 0, spa, pltpu.roll(ph[a][1], 1, 1))
        cols[a][1] = ph[a][0]
        cols[a][2] = ph[a][1]
        cols[a][3] = jnp.where(y == 31, spa, pltpu.roll(ph[a][0], 1023, 1))
    top_shift = (97, 0, 96, 127)
    low_shift = (1, 32, 0, 31)
    for s in range(4):
        pt[(4 + s) * 64 : (4 + s) * 64 + 64, :] = cols[0][s].astype(BF)
        pt[(8 + s) * 64 : (8 + s) * 64 + 64, :] = cols[1][s].astype(BF)
        up = pltpu.roll(cols[1][s], 32, 1)
        t = pltpu.roll(tb, top_shift[s], 1) if top_shift[s] else tb
        if s == 0:
            t = jnp.where(l1 == 0, 0.0, t)
        if s == 3:
            t = jnp.where(l1 == 31, 0.0, t)
        pt[s * 64 : s * 64 + 64, 128:] = up[:, 128:].astype(BF)
        pt[s * 64 : s * 64 + 64, :128] = jnp.where(l1 < 32, t, up[:, :128]).astype(BF)
        dn = pltpu.roll(cols[0][s], 992, 1)
        t = pltpu.roll(tb, low_shift[s], 1) if low_shift[s] else tb
        if s == 0:
            t = jnp.where(l1 == 96, 0.0, t)
        if s == 3:
            t = jnp.where(l1 == 127, 0.0, t)
        pt[(12 + s) * 64 : (12 + s) * 64 + 64, :896] = dn[:, :896].astype(BF)
        pt[(12 + s) * 64 : (12 + s) * 64 + 64, 896:] = jnp.where(l1 >= 96, t, dn[:, 896:]).astype(BF)
    pre_s[...] = dot(wb[...], pt[...])
    gh_s[...] = dot(lwt[...], ct[...])
    for q in range(8):
        rows = slice(q * 32, q * 32 + 32)
        v = pre_s[rows, :]
        v2 = v * v
        th = jnp.tanh(SQ * (v + 0.044715 * (v2 * v)))
        half = 0.5 * (1.0 + th)
        hd[rows, :] = (v * half).astype(BF)
        d = half + 0.5 * v * (1.0 - th * th) * (SQ * (1.0 + 3 * 0.044715 * v2))
        gp[rows, :] = (gh_s[rows, :] * d).astype(BF)
    gx = dot(wbt[...], gp[...])

    def blk(r, s):
        k = (r * 4 + s) * 64
        return gx[k : k + 64]

    x0 = lane < 32
    x31 = lane >= 992

    def down(v):
        return jnp.where(x0, 0.0, pltpu.roll(v, 32, 1))

    def up_(v):
        return jnp.where(x31, 0.0, pltpu.roll(v, 992, 1))

    qs, ms = [], []
    for r in range(4):
        q0 = blk(r, 1) + jnp.where(y == 0, 0.0, pltpu.roll(blk(r, 3), 1, 1))
        q1 = blk(r, 2) + jnp.where(y == 31, 0.0, pltpu.roll(blk(r, 0), 1023, 1))
        qs.append((q0, q1))
        ms.append(jnp.where(y == 0, blk(r, 0), jnp.where(y == 31, blk(r, 3), 0.0)))
    top = jnp.where(l1 < 32, qs[0][0][:, :128], pltpu.roll(qs[0][1][:, :128], 32, 1))
    low = jnp.where(l1 < 96, pltpu.roll(qs[3][0][:, 896:], 96, 1), qs[3][1][:, 896:])
    rim_tb = jnp.where(l1 < 64, top, low).astype(BF)
    a0 = (ms[1] + down(ms[3])).astype(BF)
    a1 = (ms[2] + up_(ms[0])).astype(BF)
    rim_lr = dot_nt(a0, edge[:, :1024]) + dot_nt(a1, edge[:, 1024:])
    rim_lr = rim_lr.astype(BF)
    for ref in (rim, p1, p2, p3):
        ref[0:64, :] = rim_tb
        ref[64:128, :] = rim_lr
    dl = dot_nt(hd[...], ct[...])
    gbt = dot_nt(pt[...], gp[...])
    packed = []
    for ij in range(9):
        i, j = divmod(ij, 3)
        u = v = None
        for a in range(2):
            k = ((a + i) * 4 + j) * 64
            ua = gbt[k : k + 64, a * 128 : a * 128 + 128]
            va = gbt[k + 64 : k + 128, a * 128 : a * 128 + 128]
            u = ua if u is None else u + ua
            v = va if v is None else v + va
        if ij % 2 == 0:
            packed.append(jnp.where(l1 < 64, u + pltpu.roll(v, 64, 1), 0.0))
        else:
            packed[-1] = jnp.where(l1 < 64, packed[-1], v + pltpu.roll(u, 64, 1))
    for hh in range(2):
        for q in range(5):
            wh[hh * 288 + q * 32 : hh * 288 + q * 32 + 32, :] = packed[q][hh * 32 : hh * 32 + 32]
        for ab in range(4):
            row = hh * 288 + 160 + ab * 32
            wh[row : row + 32, :] = dl[ab * 64 + hh * 32 : ab * 64 + hh * 32 + 32]
    for k, ref in enumerate((wown, p1, p2, p3)):
        ci = (xi + k) & 3
        chunk = jnp.concatenate(
            [wh[pl.ds(al(hh * 288 + ci * 72, 8), 72), :] for hh in range(2)], axis=0
        )
        if k == 0:
            ref[...] = chunk
        else:
            hi, lo = split(chunk)
            ref[128:272, :] = hi
            ref[272:416, :] = lo
    lv_s[...] = dot(lw[...], hd[...]).astype(BF)
    lvk[...] = lv_s[pl.ds(al(h * 64, 64), 64), :]
    lvs[...] = lv_s[pl.ds(al(64 - h * 64, 64), 64), :]
    inner = [
        [
            (qs[1][b] + down(qs[3][b])).astype(BF),
            (qs[2][b] + up_(qs[0][b])).astype(BF),
        ]
        for b in range(2)
    ]
    for g in range(8):
        for a in range(2):
            for b in range(2):
                k = (a * 2 + b) * 128
                xs[g * 64 : g * 64 + 64, k : k + 128] = inner[b][a][:, g * 128 : g * 128 + 128]
    xs[...] = dot_nt(xs[...], perm[...]).astype(BF)
    for g in range(8):
        gxk[:, g * 512 : g * 512 + 512] = xs[pl.ds(al(g * 64 + mine, 32), 32), :]
        gxs[:, g * 512 : g * 512 + 512] = xs[pl.ds(al(g * 64 + other, 32), 32), :]


def bundle_kernel(rim, wown, r1, r2, r3, out, wsum):
    w = wown[...]
    out[0:128, :] = rim[...]
    for k, ref in enumerate((r1, r2, r3)):
        out[(k + 1) * 128 : (k + 2) * 128, :] = ref[0:128, :]
        w = w + (ref[128:272, :].astype(F32) + ref[272:416, :].astype(F32))
    wsum[...] = w
    hi, lo = split(w)
    out[512:656, :] = hi
    out[656:800, :] = lo


def route_rims_kernel(meta, codes, wsum, b0, b1, b2, b3, *rest):
    outs, wk, acc, ws = rest[:8], rest[8], rest[9], rest[10]
    acc[...] = jnp.zeros((1024, 128), F32)
    half = lax.broadcasted_iota(jnp.int32, (32, 128), 1) // 64
    h, lch, zx = meta[24], meta[25], meta[27]
    for bi, bundle in enumerate((b0, b1, b2, b3)):

        @pl.loop(0, 16)
        def _(m, bi=bi, bundle=bundle):
            j = m >> 2
            r = m & 3
            base = (bi * 32 + j * 8 + h * 4 + r) * 3
            t = codes[base]
            s = codes[base + 1]

            @pl.when((t >> 3) == zx)
            def _():
                for hd in range(2):
                    k = ((t & 6) | hd) ^ lch
                    row = al(j * 128 + (r >> 1) * 64 + hd * 32, 32)
                    v = bundle[pl.ds(row, 32), :].astype(F32)
                    dst = al(k * 128 + (t & 1) * 64 + (s >> 1) * 32, 32)
                    place(acc, dst, v, r, s, half)

    w = wsum[...]
    for ref in (b1, b2, b3):
        w = w + (ref[512:656, :].astype(F32) + ref[656:800, :].astype(F32))
    ws[...] = w
    mine = ws[pl.ds(al(h * 72, 8), 72), :]
    far = ws[pl.ds(al(72 - h * 72, 8), 72), :]
    wk[...] = mine
    pieces = []
    for v in (mine, far):
        hi, lo = split(v)
        pieces.append(jnp.concatenate([hi.astype(F32), lo.astype(F32)], axis=0).astype(BF))
    for k in range(8):
        outs[k][0:128, :] = acc[k * 128 : k * 128 + 128, :].astype(BF)
        if k:
            outs[k][128:272, :] = pieces[k & 1]


def final_kernel(
    meta, own, r1, r2, r3, r4, r5, r6, r7, wk, gxk, gxr, lvk, lvr, spread, rev, gin, lev, wout
):
    h = meta[24]
    rets = (r1, r2, r3, r4, r5, r6, r7)
    acc = own[0:128, :].astype(F32)
    w = wk[...]
    for ref in rets:
        acc = acc + ref[0:128, :].astype(F32)
        pieces = ref[128:272, :].astype(F32)
        w = w + (pieces[0:72] + pieces[72:144])
    wout[...] = w
    lane = lax.broadcasted_iota(jnp.int32, (128, 128), 1)
    row = lax.broadcasted_iota(jnp.int32, (128, 128), 0)
    flag = jnp.zeros((128, 128), jnp.int32)
    for tile in range(2):
        for side in range(4):
            f = meta[(tile * 4 + side) * 3 + 2]
            here = ((row >> 5) == tile * 2 + (side >> 1)) & ((lane >> 6) == (side & 1))
            flag = jnp.where(here, f, flag)
    turned = dot(acc.astype(BF), rev[...])
    acc = jnp.where(flag == 1, turned, acc).astype(BF)
    for tile, src in ((h, gxk), (1 - h, gxr)):
        gin[tile] = src[...]
    for tile in range(2):
        st = jnp.concatenate([acc[tile * 64 : tile * 64 + 32], acc[tile * 64 + 32 : tile * 64 + 64]], axis=1)
        delta = dot(st, spread[...])
        gin[tile] = (gin[tile].astype(F32) + delta).astype(BF)
    lev[h] = lvk[...]
    lev[1 - h] = lvr[...]


def unpack_kernel(meta, own, r1, r2, r3, gc, gl, ws):
    xi = meta[26]
    for k, ref in enumerate((own, r1, r2, r3)):
        ws[pl.ds(al(((xi - k) & 3) * 72, 8), 72), :] = ref[...]
    for ij in range(9):
        v = ws[(ij // 2) * 32 : (ij // 2) * 32 + 32, :]
        if ij % 2:
            v = pltpu.roll(v, 64, 1)
        gc[ij] = v[:, :64]
    for ab in range(4):
        gl[ab] = ws[160 + ab * 32 : 192 + ab * 32, :]


def call(kernel, outs, args, smem, scratch=(), name=None):
    specs = [
        pl.BlockSpec(memory_space=pltpu.SMEM if i < smem else pltpu.VMEM) for i in range(len(args))
    ]
    single = not isinstance(outs, list)
    shapes = [outs] if single else outs
    res = pl.pallas_call(
        kernel,
        out_shape=[jax.ShapeDtypeStruct(s, d) for s, d in shapes],
        in_specs=specs,
        out_specs=[pl.BlockSpec(memory_space=pltpu.VMEM) for _ in shapes],
        scratch_shapes=list(scratch),
        compiler_params=pltpu.CompilerParams(vmem_limit_bytes=58 << 20),
        name=name,
    )(*args)
    return res[0] if single else res


def ring(v, axis, k):
    return lax.ppermute(v, axis, [(i, (i + k) % 4) for i in range(4)])


def swap(v):
    return lax.ppermute(v, "h", [(0, 1), (1, 0)])


def octet(v, k):
    return lax.ppermute(v, ("l", "c", "h"), [(i, i ^ k) for i in range(8)])


def on_device(inputs, gluing, conv_weight, level_weight, cotangent):
    perm, edge, rev, spread = constants()
    zi, xi, li, ci, hi = (lax.axis_index(n) for n in ("z", "x", "l", "c", "h"))
    extra = jnp.stack([hi, li * 4 + ci * 2 + hi, xi, zi * 4 + xi]).astype(jnp.int32)
    meta = jnp.concatenate([gluing.reshape(24), extra])

    strips = call(strips_kernel, ((144, 128), BF), (meta, inputs, spread), 1, name="strips")
    got = [ring(strips, "x", k) for k in (1, 2, 3)]
    bundle = jnp.concatenate([strips] + got, axis=0)
    send_in, send_cot = call(
        send_kernel, [((32, 4096), BF), ((64, 1024), BF)], (meta, inputs, cotangent), 1, name="send"
    )
    rin, rcot = swap(send_in), swap(send_cot)
    bundles = [bundle] + [ring(bundle, "z", k) for k in (1, 2, 3)]
    codes = jnp.stack([b.reshape(4, 144, 128)[:, 128, :24] for b in bundles])
    codes = codes.astype(jnp.int32).reshape(384)
    routed = call(
        route_strips_kernel,
        [((64, 128), BF)] * 8,
        (meta, codes, *bundles),
        2,
        [pltpu.VMEM((512, 128), F32)],
        name="route_strips",
    )
    halos = [routed[0]] + [octet(routed[k], k) for k in range(1, 8)]

    w9 = jnp.transpose(conv_weight, (2, 3, 0, 1))
    w9t = jnp.transpose(conv_weight, (2, 3, 1, 0))
    wb, wbt = call(
        weight_kernel, [((256, 1024), BF), ((1024, 256), BF)], (w9, w9t), 0, name="weights"
    )
    lwt = jnp.transpose(level_weight, (2, 3, 1, 0)).reshape(256, 128)
    lw = jnp.transpose(level_weight, (0, 2, 3, 1)).reshape(128, 256)
    gxk, gxs, lvk, lvs, rim, wown, p1, p2, p3 = call(
        main_kernel,
        [
            ((32, 4096), BF), ((32, 4096), BF), ((64, 1024), BF), ((64, 1024), BF), ((128, 128), BF),
            ((144, 128), F32), ((416, 128), BF), ((416, 128), BF), ((416, 128), BF),
        ],
        (meta, inputs, rin, cotangent, rcot, *halos, wb, wbt, lw, lwt, perm, edge, rev),
        1,
        [
            pltpu.VMEM((512, 512), BF), pltpu.VMEM((1024, 1024), BF), pltpu.VMEM((128, 1024), BF),
            pltpu.VMEM((64, 128), F32), pltpu.VMEM((64, 128), F32), pltpu.VMEM((256, 1024), F32),
            pltpu.VMEM((256, 1024), F32), pltpu.VMEM((256, 1024), BF), pltpu.VMEM((256, 1024), BF),
            pltpu.VMEM((576, 128), F32), pltpu.VMEM((128, 1024), BF),
        ],
        name="main",
    )
    back = [ring(p, "x", k) for p, k in ((p1, 1), (p2, 2), (p3, 3))]
    zpay, wsum = call(
        bundle_kernel, [((800, 128), BF), ((144, 128), F32)], (rim, wown, *back), 0, name="bundle"
    )
    zback = [zpay] + [ring(zpay, "z", k) for k in (1, 2, 3)]
    gxr, lvr = swap(gxs), swap(lvs)
    *rets, wk = call(
        route_rims_kernel,
        [((272, 128), BF)] * 8 + [((72, 128), F32)],
        (meta, codes, wsum, *zback),
        2,
        [pltpu.VMEM((1024, 128), F32), pltpu.VMEM((144, 128), F32)],
        name="route_rims",
    )
    rets = [rets[0]] + [octet(rets[k], k) for k in range(1, 8)]
    gin, lev, wpart = call(
        final_kernel,
        [((2, 32, 4096), BF), ((2, 64, 1024), BF), ((72, 128), F32)],
        (meta, *rets, wk, gxk, gxr, lvk, lvr, spread, rev),
        1,
        name="final",
    )
    wall = [wpart] + [ring(wpart, "x", k) for k in (1, 2, 3)]
    gc, gl = call(
        unpack_kernel,
        [((9, 32, 64), F32), ((4, 32, 128), F32)],
        (meta, *wall),
        1,
        [pltpu.VMEM((288, 128), F32)],
        name="unpack",
    )
    grad_conv = jnp.transpose(gc.reshape(3, 3, 32, 64), (3, 2, 0, 1))
    grad_level = jnp.transpose(gl.reshape(2, 2, 32, 128), (3, 2, 0, 1))
    return lev, gin, grad_conv, grad_level


def solution(mesh):
    fine = Mesh(mesh.devices.reshape(4, 4, 2, 2, 2), ("z", "x", "l", "c", "h"))
    tile = ("z", "x", "l", "c")
    return jax.shard_map(
        on_device,
        mesh=fine,
        in_specs=(
            P(tile, "h", None),
            P(tile, None, None),
            P(),
            P(),
            P(tile, "h", None),
        ),
        out_specs=(
            P(tile, "h", None),
            P(tile, "h", None),
            P(None, "h", None, None),
            P(None, "h", None, None),
        ),
        check_vma=False,
    )
```

time: 1160 us -> 114 us (0.10); the launches traced: 1140 us -> 113 us
  waiting for transfers between devices: 530 us -> 26.9 us
  local copies, waits for them, and re-layouts: 411 us -> 9.32 us
  matrix products: 104 us -> 0 us
  blocking collectives: 47.9 us -> 0 us
  starting transfers between devices: 1.43 us -> 46.5 us
  other arithmetic: 32.2 us -> 0.79 us
  Pallas kernels: 0 us -> 28.9 us
  between operations: 15 us -> 0.93 us
    psum x1 -> x0, waiting for transfers between devices: 279 us -> none  [on_device(): grad_conv, grad_level = lax.psum((grad_conv, grad_level), 'tile')]
    all_gather x3 -> x0, waiting for transfers between devices: 227 us -> none  [the longest x1 105 us: on_device(): lax.all_gather(strips, 'tile', axis=0, tiled=True)]
    scatter-add x11 -> x0, local copies, waits for them, and re-layouts: 183 us -> none  [the longest x9 166 us: conv_grads(): grad_padded = grad_padded.at[:, :, row_tap:row_tap + extent, col_tap:col_...]
    slice x13 -> x4, local copies, waits for them, and re-layouts: 134 us -> 0.02 us  [on_device(): codes = jnp.stack([b.reshape(4, 144, 128)[:, 128, :24] for b in bundles])]
    dot_general x39 -> x0, matrix products: 104 us -> none  [the longest x9 43.8 us: conv_three(): jnp.einsum('oc,ncxy->noxy', weight[:, :, row_tap, col_tap], padded[:, :,...]
    all_gather x1 -> x0, blocking collectives: 47.9 us -> none  [on_device(): cot_full = lax.all_gather(cotangent, 'chan', axis=1, tiled=True)]
    ppermute x0 -> x33, starting transfers between devices: none -> 46.5 us  [the longest x14 22.6 us: octet(): return lax.ppermute(v, ('l', 'c', 'h'), [(i, i ^ k) for i in range(8)])]
    pallas_call x0 -> x9, Pallas kernels: none -> 28.9 us  [call(): pl.pallas_call(kernel, out_shape=[jax.ShapeDtypeStruct(s, d) for s, d in...]
  transfers between devices with their start and end apart: 6 -> 33, of which waited for: 5 -> 13; matrix products, arithmetic and copies ran while one was open for 24% -> 3% of each run, Pallas kernels for 0% -> 9%
where the time goes in v1:
time: 114 us; the launch traced here: 113 us
  starting transfers between devices  46.5 us (41%)
  Pallas kernels  28.9 us (25%)
  waiting for transfers between devices  26.9 us (24%)
  local copies, waits for them, and re-layouts  9.32 us (8%)
    pallas_call x9, Pallas kernels, call(): pl.pallas_call(kernel, out_shape=[jax.ShapeDtypeStruct(s, d) for s, d in...  28.9 us
    ppermute x15, waiting for transfers between devices, ring(): return lax.ppermute(v, axis, [(i, (i + k) % 4) for i in range(4)])  22.7 us
    ppermute x14, starting transfers between devices, octet(): return lax.ppermute(v, ('l', 'c', 'h'), [(i, i ^ k) for i in range(8)])  22.6 us
    ppermute x15, starting transfers between devices, ring(): return lax.ppermute(v, axis, [(i, (i + k) % 4) for i in range(4)])  17.9 us
    ppermute x4, starting transfers between devices, swap(): return lax.ppermute(v, 'h', [(0, 1), (1, 0)])  5.94 us
    unnamed x69, local copies, waits for them, and re-layouts  4.96 us
    ppermute x14, waiting for transfers between devices, octet(): return lax.ppermute(v, ('l', 'c', 'h'), [(i, i ^ k) for i in range(8)])  4.18 us
  transfers between devices with their start and end apart: 33, of which 13 were waited for; matrix products, arithmetic and copies ran while one was open for 3% of the time, Pallas kernels for 9%

profile of v1, /device:TPU:1, one launch (start us, length us, event | category | flops | bytes accessed | tf_op | source)
XLA Modules:
  0.0 113.3 jit_solution(1200667971764016899)
XLA Ops:
  0.6 0.8 copy.22
  1.5 0.7 concatenate.6.meta
  2.2 3.2 %strips.1 = bf16[144,128]{1,0:T(8,128)(2,1)} custom-call(s32[28]{0:T(128)} %concatenate.6.meta, bf16[2,32,4096]{2,1,0:T(8,128)(2,1)} %inp.5, bf16[256,4096]{1,0:T(8,128)(2,1)} %constant.33.clone.spread), custom_call_target="tpu_custom_call" | custom-call | tf_op jit(solution)/shard_map/strips/pallas_call | solution.py:394
  5.4 3.3 %collective-permute-start.2 = (bf16[144,128]{1,0:T(8,128)(2,1)}, bf16[144,128]{1,0:T(8,128)(2,1)S(1)}, u32[]{:S(2)}, u32[]{:S(2)}) collective-permute-start(bf16[144,128]{1,0:T(8,128)(2,1)} %strips.1), channel_id=1, source_target_pairs={{0,24},{8,0},{16,8},{24,16},{1,25},{9,1},{17,9},{25,17},{2,26},{10... | collective-permute-start | bytes 110600 | tf_op jit(solution)/shard_map/ppermute | solution.py:407
  10.0 3.2 %collective-permute-done.1 = bf16[144,128]{1,0:T(8,128)(2,1)S(1)} collective-permute-done((bf16[144,128]{1,0:T(8,128)(2,1)}, bf16[144,128]{1,0:T(8,128)(2,1)S(1)}, u32[]{:S(2)}, u32[]{:S(2)}) %collective-permute-start.1) | collective-permute-done | bytes 36896 | tf_op jit(solution)/shard_map/ppermute | solution.py:407
  13.6 0.8 pad_maximum_fusion.b0
  14.4 3.8 %collective-permute-start.5 = (bf16[576,128]{1,0:T(8,128)(2,1)S(1)}, bf16[576,128]{1,0:T(8,128)(2,1)S(1)}, u32[]{:S(2)}, u32[]{:S(2)}) collective-permute-start(bf16[576,128]{1,0:T(8,128)(2,1)S(1)} %pad_maximum_fusion.b0), channel_id=1, source_target_pairs={{0,96},{32,0},{64,32},{96,64},{1,97},{33,1},{65,33},{97,65},{2,98}... | collective-permute-start | bytes 442376 | tf_op jit(solution)/shard_map/ppermute | solution.py:407
  18.2 0.7 collective-permute-start.3
  18.9 1.9 %send.1 = (bf16[32,4096]{1,0:T(8,128)(2,1)}, bf16[64,1024]{1,0:T(8,128)(2,1)}) custom-call(s32[28]{0:T(128)} %concatenate.6.meta, bf16[2,32,4096]{2,1,0:T(8,128)(2,1)} %inp.5, bf16[2,64,1024]{2,1,0:T(8,128)(2,1)} %cot.3), custom_call_target="tpu_custom_call" | custom-call | tf_op jit(solution)/shard_map/send/pallas_call | solution.py:394
  20.8 2.9 %collective-permute-start.7 = (bf16[64,1024]{1,0:T(8,128)(2,1)}, bf16[64,1024]{1,0:T(8,128)(2,1)S(1)}, u32[]{:S(2)}, u32[]{:S(2)}) collective-permute-start(bf16[64,1024]{1,0:T(8,128)(2,1)} %get-tuple-element.42), channel_id=1, source_target_pairs={{0,1},{1,0},{2,3},{3,2},{4,5},{5,4},{6,7},{7,6},{8,9},{9,8},{10,11... | collective-permute-start | bytes 393224 | tf_op jit(solution)/shard_map/ppermute | solution.py:411
  23.8 1.8 %collective-permute-done.3.b1 = bf16[576,128]{1,0:T(8,128)(2,1)S(1)} collective-permute-done((bf16[576,128]{1,0:T(8,128)(2,1)S(1)}, bf16[576,128]{1,0:T(8,128)(2,1)S(1)}, u32[]{:S(2)}, u32[]{:S(2)}) %collective-permute-start.3) | collective-permute-done | bytes 147488 | tf_op jit(solution)/shard_map/ppermute | solution.py:407
  25.6 0.7 reshape.48.codes
  26.3 4.0 %route_strips.1 = (bf16[64,128]{1,0:T(8,128)(2,1)}, bf16[64,128]{1,0:T(8,128)(2,1)}, bf16[64,128]{1,0:T(8,128)(2,1)}, bf16[64,128]{1,0:T(8,128)(2,1)}, bf16[64,1...) custom-call(s32[28]{0:T(128)} %concatenate.6.meta, ...), custom_call_target="tpu_custom_call" | custom-call | tf_op jit(solution)/shard_map/route_strips/pallas_call | solution.py:394
  30.3 2.9 %collective-permute-start.8 = (bf16[64,128]{1,0:T(8,128)(2,1)}, bf16[64,128]{1,0:T(8,128)(2,1)S(1)}, u32[]{:S(2)}, u32[]{:S(2)}) collective-permute-start(bf16[64,128]{1,0:T(8,128)(2,1)} %get-tuple-element.44), channel_id=1, source_target_pairs={{0,1},{1,0},{2,3},{3,2},{4,5},{5,4},{6,7},{7,6},{8,9},{9,8},{10,11... | collective-permute-start | bytes 49160 | tf_op jit(solution)/shard_map/ppermute | solution.py:415
  33.3 3.4 %collective-permute-start.9 = (bf16[64,128]{1,0:T(8,128)(2,1)}, bf16[64,128]{1,0:T(8,128)(2,1)S(1)}, u32[]{:S(2)}, u32[]{:S(2)}) collective-permute-start(bf16[64,128]{1,0:T(8,128)(2,1)} %get-tuple-element.45), channel_id=1, source_target_pairs={{0,2},{1,3},{2,0},{3,1},{4,6},{5,7},{6,4},{7,5},{8,10},{9,11},{10,... | collective-permute-start | bytes 49160 | tf_op jit(solution)/shard_map/ppermute | solution.py:415
  36.7 1.4 %collective-permute-start.11 = (bf16[64,128]{1,0:T(8,128)(2,1)}, bf16[64,128]{1,0:T(8,128)(2,1)S(1)}, u32[]{:S(2)}, u32[]{:S(2)}) collective-permute-start(bf16[64,128]{1,0:T(8,128)(2,1)} %get-tuple-element.47), channel_id=1, source_target_pairs={{0,4},{1,5},{2,6},{3,7},{4,0},{5,1},{6,2},{7,3},{8,12},{9,13},{10,... | collective-permute-start | bytes 49160 | tf_op jit(solution)/shard_map/ppermute | solution.py:415
  38.2 1.7 %collective-permute-start.12 = (bf16[64,128]{1,0:T(8,128)(2,1)}, bf16[64,128]{1,0:T(8,128)(2,1)S(1)}, u32[]{:S(2)}, u32[]{:S(2)}) collective-permute-start(bf16[64,128]{1,0:T(8,128)(2,1)} %get-tuple-element.48), channel_id=1, source_target_pairs={{0,5},{1,4},{2,7},{3,6},{4,1},{5,0},{6,3},{7,2},{8,13},{9,12},{10,... | collective-permute-start | bytes 49160 | tf_op jit(solution)/shard_map/ppermute | solution.py:415
  39.9 1.9 %collective-permute-start.13 = (bf16[64,128]{1,0:T(8,128)(2,1)}, bf16[64,128]{1,0:T(8,128)(2,1)S(1)}, u32[]{:S(2)}, u32[]{:S(2)}) collective-permute-start(bf16[64,128]{1,0:T(8,128)(2,1)} %get-tuple-element.49), channel_id=1, source_target_pairs={{0,6},{1,7},{2,4},{3,5},{4,2},{5,3},{6,0},{7,1},{8,14},{9,15},{10,... | collective-permute-start | bytes 49160 | tf_op jit(solution)/shard_map/ppermute | solution.py:415
  41.8 0.7 collective-permute-start.14
  43.1 0.7 copy.30.lw
  43.9 0.8 copy.27
  44.6 2.4 %weights.1 = (bf16[256,1024]{1,0:T(8,128)(2,1)}, bf16[1024,256]{1,0:T(8,128)(2,1)}) custom-call(bf16[3,3,64,64]{3,2,1,0:T(8,128)(2,1)} %bitcast.31, bf16[3,3,64,64]{3,2,1,0:T(8,128)(2,1)} %bitcast.32), custom_call_target="tpu_custom_call" | custom-call | tf_op jit(solution)/shard_map/weights/pallas_call | solution.py:394
  47.8 6.9 %main.1 = (bf16[32,4096]{1,0:T(8,128)(2,1)}, bf16[32,4096]{1,0:T(8,128)(2,1)}, bf16[64,1024]{1,0:T(8,128)(2,1)}, bf16[64,1024]{1,0:T(8,128)(2,1)}, bf16[128,128]...) custom-call(s32[28]{0:T(128)} %concatenate.6.meta, ...), custom_call_target="tpu_custom_call" | custom-call | tf_op jit(solution)/shard_map/main/pallas_call | solution.py:394
  54.7 1.6 %collective-permute-start.16 = (bf16[416,128]{1,0:T(8,128)(2,1)}, bf16[416,128]{1,0:T(8,128)(2,1)S(1)}, u32[]{:S(2)}, u32[]{:S(2)}) collective-permute-start(bf16[416,128]{1,0:T(8,128)(2,1)} %get-tuple-element.56), channel_id=1, source_target_pairs={{0,16},{8,24},{16,0},{24,8},{1,17},{9,25},{17,1},{25,9},{2,18},{10... | collective-permute-start | bytes 319496 | tf_op jit(solution)/shard_map/ppermute | solution.py:407
  56.3 1.4 %collective-permute-start.17 = (bf16[416,128]{1,0:T(8,128)(2,1)}, bf16[416,128]{1,0:T(8,128)(2,1)S(1)}, u32[]{:S(2)}, u32[]{:S(2)}) collective-permute-start(bf16[416,128]{1,0:T(8,128)(2,1)} %get-tuple-element.57), channel_id=1, source_target_pairs={{0,24},{8,0},{16,8},{24,16},{1,25},{9,1},{17,9},{25,17},{2,26},{10... | collective-permute-start | bytes 319496 | tf_op jit(solution)/shard_map/ppermute | solution.py:407
  57.8 4.9 %collective-permute-done.15.r1 = bf16[416,128]{1,0:T(8,128)(2,1)S(1)} collective-permute-done((bf16[416,128]{1,0:T(8,128)(2,1)}, bf16[416,128]{1,0:T(8,128)(2,1)S(1)}, u32[]{:S(2)}, u32[]{:S(2)}) %collective-permute-start.15) | collective-permute-done | bytes 106528 | tf_op jit(solution)/shard_map/ppermute | solution.py:407
  63.4 1.8 %bundle.1 = (bf16[800,128]{1,0:T(8,128)(2,1)}, f32[144,128]{1,0:T(8,128)}) custom-call(bf16[128,128]{1,0:T(8,128)(2,1)} %get-tuple-element.53.rim, f32[144,128]{1,0:T(8,128)} %get-tuple-element.54.wown, bf16[416,128]{1,0:T(8,128)(2,1)} %copy-done.13, bf16[416,128]{1,0:T(8,128)(2,1)} %copy-done.14, bf16[416,128]{1,0:T(8,128)(2,1)} %copy-done.15), custom_call_target="tpu_custom_call" | custom-call | tf_op jit(solution)/shard_map/bundle/pallas_call | solution.py:394
  65.6 1.7 %collective-permute-start.19 = (bf16[800,128]{1,0:T(8,128)(2,1)}, bf16[800,128]{1,0:T(8,128)(2,1)S(1)}, u32[]{:S(2)}, u32[]{:S(2)}) collective-permute-start(bf16[800,128]{1,0:T(8,128)(2,1)} %get-tuple-element.59.b0), channel_id=1, source_target_pairs={{0,64},{32,96},{64,0},{96,32},{1,65},{33,97},{65,1},{97,33},{2,66}... | collective-permute-start | bytes 614408 | tf_op jit(solution)/shard_map/ppermute | solution.py:407
  67.9 2.4 %collective-permute-start.29 = (bf16[64,1024]{1,0:T(8,128)(2,1)}, bf16[64,1024]{1,0:T(8,128)(2,1)S(1)}, u32[]{:S(2)}, u32[]{:S(2)}) collective-permute-start(bf16[64,1024]{1,0:T(8,128)(2,1)} %get-tuple-element.72), channel_id=1, source_target_pairs={{0,1},{1,0},{2,3},{3,2},{4,5},{5,4},{6,7},{7,6},{8,9},{9,8},{10,11... | collective-permute-start | bytes 393224 | tf_op jit(solution)/shard_map/ppermute | solution.py:411
  70.4 1.6 %collective-permute-done.19.b2 = bf16[800,128]{1,0:T(8,128)(2,1)S(1)} collective-permute-done((bf16[800,128]{1,0:T(8,128)(2,1)}, bf16[800,128]{1,0:T(8,128)(2,1)S(1)}, u32[]{:S(2)}, u32[]{:S(2)}) %collective-permute-start.19) | collective-permute-done | bytes 204832 | tf_op jit(solution)/shard_map/ppermute | solution.py:407
  72.0 5.7 %collective-permute-done.18.b1 = bf16[800,128]{1,0:T(8,128)(2,1)S(1)} collective-permute-done((bf16[800,128]{1,0:T(8,128)(2,1)}, bf16[800,128]{1,0:T(8,128)(2,1)S(1)}, u32[]{:S(2)}, u32[]{:S(2)}) %collective-permute-start.18) | collective-permute-done | bytes 204832 | tf_op jit(solution)/shard_map/ppermute | solution.py:407
  77.7 0.7 copy-done.7
  78.4 3.4 %route_rims.1 = (bf16[272,128]{1,0:T(8,128)(2,1)}, bf16[272,128]{1,0:T(8,128)(2,1)}, bf16[272,128]{1,0:T(8,128)(2,1)}, bf16[272,128]{1,0:T(8,128)(2,1)}, bf16[27...) custom-call(s32[28]{0:T(128)} %concatenate.6.meta, ...), custom_call_target="tpu_custom_call" | custom-call | tf_op jit(solution)/shard_map/route_rims/pallas_call | solution.py:394
  81.9 2.2 %collective-permute-start.22 = (bf16[272,128]{1,0:T(8,128)(2,1)}, bf16[272,128]{1,0:T(8,128)(2,1)S(1)}, u32[]{:S(2)}, u32[]{:S(2)}) collective-permute-start(bf16[272,128]{1,0:T(8,128)(2,1)} %get-tuple-element.62), channel_id=1, source_target_pairs={{0,2},{1,3},{2,0},{3,1},{4,6},{5,7},{6,4},{7,5},{8,10},{9,11},{10,... | collective-permute-start | bytes 208904 | tf_op jit(solution)/shard_map/ppermute | solution.py:415
  84.1 2.4 %collective-permute-start.23 = (bf16[272,128]{1,0:T(8,128)(2,1)}, bf16[272,128]{1,0:T(8,128)(2,1)S(1)}, u32[]{:S(2)}, u32[]{:S(2)}) collective-permute-start(bf16[272,128]{1,0:T(8,128)(2,1)} %get-tuple-element.63), channel_id=1, source_target_pairs={{0,3},{1,2},{2,1},{3,0},{4,7},{5,6},{6,5},{7,4},{8,11},{9,10},{10,... | collective-permute-start | bytes 208904 | tf_op jit(solution)/shard_map/ppermute | solution.py:415
  86.4 2.1 %collective-permute-start.24 = (bf16[272,128]{1,0:T(8,128)(2,1)}, bf16[272,128]{1,0:T(8,128)(2,1)S(1)}, u32[]{:S(2)}, u32[]{:S(2)}) collective-permute-start(bf16[272,128]{1,0:T(8,128)(2,1)} %get-tuple-element.64), channel_id=1, source_target_pairs={{0,4},{1,5},{2,6},{3,7},{4,0},{5,1},{6,2},{7,3},{8,12},{9,13},{10,... | collective-permute-start | bytes 208904 | tf_op jit(solution)/shard_map/ppermute | solution.py:415
  88.6 0.9 collective-permute-start.25
  89.4 1.9 %collective-permute-start.26 = (bf16[272,128]{1,0:T(8,128)(2,1)}, bf16[272,128]{1,0:T(8,128)(2,1)S(1)}, u32[]{:S(2)}, u32[]{:S(2)}) collective-permute-start(bf16[272,128]{1,0:T(8,128)(2,1)} %get-tuple-element.66), channel_id=1, source_target_pairs={{0,6},{1,7},{2,4},{3,5},{4,2},{5,3},{6,0},{7,1},{8,14},{9,15},{10,... | collective-permute-start | bytes 208904 | tf_op jit(solution)/shard_map/ppermute | solution.py:415
  91.3 1.0 collective-permute-start.27
  92.3 0.8 collective-permute-done.25.r5
  93.1 1.4 %collective-permute-done.26.r6 = bf16[272,128]{1,0:T(8,128)(2,1)S(1)} collective-permute-done((bf16[272,128]{1,0:T(8,128)(2,1)}, bf16[272,128]{1,0:T(8,128)(2,1)S(1)}, u32[]{:S(2)}, u32[]{:S(2)}) %collective-permute-start.26) | collective-permute-done | bytes 69664 | tf_op jit(solution)/shard_map/ppermute | solution.py:415
  94.5 2.0 %collective-permute-done.27.r7 = bf16[272,128]{1,0:T(8,128)(2,1)S(1)} collective-permute-done((bf16[272,128]{1,0:T(8,128)(2,1)}, bf16[272,128]{1,0:T(8,128)(2,1)S(1)}, u32[]{:S(2)}, u32[]{:S(2)}) %collective-permute-start.27) | collective-permute-done | bytes 69664 | tf_op jit(solution)/shard_map/ppermute | solution.py:415
  97.1 3.8 %final.1 = (bf16[2,32,4096]{2,1,0:T(8,128)(2,1)}, bf16[2,64,1024]{2,1,0:T(8,128)(2,1)}, f32[72,128]{1,0:T(8,128)}) custom-call(s32[28]{0:T(128)} %concatenate.6.meta, bf16[272,128]{1,0:T(8,128)(2,1)} %get-tuple-element.60.own, bf16[272,128]{1,0:T(8,128)(2,1)} %copy-done.16, bf16[272,128]{1,0:T(8,128)(2,1)} %copy-done.17, bf16[272,128]{1,0:T(8,128)(2,1)} %copy-done.18, ...), custom_call_target="tpu_custom_call" | custom-call | tf_op jit(solution)/shard_map/final/pallas_call | solution.py:394
  100.9 3.0 %collective-permute-start.32 = (f32[72,128]{1,0:T(8,128)}, f32[72,128]{1,0:T(8,128)S(1)}, u32[]{:S(2)}, u32[]{:S(2)}) collective-permute-start(f32[72,128]{1,0:T(8,128)} %get-tuple-element.75.own), channel_id=1, source_target_pairs={{0,24},{8,0},{16,8},{24,16},{1,25},{9,1},{17,9},{25,17},{2,26},{10... | collective-permute-start | bytes 110600 | tf_op jit(solution)/shard_map/ppermute | solution.py:407
  104.6 1.7 %collective-permute-done.32.r3 = f32[72,128]{1,0:T(8,128)S(1)} collective-permute-done((f32[72,128]{1,0:T(8,128)}, f32[72,128]{1,0:T(8,128)S(1)}, u32[]{:S(2)}, u32[]{:S(2)}) %collective-permute-start.32) | collective-permute-done | bytes 36896 | tf_op jit(solution)/shard_map/ppermute | solution.py:407
  106.2 2.7 %collective-permute-done.31.r2 = f32[72,128]{1,0:T(8,128)S(1)} collective-permute-done((f32[72,128]{1,0:T(8,128)}, f32[72,128]{1,0:T(8,128)S(1)}, u32[]{:S(2)}, u32[]{:S(2)}) %collective-permute-start.31) | collective-permute-done | bytes 36896 | tf_op jit(solution)/shard_map/ppermute | solution.py:407
  110.1 1.6 %unpack.1 = (f32[9,32,64]{2,1,0:T(8,128)}, f32[4,32,128]{2,1,0:T(8,128)}) custom-call(s32[28]{0:T(128)} %concatenate.6.meta, f32[72,128]{1,0:T(8,128)} %get-tuple-element.75.own, f32[72,128]{1,0:T(8,128)} %copy-done.25, f32[72,128]{1,0:T(8,128)} %copy-done.24, f32[72,128]{1,0:T(8,128)} %copy-done.23), custom_call_target="tpu_custom_call" | custom-call | tf_op jit(solution)/shard_map/unpack/pallas_call | solution.py:394
  111.7 1.5 %copy.41 = f32[2,2,32,128]{3,1,0,2:T(2,128)} copy(f32[2,2,32,128]{3,2,1,0:T(8,128)} %bitcast.40) | data formatting | bytes 131072 | tf_op jit(solution)/shard_map/reshape | solution.py:499
  (110 shorter events, 7.7 us)
Async XLA Ops:
  2.2 40.3 %copy-start.3 = (bf16[128,64,2,2]{0,3,2,1:T(2,128)(2,1)S(1)}, bf16[128,64,2,2]{0,3,2,1:T(2,128)(2,1)}, u32[]{:S(2)}) copy-start(bf16[128,64,2,2]{0,3,2,1:T(2,128)(2,1)} %param.12) | copy-start | bytes 196612
  2.2 41.7 %copy-start.1 = (bf16[64,64,3,3]{1,0,3,2:T(8,128)(2,1)S(1)}, bf16[64,64,3,3]{1,0,3,2:T(8,128)(2,1)}, u32[]{:S(2)}) copy-start(bf16[64,64,3,3]{1,0,3,2:T(8,128)(2,1)} %param.11) | copy-start | bytes 221188
  5.4 4.7 %collective-permute-start.2 = (bf16[144,128]{1,0:T(8,128)(2,1)}, bf16[144,128]{1,0:T(8,128)(2,1)S(1)}, u32[]{:S(2)}, u32[]{:S(2)}) collective-permute-start(bf16[144,128]{1,0:T(8,128)(2,1)} %strips.1), channel_id=1, source_target_pairs={{0,24},{8,0},{16,8},{24,16},{1,25},{9,1},{17,9},{25,17},{2,26},{10... | collective-permute-start | bytes 110600 | tf_op jit(solution)/shard_map/ppermute | solution.py:407
  8.7 4.5 %collective-permute-start.1 = (bf16[144,128]{1,0:T(8,128)(2,1)}, bf16[144,128]{1,0:T(8,128)(2,1)S(1)}, u32[]{:S(2)}, u32[]{:S(2)}) collective-permute-start(bf16[144,128]{1,0:T(8,128)(2,1)} %strips.1), channel_id=1, source_target_pairs={{0,16},{8,24},{16,0},{24,8},{1,17},{9,25},{17,1},{25,9},{2,18},{10... | collective-permute-start | bytes 110600 | tf_op jit(solution)/shard_map/ppermute | solution.py:407
  9.2 4.4 %collective-permute-start = (bf16[144,128]{1,0:T(8,128)(2,1)}, bf16[144,128]{1,0:T(8,128)(2,1)S(1)}, u32[]{:S(2)}, u32[]{:S(2)}) collective-permute-start(bf16[144,128]{1,0:T(8,128)(2,1)} %strips.1), channel_id=1, source_target_pairs={{0,8},{8,16},{16,24},{24,0},{1,9},{9,17},{17,25},{25,1},{2,10},{10... | collective-permute-start | bytes 110600 | tf_op jit(solution)/shard_map/ppermute | solution.py:407
  14.4 12.0 %copy-start = (bf16[576,128]{1,0:T(8,128)(2,1)}, bf16[576,128]{1,0:T(8,128)(2,1)S(1)}, u32[]{:S(2)}) copy-start(bf16[576,128]{1,0:T(8,128)(2,1)S(1)} %pad_maximum_fusion.b0) | copy-start | bytes 442372
  14.4 9.4 %collective-permute-start.5 = (bf16[576,128]{1,0:T(8,128)(2,1)S(1)}, bf16[576,128]{1,0:T(8,128)(2,1)S(1)}, u32[]{:S(2)}, u32[]{:S(2)}) collective-permute-start(bf16[576,128]{1,0:T(8,128)(2,1)S(1)} %pad_maximum_fusion.b0), channel_id=1, source_target_pairs={{0,96},{32,0},{64,32},{96,64},{1,97},{33,1},{65,33},{97,65},{2,98}... | collective-permute-start | bytes 442376 | tf_op jit(solution)/shard_map/ppermute | solution.py:407
  18.2 5.6 %collective-permute-start.4 = (bf16[576,128]{1,0:T(8,128)(2,1)S(1)}, bf16[576,128]{1,0:T(8,128)(2,1)S(1)}, u32[]{:S(2)}, u32[]{:S(2)}) collective-permute-start(bf16[576,128]{1,0:T(8,128)(2,1)S(1)} %pad_maximum_fusion.b0), channel_id=1, source_target_pairs={{0,64},{32,96},{64,0},{96,32},{1,65},{33,97},{65,1},{97,33},{2,66}... | collective-permute-start | bytes 442376 | tf_op jit(solution)/shard_map/ppermute | solution.py:407
  18.2 7.4 %collective-permute-start.3 = (bf16[576,128]{1,0:T(8,128)(2,1)S(1)}, bf16[576,128]{1,0:T(8,128)(2,1)S(1)}, u32[]{:S(2)}, u32[]{:S(2)}) collective-permute-start(bf16[576,128]{1,0:T(8,128)(2,1)S(1)} %pad_maximum_fusion.b0), channel_id=1, source_target_pairs={{0,32},{32,64},{64,96},{96,0},{1,33},{33,65},{65,97},{97,1},{2,34}... | collective-permute-start | bytes 442376 | tf_op jit(solution)/shard_map/ppermute | solution.py:407
  20.8 16.0 %collective-permute-start.7 = (bf16[64,1024]{1,0:T(8,128)(2,1)}, bf16[64,1024]{1,0:T(8,128)(2,1)S(1)}, u32[]{:S(2)}, u32[]{:S(2)}) collective-permute-start(bf16[64,1024]{1,0:T(8,128)(2,1)} %get-tuple-element.42), channel_id=1, source_target_pairs={{0,1},{1,0},{2,3},{3,2},{4,5},{5,4},{6,7},{7,6},{8,9},{9,8},{10,11... | collective-permute-start | bytes 393224 | tf_op jit(solution)/shard_map/ppermute | solution.py:411
  23.7 23.4 %collective-permute-start.6 = (bf16[32,4096]{1,0:T(8,128)(2,1)}, bf16[32,4096]{1,0:T(8,128)(2,1)S(1)}, u32[]{:S(2)}, u32[]{:S(2)}) collective-permute-start(bf16[32,4096]{1,0:T(8,128)(2,1)} %get-tuple-element.41), channel_id=1, source_target_pairs={{0,1},{1,0},{2,3},{3,2},{4,5},{5,4},{6,7},{7,6},{8,9},{9,8},{10,11... | collective-permute-start | bytes 786440 | tf_op jit(solution)/shard_map/ppermute | solution.py:411
  30.3 7.8 %collective-permute-start.8 = (bf16[64,128]{1,0:T(8,128)(2,1)}, bf16[64,128]{1,0:T(8,128)(2,1)S(1)}, u32[]{:S(2)}, u32[]{:S(2)}) collective-permute-start(bf16[64,128]{1,0:T(8,128)(2,1)} %get-tuple-element.44), channel_id=1, source_target_pairs={{0,1},{1,0},{2,3},{3,2},{4,5},{5,4},{6,7},{7,6},{8,9},{9,8},{10,11... | collective-permute-start | bytes 49160 | tf_op jit(solution)/shard_map/ppermute | solution.py:415
  33.3 6.6 %collective-permute-start.9 = (bf16[64,128]{1,0:T(8,128)(2,1)}, bf16[64,128]{1,0:T(8,128)(2,1)S(1)}, u32[]{:S(2)}, u32[]{:S(2)}) collective-permute-start(bf16[64,128]{1,0:T(8,128)(2,1)} %get-tuple-element.45), channel_id=1, source_target_pairs={{0,2},{1,3},{2,0},{3,1},{4,6},{5,7},{6,4},{7,5},{8,10},{9,11},{10,... | collective-permute-start | bytes 49160 | tf_op jit(solution)/shard_map/ppermute | solution.py:415
  36.7 5.0 %collective-permute-start.10 = (bf16[64,128]{1,0:T(8,128)(2,1)}, bf16[64,128]{1,0:T(8,128)(2,1)S(1)}, u32[]{:S(2)}, u32[]{:S(2)}) collective-permute-start(bf16[64,128]{1,0:T(8,128)(2,1)} %get-tuple-element.46), channel_id=1, source_target_pairs={{0,3},{1,2},{2,1},{3,0},{4,7},{5,6},{6,5},{7,4},{8,11},{9,10},{10,... | collective-permute-start | bytes 49160 | tf_op jit(solution)/shard_map/ppermute | solution.py:415
  36.7 10.4 %copy-start.12 = (bf16[64,1024]{1,0:T(8,128)(2,1)}, bf16[64,1024]{1,0:T(8,128)(2,1)S(1)}, u32[]{:S(2)}) copy-start(bf16[64,1024]{1,0:T(8,128)(2,1)S(1)} %collective-permute-done.7.rcot) | copy-start | bytes 393220
  36.7 10.3 %collective-permute-start.11 = (bf16[64,128]{1,0:T(8,128)(2,1)}, bf16[64,128]{1,0:T(8,128)(2,1)S(1)}, u32[]{:S(2)}, u32[]{:S(2)}) collective-permute-start(bf16[64,128]{1,0:T(8,128)(2,1)} %get-tuple-element.47), channel_id=1, source_target_pairs={{0,4},{1,5},{2,6},{3,7},{4,0},{5,1},{6,2},{7,3},{8,12},{9,13},{10,... | collective-permute-start | bytes 49160 | tf_op jit(solution)/shard_map/ppermute | solution.py:415
  38.2 9.0 %copy-start.26 = (bf16[64,128]{1,0:T(8,128)(2,1)}, bf16[64,128]{1,0:T(8,128)(2,1)S(1)}, u32[]{:S(2)}) copy-start(bf16[64,128]{1,0:T(8,128)(2,1)S(1)} %collective-permute-done.8.h1) | copy-start | bytes 49156
  38.2 8.9 %collective-permute-start.12 = (bf16[64,128]{1,0:T(8,128)(2,1)}, bf16[64,128]{1,0:T(8,128)(2,1)S(1)}, u32[]{:S(2)}, u32[]{:S(2)}) collective-permute-start(bf16[64,128]{1,0:T(8,128)(2,1)} %get-tuple-element.48), channel_id=1, source_target_pairs={{0,5},{1,4},{2,7},{3,6},{4,1},{5,0},{6,3},{7,2},{8,13},{9,12},{10,... | collective-permute-start | bytes 49160 | tf_op jit(solution)/shard_map/ppermute | solution.py:415
  39.9 7.2 %copy-start.27 = (bf16[64,128]{1,0:T(8,128)(2,1)}, bf16[64,128]{1,0:T(8,128)(2,1)S(1)}, u32[]{:S(2)}) copy-start(bf16[64,128]{1,0:T(8,128)(2,1)S(1)} %collective-permute-done.9.h2) | copy-start | bytes 49156
  39.9 7.1 %collective-permute-start.13 = (bf16[64,128]{1,0:T(8,128)(2,1)}, bf16[64,128]{1,0:T(8,128)(2,1)S(1)}, u32[]{:S(2)}, u32[]{:S(2)}) collective-permute-start(bf16[64,128]{1,0:T(8,128)(2,1)} %get-tuple-element.49), channel_id=1, source_target_pairs={{0,6},{1,7},{2,4},{3,5},{4,2},{5,3},{6,0},{7,1},{8,14},{9,15},{10,... | collective-permute-start | bytes 49160 | tf_op jit(solution)/shard_map/ppermute | solution.py:415
  41.8 5.4 %copy-start.28 = (bf16[64,128]{1,0:T(8,128)(2,1)}, bf16[64,128]{1,0:T(8,128)(2,1)S(1)}, u32[]{:S(2)}) copy-start(bf16[64,128]{1,0:T(8,128)(2,1)S(1)} %collective-permute-done.10.h3) | copy-start | bytes 49156
  41.8 5.3 %collective-permute-start.14 = (bf16[64,128]{1,0:T(8,128)(2,1)}, bf16[64,128]{1,0:T(8,128)(2,1)S(1)}, u32[]{:S(2)}, u32[]{:S(2)}) collective-permute-start(bf16[64,128]{1,0:T(8,128)(2,1)} %get-tuple-element.50), channel_id=1, source_target_pairs={{0,7},{1,6},{2,5},{3,4},{4,3},{5,2},{6,1},{7,0},{8,15},{9,14},{10,... | collective-permute-start | bytes 49160 | tf_op jit(solution)/shard_map/ppermute | solution.py:415
  54.7 8.0 %collective-permute-start.15 = (bf16[416,128]{1,0:T(8,128)(2,1)}, bf16[416,128]{1,0:T(8,128)(2,1)S(1)}, u32[]{:S(2)}, u32[]{:S(2)}) collective-permute-start(bf16[416,128]{1,0:T(8,128)(2,1)} %get-tuple-element.55), channel_id=1, source_target_pairs={{0,8},{8,16},{16,24},{24,0},{1,9},{9,17},{17,25},{25,1},{2,10},{10... | collective-permute-start | bytes 319496 | tf_op jit(solution)/shard_map/ppermute | solution.py:407
  54.7 7.9 %collective-permute-start.16 = (bf16[416,128]{1,0:T(8,128)(2,1)}, bf16[416,128]{1,0:T(8,128)(2,1)S(1)}, u32[]{:S(2)}, u32[]{:S(2)}) collective-permute-start(bf16[416,128]{1,0:T(8,128)(2,1)} %get-tuple-element.56), channel_id=1, source_target_pairs={{0,16},{8,24},{16,0},{24,8},{1,17},{9,25},{17,1},{25,9},{2,18},{10... | collective-permute-start | bytes 319496 | tf_op jit(solution)/shard_map/ppermute | solution.py:407
  56.3 6.4 %collective-permute-start.17 = (bf16[416,128]{1,0:T(8,128)(2,1)}, bf16[416,128]{1,0:T(8,128)(2,1)S(1)}, u32[]{:S(2)}, u32[]{:S(2)}) collective-permute-start(bf16[416,128]{1,0:T(8,128)(2,1)} %get-tuple-element.57), channel_id=1, source_target_pairs={{0,24},{8,0},{16,8},{24,16},{1,25},{9,1},{17,9},{25,17},{2,26},{10... | collective-permute-start | bytes 319496 | tf_op jit(solution)/shard_map/ppermute | solution.py:407
  65.2 5.2 %collective-permute-start.20 = (bf16[800,128]{1,0:T(8,128)(2,1)}, bf16[800,128]{1,0:T(8,128)(2,1)S(1)}, u32[]{:S(2)}, u32[]{:S(2)}) collective-permute-start(bf16[800,128]{1,0:T(8,128)(2,1)} %get-tuple-element.59.b0), channel_id=1, source_target_pairs={{0,96},{32,0},{64,32},{96,64},{1,97},{33,1},{65,33},{97,65},{2,98}... | collective-permute-start | bytes 614408 | tf_op jit(solution)/shard_map/ppermute | solution.py:407
  65.6 6.4 %collective-permute-start.19 = (bf16[800,128]{1,0:T(8,128)(2,1)}, bf16[800,128]{1,0:T(8,128)(2,1)S(1)}, u32[]{:S(2)}, u32[]{:S(2)}) collective-permute-start(bf16[800,128]{1,0:T(8,128)(2,1)} %get-tuple-element.59.b0), channel_id=1, source_target_pairs={{0,64},{32,96},{64,0},{96,32},{1,65},{33,97},{65,1},{97,33},{2,66}... | collective-permute-start | bytes 614408 | tf_op jit(solution)/shard_map/ppermute | solution.py:407
  67.4 10.3 %collective-permute-start.18 = (bf16[800,128]{1,0:T(8,128)(2,1)}, bf16[800,128]{1,0:T(8,128)(2,1)S(1)}, u32[]{:S(2)}, u32[]{:S(2)}) collective-permute-start(bf16[800,128]{1,0:T(8,128)(2,1)} %get-tuple-element.59.b0), channel_id=1, source_target_pairs={{0,32},{32,64},{64,96},{96,0},{1,33},{33,65},{65,97},{97,1},{2,34}... | collective-permute-start | bytes 614408 | tf_op jit(solution)/shard_map/ppermute | solution.py:407
  67.4 21.2 %collective-permute-start.28 = (bf16[32,4096]{1,0:T(8,128)(2,1)}, bf16[32,4096]{1,0:T(8,128)(2,1)S(1)}, u32[]{:S(2)}, u32[]{:S(2)}) collective-permute-start(bf16[32,4096]{1,0:T(8,128)(2,1)} %get-tuple-element.70), channel_id=1, source_target_pairs={{0,1},{1,0},{2,3},{3,2},{4,5},{5,4},{6,7},{7,6},{8,9},{9,8},{10,11... | collective-permute-start | bytes 786440 | tf_op jit(solution)/shard_map/ppermute | solution.py:411
  67.9 18.5 %collective-permute-start.29 = (bf16[64,1024]{1,0:T(8,128)(2,1)}, bf16[64,1024]{1,0:T(8,128)(2,1)S(1)}, u32[]{:S(2)}, u32[]{:S(2)}) collective-permute-start(bf16[64,1024]{1,0:T(8,128)(2,1)} %get-tuple-element.72), channel_id=1, source_target_pairs={{0,1},{1,0},{2,3},{3,2},{4,5},{5,4},{6,7},{7,6},{8,9},{9,8},{10,11... | collective-permute-start | bytes 393224 | tf_op jit(solution)/shard_map/ppermute | solution.py:411
  70.4 7.3 %copy-start.5 = (bf16[800,128]{1,0:T(8,128)(2,1)}, bf16[800,128]{1,0:T(8,128)(2,1)S(1)}, u32[]{:S(2)}) copy-start(bf16[800,128]{1,0:T(8,128)(2,1)S(1)} %collective-permute-done.20.b3) | copy-start | bytes 614404
  72.0 5.7 %copy-start.6 = (bf16[800,128]{1,0:T(8,128)(2,1)}, bf16[800,128]{1,0:T(8,128)(2,1)S(1)}, u32[]{:S(2)}) copy-start(bf16[800,128]{1,0:T(8,128)(2,1)S(1)} %collective-permute-done.19.b2) | copy-start | bytes 614404
  81.8 7.6 %collective-permute-start.21 = (bf16[272,128]{1,0:T(8,128)(2,1)}, bf16[272,128]{1,0:T(8,128)(2,1)S(1)}, u32[]{:S(2)}, u32[]{:S(2)}) collective-permute-start(bf16[272,128]{1,0:T(8,128)(2,1)} %get-tuple-element.61), channel_id=1, source_target_pairs={{0,1},{1,0},{2,3},{3,2},{4,5},{5,4},{6,7},{7,6},{8,9},{9,8},{10,11... | collective-permute-start | bytes 208904 | tf_op jit(solution)/shard_map/ppermute | solution.py:415
  81.9 9.5 %collective-permute-start.22 = (bf16[272,128]{1,0:T(8,128)(2,1)}, bf16[272,128]{1,0:T(8,128)(2,1)S(1)}, u32[]{:S(2)}, u32[]{:S(2)}) collective-permute-start(bf16[272,128]{1,0:T(8,128)(2,1)} %get-tuple-element.62), channel_id=1, source_target_pairs={{0,2},{1,3},{2,0},{3,1},{4,6},{5,7},{6,4},{7,5},{8,10},{9,11},{10,... | collective-permute-start | bytes 208904 | tf_op jit(solution)/shard_map/ppermute | solution.py:415
  84.1 8.2 %collective-permute-start.23 = (bf16[272,128]{1,0:T(8,128)(2,1)}, bf16[272,128]{1,0:T(8,128)(2,1)S(1)}, u32[]{:S(2)}, u32[]{:S(2)}) collective-permute-start(bf16[272,128]{1,0:T(8,128)(2,1)} %get-tuple-element.63), channel_id=1, source_target_pairs={{0,3},{1,2},{2,1},{3,0},{4,7},{5,6},{6,5},{7,4},{8,11},{9,10},{10,... | collective-permute-start | bytes 208904 | tf_op jit(solution)/shard_map/ppermute | solution.py:415
  86.4 10.0 %copy-start.11 = (bf16[64,1024]{1,0:T(8,128)(2,1)}, bf16[64,1024]{1,0:T(8,128)(2,1)S(1)}, u32[]{:S(2)}) copy-start(bf16[64,1024]{1,0:T(8,128)(2,1)S(1)} %collective-permute-done.29.lvr) | copy-start | bytes 393220
  86.4 5.9 %collective-permute-start.24 = (bf16[272,128]{1,0:T(8,128)(2,1)}, bf16[272,128]{1,0:T(8,128)(2,1)S(1)}, u32[]{:S(2)}, u32[]{:S(2)}) collective-permute-start(bf16[272,128]{1,0:T(8,128)(2,1)} %get-tuple-element.64), channel_id=1, source_target_pairs={{0,4},{1,5},{2,6},{3,7},{4,0},{5,1},{6,2},{7,3},{8,12},{9,13},{10,... | collective-permute-start | bytes 208904 | tf_op jit(solution)/shard_map/ppermute | solution.py:415
  88.6 7.9 %copy-start.2 = (bf16[32,4096]{1,0:T(8,128)(2,1)}, bf16[32,4096]{1,0:T(8,128)(2,1)S(1)}, u32[]{:S(2)}) copy-start(bf16[32,4096]{1,0:T(8,128)(2,1)S(1)} %collective-permute-done.28.gxr) | copy-start | bytes 786436
  88.6 4.6 %collective-permute-start.25 = (bf16[272,128]{1,0:T(8,128)(2,1)}, bf16[272,128]{1,0:T(8,128)(2,1)S(1)}, u32[]{:S(2)}, u32[]{:S(2)}) collective-permute-start(bf16[272,128]{1,0:T(8,128)(2,1)} %get-tuple-element.65), channel_id=1, source_target_pairs={{0,5},{1,4},{2,7},{3,6},{4,1},{5,0},{6,3},{7,2},{8,13},{9,12},{10,... | collective-permute-start | bytes 208904 | tf_op jit(solution)/shard_map/ppermute | solution.py:415
  89.4 7.1 %copy-start.16 = (bf16[272,128]{1,0:T(8,128)(2,1)}, bf16[272,128]{1,0:T(8,128)(2,1)S(1)}, u32[]{:S(2)}) copy-start(bf16[272,128]{1,0:T(8,128)(2,1)S(1)} %collective-permute-done.21.r1) | copy-start | bytes 208900
  89.4 5.1 %collective-permute-start.26 = (bf16[272,128]{1,0:T(8,128)(2,1)}, bf16[272,128]{1,0:T(8,128)(2,1)S(1)}, u32[]{:S(2)}, u32[]{:S(2)}) collective-permute-start(bf16[272,128]{1,0:T(8,128)(2,1)} %get-tuple-element.66), channel_id=1, source_target_pairs={{0,6},{1,7},{2,4},{3,5},{4,2},{5,3},{6,0},{7,1},{8,14},{9,15},{10,... | collective-permute-start | bytes 208904 | tf_op jit(solution)/shard_map/ppermute | solution.py:415
  91.3 5.2 %copy-start.17 = (bf16[272,128]{1,0:T(8,128)(2,1)}, bf16[272,128]{1,0:T(8,128)(2,1)S(1)}, u32[]{:S(2)}) copy-start(bf16[272,128]{1,0:T(8,128)(2,1)S(1)} %collective-permute-done.22.r2) | copy-start | bytes 208900
  91.3 5.2 %collective-permute-start.27 = (bf16[272,128]{1,0:T(8,128)(2,1)}, bf16[272,128]{1,0:T(8,128)(2,1)S(1)}, u32[]{:S(2)}, u32[]{:S(2)}) collective-permute-start(bf16[272,128]{1,0:T(8,128)(2,1)} %get-tuple-element.67), channel_id=1, source_target_pairs={{0,7},{1,6},{2,5},{3,4},{4,3},{5,2},{6,1},{7,0},{8,15},{9,14},{10,... | collective-permute-start | bytes 208904 | tf_op jit(solution)/shard_map/ppermute | solution.py:415
  92.3 4.2 %copy-start.18 = (bf16[272,128]{1,0:T(8,128)(2,1)}, bf16[272,128]{1,0:T(8,128)(2,1)S(1)}, u32[]{:S(2)}) copy-start(bf16[272,128]{1,0:T(8,128)(2,1)S(1)} %collective-permute-done.23.r3) | copy-start | bytes 208900
  92.3 4.2 %copy-start.19 = (bf16[272,128]{1,0:T(8,128)(2,1)}, bf16[272,128]{1,0:T(8,128)(2,1)S(1)}, u32[]{:S(2)}) copy-start(bf16[272,128]{1,0:T(8,128)(2,1)S(1)} %collective-permute-done.24.r4) | copy-start | bytes 208900
  100.9 5.4 %collective-permute-start.32 = (f32[72,128]{1,0:T(8,128)}, f32[72,128]{1,0:T(8,128)S(1)}, u32[]{:S(2)}, u32[]{:S(2)}) collective-permute-start(f32[72,128]{1,0:T(8,128)} %get-tuple-element.75.own), channel_id=1, source_target_pairs={{0,24},{8,0},{16,8},{24,16},{1,25},{9,1},{17,9},{25,17},{2,26},{10... | collective-permute-start | bytes 110600 | tf_op jit(solution)/shard_map/ppermute | solution.py:407
  103.9 5.0 %collective-permute-start.31 = (f32[72,128]{1,0:T(8,128)}, f32[72,128]{1,0:T(8,128)S(1)}, u32[]{:S(2)}, u32[]{:S(2)}) collective-permute-start(f32[72,128]{1,0:T(8,128)} %get-tuple-element.75.own), channel_id=1, source_target_pairs={{0,16},{8,24},{16,0},{24,8},{1,17},{9,25},{17,1},{25,9},{2,18},{10... | collective-permute-start | bytes 110600 | tf_op jit(solution)/shard_map/ppermute | solution.py:407
  103.9 5.5 %collective-permute-start.30 = (f32[72,128]{1,0:T(8,128)}, f32[72,128]{1,0:T(8,128)S(1)}, u32[]{:S(2)}, u32[]{:S(2)}) collective-permute-start(f32[72,128]{1,0:T(8,128)} %get-tuple-element.75.own), channel_id=1, source_target_pairs={{0,8},{8,16},{16,24},{24,0},{1,9},{9,17},{17,25},{25,1},{2,10},{10... | collective-permute-start | bytes 110600 | tf_op jit(solution)/shard_map/ppermute | solution.py:407
  (18 other events, 22.1 us)

commit v2 on v1

v2 whole, which is shorter than its diff:
```python
import functools

import jax
import jax.numpy as jnp
import numpy as np
from jax import lax
from jax.experimental import pallas as pl
from jax.experimental.pallas import tpu as pltpu
from jax.sharding import Mesh
from jax.sharding import PartitionSpec as P

BF = jnp.bfloat16
F32 = jnp.float32
NT = (((1,), (1,)), ((), ()))
SQ = float(np.sqrt(2.0 / np.pi))


def constants():
    perm = np.zeros((512, 512), np.float32)
    for i in range(8):
        for j in range(64):
            perm[i * 64 + j, ((i % 2) * 2 + j % 2) * 128 + (i // 2) * 32 + j // 2] = 1
    edge = np.zeros((128, 2048), np.float32)
    pick = np.zeros((4096, 128), np.float32)
    for side in range(2):
        for a in range(2):
            for x in range(32):
                k = side * 64 + a * 32 + x
                edge[k, a * 1024 + x * 32 + 31 * side] = 1
                pick[(2 * x + a) * 64 + 63 * side, k] = 1
    ends = np.zeros((256, 128), np.float32)
    for b in range(2):
        for y in range(32):
            ends[2 * y + b, b * 32 + y] = 1
            ends[128 + 64 + 2 * y + b, 64 + b * 32 + y] = 1
    rev = np.zeros((128, 128), np.float32)
    for half in range(2):
        for i in range(64):
            rev[half * 64 + i, half * 64 + 63 - i] = 1
    return [jnp.asarray(m, BF) for m in (perm, edge, pick, ends, rev)]


def dot(a, b):
    return jnp.dot(a, b, preferred_element_type=F32)


def dot_nt(a, b):
    return lax.dot_general(a, b, NT, preferred_element_type=F32)


def al(v, m):
    return pl.multiple_of(v, m)


def split(v):
    hi = v.astype(BF)
    return hi, (v - hi.astype(F32)).astype(BF)


def strips_kernel(glue, inp, cot, pick, ends, out, send):
    both = inp[...].reshape(64, 4096)
    lr = dot(both, pick[...]).astype(BF)
    tb = dot(jnp.concatenate([both[:, :128], both[:, 3968:]], axis=1), ends[...]).astype(BF)
    lane = lax.broadcasted_iota(jnp.int32, (16, 128), 1)
    codes = jnp.zeros((16, 128), jnp.int32)
    for tile in range(2):
        for side in range(4):
            t, s = glue[0, tile, side], glue[1, tile, side]
            k = tile * 4 + side
            codes = jnp.where(lane == k, t >> 3, codes)
            codes = jnp.where(lane == k + 8, (t & 7) * 4 + s, codes)
    codes = codes.astype(F32).astype(BF)
    for d in range(16):
        for tile in range(2):
            out[d, tile * 64 : tile * 64 + 32, :] = tb[tile * 32 : tile * 32 + 32]
            out[d, tile * 64 + 32 : tile * 64 + 64, :] = lr[tile * 32 : tile * 32 + 32]
        out[d, 128:144, :] = codes
    o = 1 - lax.axis_index("h")
    send[:, :4096] = inp[o]
    send[:, 4096:5120] = cot[o, :32]
    send[:, 5120:] = cot[o, 32:]


def weight_kernel(w, lwc, wb, wbt, lw, lwt):
    wb[...] = jnp.zeros((256, 1024), BF)
    for a in range(2):
        for b in range(2):
            ab = (a * 2 + b) * 64
            for i in range(3):
                for j in range(3):
                    rs = ((a + i) * 4 + b + j) * 64
                    wb[ab : ab + 64, rs : rs + 64] = w[i, j]
    wbt[...] = wb[...].T
    row = lax.broadcasted_iota(jnp.int32, (256, 256), 0)
    col = lax.broadcasted_iota(jnp.int32, (256, 256), 1)
    order = jnp.where((row & 63) * 4 + (row >> 6) == col, 1.0, 0.0).astype(BF)
    v = dot(order, lwc[...]).astype(BF)
    lwt[...] = v
    lw[...] = v.T


def place(acc, row, v, flip_half, dst_side, half):
    v = pltpu.roll(v, flip_half * 64, 1)
    acc[pl.ds(row, 32), :] = jnp.where(half == (dst_side & 1), v, acc[pl.ds(row, 32), :])


def route_strips_kernel(codes, got, out, acc):
    acc[...] = jnp.zeros((512, 128), F32)
    half = lax.broadcasted_iota(jnp.int32, (32, 128), 1) // 64

    @pl.loop(0, 16)
    def _(i):
        for m in range(8):
            c = codes[i * 8 + m]
            r = m & 3

            @pl.when(c >= 0)
            def _(m=m, c=c, r=r):
                v = got[i, (m >> 1) * 32 : (m >> 1) * 32 + 32, :].astype(F32)
                place(acc, al((c >> 1) * 32, 32), v, (r ^ c) & 1, c, half)

    for k in range(8):
        out[k] = acc[k * 64 : k * 64 + 64, :].astype(BF)


def flip(strips, rev, first, second):
    n = strips.shape[0]
    turned = dot(strips.astype(BF), rev)
    lane = lax.broadcasted_iota(jnp.int32, (n, 128), 1)
    flag = jnp.where(lane < 64, first, second)
    return jnp.where(flag == 1, turned, strips)


def main_kernel(
    glue, inp, rcv, cot, halo, wb, wbt, lw, lwt, perm, edge, rev,
    keep, send, pay,
    xs, pt, ct, pre_s, gh_s, hd, gp, wh, gs, lv_s,
):
    h = lax.axis_index("h")
    mine, other = h * 32, 32 - h * 32
    for g in range(8):
        xs[pl.ds(al(g * 64 + mine, 32), 32), :] = inp[h, :, g * 512 : g * 512 + 512]
        xs[pl.ds(al(g * 64 + other, 32), 32), :] = rcv[:, g * 512 : g * 512 + 512]
    ct[pl.ds(al(h * 64, 64), 64), :] = cot[h]
    ct[pl.ds(al(64 - h * 64, 64), 32), :] = rcv[:, 4096:5120]
    ct[pl.ds(al(96 - h * 64, 32), 32), :] = rcv[:, 5120:]
    nat = dot(xs[...], perm[...])
    ph = [
        [
            jnp.concatenate(
                [nat[g * 64 : g * 64 + 64, (a * 2 + b) * 128 : (a * 2 + b) * 128 + 128] for g in range(8)],
                axis=1,
            )
            for b in range(2)
        ]
        for a in range(2)
    ]
    parts = []
    for q in range(2):
        t = [halo[k].astype(F32) for k in range(q, 8, 2)]
        parts.append((t[0] + t[1]) + (t[2] + t[3]))
    tb, lr = (
        jnp.concatenate([parts[0][k : k + 32], parts[1][k : k + 32]], axis=0) for k in (0, 32)
    )
    fl = [glue[2, h, s] for s in range(4)]
    tb = flip(tb, rev[...], fl[0], fl[1])
    lr = flip(lr, rev[...], fl[2], fl[3])
    sp = dot(lr.astype(BF), edge[...])
    lane = lax.broadcasted_iota(jnp.int32, (64, 1024), 1)
    y = lane & 31
    l1 = lax.broadcasted_iota(jnp.int32, (64, 128), 1)
    cols = [[None] * 4 for _ in range(2)]
    for a in range(2):
        spa = sp[:, a * 1024 : a * 1024 + 1024]
        cols[a][0] = jnp.where(y == 0, spa, pltpu.roll(ph[a][1], 1, 1))
        cols[a][1] = ph[a][0]
        cols[a][2] = ph[a][1]
        cols[a][3] = jnp.where(y == 31, spa, pltpu.roll(ph[a][0], 1023, 1))
    top_shift = (97, 0, 96, 127)
    low_shift = (1, 32, 0, 31)
    for s in range(4):
        pt[(4 + s) * 64 : (4 + s) * 64 + 64, :] = cols[0][s].astype(BF)
        pt[(8 + s) * 64 : (8 + s) * 64 + 64, :] = cols[1][s].astype(BF)
        up = pltpu.roll(cols[1][s], 32, 1)
        t = pltpu.roll(tb, top_shift[s], 1) if top_shift[s] else tb
        if s == 0:
            t = jnp.where(l1 == 0, 0.0, t)
        if s == 3:
            t = jnp.where(l1 == 31, 0.0, t)
        pt[s * 64 : s * 64 + 64, 128:] = up[:, 128:].astype(BF)
        pt[s * 64 : s * 64 + 64, :128] = jnp.where(l1 < 32, t, up[:, :128]).astype(BF)
        dn = pltpu.roll(cols[0][s], 992, 1)
        t = pltpu.roll(tb, low_shift[s], 1) if low_shift[s] else tb
        if s == 0:
            t = jnp.where(l1 == 96, 0.0, t)
        if s == 3:
            t = jnp.where(l1 == 127, 0.0, t)
        pt[(12 + s) * 64 : (12 + s) * 64 + 64, :896] = dn[:, :896].astype(BF)
        pt[(12 + s) * 64 : (12 + s) * 64 + 64, 896:] = jnp.where(l1 >= 96, t, dn[:, 896:]).astype(BF)
    pre_s[...] = dot(wb[...], pt[...])
    gh_s[...] = dot(lwt[...], ct[...])
    for q in range(8):
        rows = slice(q * 32, q * 32 + 32)
        v = pre_s[rows, :]
        v2 = v * v
        th = jnp.tanh(SQ * (v + 0.044715 * (v2 * v)))
        half = 0.5 * (1.0 + th)
        hd[rows, :] = (v * half).astype(BF)
        d = half + 0.5 * v * (1.0 - th * th) * (SQ * (1.0 + 3 * 0.044715 * v2))
        gp[rows, :] = (gh_s[rows, :] * d).astype(BF)
    gx = dot(wbt[...], gp[...])

    def blk(r, s):
        k = (r * 4 + s) * 64
        return gx[k : k + 64]

    x0 = lane < 32
    x31 = lane >= 992

    def down(v):
        return jnp.where(x0, 0.0, pltpu.roll(v, 32, 1))

    def up_(v):
        return jnp.where(x31, 0.0, pltpu.roll(v, 992, 1))

    qs, ms = [], []
    for r in range(4):
        q0 = blk(r, 1) + jnp.where(y == 0, 0.0, pltpu.roll(blk(r, 3), 1, 1))
        q1 = blk(r, 2) + jnp.where(y == 31, 0.0, pltpu.roll(blk(r, 0), 1023, 1))
        qs.append((q0, q1))
        ms.append(jnp.where(y == 0, blk(r, 0), jnp.where(y == 31, blk(r, 3), 0.0)))
    top = jnp.where(l1 < 32, qs[0][0][:, :128], pltpu.roll(qs[0][1][:, :128], 32, 1))
    low = jnp.where(l1 < 96, pltpu.roll(qs[3][0][:, 896:], 96, 1), qs[3][1][:, 896:])
    rim_tb = jnp.where(l1 < 64, top, low).astype(BF)
    a0 = (ms[1] + down(ms[3])).astype(BF)
    a1 = (ms[2] + up_(ms[0])).astype(BF)
    rim_lr = dot_nt(a0, edge[:, :1024]) + dot_nt(a1, edge[:, 1024:])
    rim_lr = rim_lr.astype(BF)
    for d in range(16):
        pay[d, 0:64, :] = rim_tb
        pay[d, 64:128, :] = rim_lr
    dl = dot_nt(hd[...], ct[...])
    gbt = dot_nt(pt[...], gp[...])
    packed = []
    for ij in range(9):
        i, j = divmod(ij, 3)
        u = v = None
        for a in range(2):
            k = ((a + i) * 4 + j) * 64
            ua = gbt[k : k + 64, a * 128 : a * 128 + 128]
            va = gbt[k + 64 : k + 128, a * 128 : a * 128 + 128]
            u = ua if u is None else u + ua
            v = va if v is None else v + va
        if ij % 2 == 0:
            packed.append(jnp.where(l1 < 64, u + pltpu.roll(v, 64, 1), 0.0))
        else:
            packed[-1] = jnp.where(l1 < 64, packed[-1], v + pltpu.roll(u, 64, 1))
    for hh in range(2):
        base = hh * 384
        for q in range(5):
            wh[base + q * 32 : base + q * 32 + 32, :] = packed[q][hh * 32 : hh * 32 + 32]
        for ab in range(4):
            row = base + 160 + ab * 32
            wh[row : row + 32, :] = dl[ab * 64 + hh * 32 : ab * 64 + hh * 32 + 32]
        wh[base + 288 : base + 384, :] = jnp.zeros((96, 128), F32)
    for d in range(16):
        chunk = jnp.concatenate([wh[d * 24 : d * 24 + 24, :], wh[384 + d * 24 : 408 + d * 24, :]], axis=0)
        hi, lo = split(chunk)
        pay[d, 128:176, :] = hi
        pay[d, 176:224, :] = lo
    lv_s[...] = dot(lw[...], hd[...]).astype(BF)
    for b in range(2):
        gs[:, b * 1024 : b * 1024 + 1024] = (qs[1][b] + down(qs[3][b])).astype(BF)
        gs[:, 2048 + b * 1024 : 3072 + b * 1024] = (qs[2][b] + up_(qs[0][b])).astype(BF)
    for ref, row in ((keep, h * 32), (send, 32 - h * 32)):
        ref[:, :4096] = gs[pl.ds(al(row, 32), 32), :]
        ref[:, 4096:5120] = lv_s[pl.ds(al(row * 2, 64), 32), :]
        ref[:, 5120:] = lv_s[pl.ds(al(row * 2 + 32, 32), 32), :]


def route_rims_kernel(codes, got, out, acc):
    acc[...] = jnp.zeros((1024, 128), F32)
    half = lax.broadcasted_iota(jnp.int32, (32, 128), 1) // 64
    h = lax.axis_index("h")

    @pl.loop(0, 16)
    def _(i):
        for r in range(4):
            c = codes[i * 8 + h * 4 + r]

            @pl.when(c >= 0)
            def _(c=c, r=r):
                t, s = c >> 2, c & 3
                for hh in range(2):
                    row = (r >> 1) * 64 + hh * 32
                    v = got[i, row : row + 32, :].astype(F32)
                    dst = ((t & 6) | hh) * 128 + (t & 1) * 64 + (s >> 1) * 32
                    place(acc, al(dst, 32), v, (r ^ s) & 1, s, half)

    w = None
    for i in range(16):
        v = got[i, 128:176, :].astype(F32) + got[i, 176:224, :].astype(F32)
        w = v if w is None else w + v
    pieces = []
    for q in range(2):
        hi, lo = split(w[q * 24 : q * 24 + 24])
        pieces.append(jnp.concatenate([hi.astype(F32), lo.astype(F32)], axis=0).astype(BF))
    for k in range(8):
        out[k, 0:128, :] = acc[k * 128 : k * 128 + 128, :].astype(BF)
        out[k, 128:176, :] = pieces[k & 1]


def final_kernel(glue, ret, keep, rcv, perm, edge, rev, gin, lev, wout, gs, xs):
    h = lax.axis_index("h")
    acc = w = None
    for k in range(8):
        v = ret[k, 0:128, :].astype(F32)
        p = ret[k, 128:176, :].astype(F32)
        p = p[0:24] + p[24:48]
        acc = v if acc is None else acc + v
        w = p if w is None else w + p
    for d in range(16):
        wout[d] = w
    lane = lax.broadcasted_iota(jnp.int32, (128, 128), 1)
    row = lax.broadcasted_iota(jnp.int32, (128, 128), 0)
    flag = jnp.zeros((128, 128), jnp.int32)
    for tile in range(2):
        for side in range(4):
            here = ((row >> 5) == tile * 2 + (side >> 1)) & ((lane >> 6) == (side & 1))
            flag = jnp.where(here, glue[2, tile, side], flag)
    turned = dot(acc.astype(BF), rev[...])
    acc = jnp.where(flag == 1, turned, acc)
    tb = jnp.concatenate([acc[0:32], acc[64:96]], axis=0)
    lr = jnp.concatenate([acc[32:64], acc[96:128]], axis=0)
    sp = dot(lr.astype(BF), edge[...])
    gs[pl.ds(al(h * 32, 32), 32), :] = keep[:, :4096]
    gs[pl.ds(al(32 - h * 32, 32), 32), :] = rcv[:, :4096]
    y = lax.broadcasted_iota(jnp.int32, (64, 1024), 1) & 31
    l1 = lax.broadcasted_iota(jnp.int32, (64, 128), 1)
    for a in range(2):
        for b in range(2):
            ab = a * 2 + b
            v = gs[:, ab * 1024 : ab * 1024 + 1024].astype(F32)
            v = v + jnp.where(y == 31 * b, sp[:, a * 1024 : a * 1024 + 1024], 0.0)
            shift = ((0, 96), (32, 0))[a][b]
            t = pltpu.roll(tb, shift, 1) if shift else tb
            t = jnp.where((l1 >= 96) if a else (l1 < 32), t, 0.0)
            for g in range(8):
                part = v[:, g * 128 : g * 128 + 128]
                if g == 7 * a:
                    part = part + t
                xs[g * 64 : g * 64 + 64, ab * 128 : ab * 128 + 128] = part.astype(BF)
    nat = dot_nt(xs[...], perm[...]).astype(BF)
    for g in range(8):
        for tile in range(2):
            k = g * 64 + tile * 32
            gin[tile, :, g * 512 : g * 512 + 512] = nat[k : k + 32]
    for tile, src in ((h, keep), (1 - h, rcv)):
        lev[tile, :32] = src[:, 4096:5120]
        lev[tile, 32:] = src[:, 5120:]


def unpack_kernel(ws, gc, gl):
    w = ws[...].reshape(384, 128)
    for ij in range(9):
        v = w[(ij // 2) * 32 : (ij // 2) * 32 + 32, :]
        if ij % 2:
            v = pltpu.roll(v, 64, 1)
        gc[ij] = v[:, :64]
    for ab in range(4):
        gl[ab] = w[160 + ab * 32 : 192 + ab * 32, :]


def call(kernel, outs, args, smem, scratch=(), name=None):
    specs = [
        pl.BlockSpec(memory_space=pltpu.SMEM if i < smem else pltpu.VMEM) for i in range(len(args))
    ]
    single = not isinstance(outs, list)
    shapes = [outs] if single else outs
    res = pl.pallas_call(
        kernel,
        out_shape=[jax.ShapeDtypeStruct(s, d) for s, d in shapes],
        in_specs=specs,
        out_specs=[pl.BlockSpec(memory_space=pltpu.VMEM) for _ in shapes],
        scratch_shapes=list(scratch),
        compiler_params=pltpu.CompilerParams(vmem_limit_bytes=58 << 20),
        name=name,
    )(*args)
    return res[0] if single else res


def swap(v):
    return lax.ppermute(v, "h", [(0, 1), (1, 0)])


def plane(v):
    return lax.all_to_all(v, ("z", "x"), 0, 0)


def octet(v):
    return lax.all_to_all(v, ("l", "c", "h"), 0, 0)


def on_device(inputs, gluing, conv_weight, level_weight, cotangent):
    perm, edge, pick, ends, rev = constants()
    glue = jnp.transpose(gluing, (2, 0, 1))
    strips, send = call(
        strips_kernel,
        [((16, 144, 128), BF), ((32, 6144), BF)],
        (glue, inputs, cotangent, pick, ends),
        1,
        name="strips",
    )
    rcv = swap(send)
    got = plane(strips)
    here = (lax.axis_index("z") * 4 + lax.axis_index("x")).astype(BF)
    codes = jnp.where(got[:, 128, :8] == here, got[:, 128, 8:16], -1).astype(jnp.int32).reshape(128)
    routed = call(
        route_strips_kernel,
        ((8, 64, 128), BF),
        (codes, got),
        1,
        [pltpu.VMEM((512, 128), F32)],
        name="route_strips",
    )
    halos = octet(routed)
    w9 = jnp.transpose(conv_weight, (2, 3, 0, 1))
    lwc = jnp.transpose(level_weight, (1, 2, 3, 0)).reshape(256, 128)
    wb, wbt, lw, lwt = call(
        weight_kernel,
        [((256, 1024), BF), ((1024, 256), BF), ((128, 256), BF), ((256, 128), BF)],
        (w9, lwc),
        0,
        name="weights",
    )
    keep, back, pay = call(
        main_kernel,
        [((32, 6144), BF), ((32, 6144), BF), ((16, 224, 128), BF)],
        (glue, inputs, rcv, cotangent, halos, wb, wbt, lw, lwt, perm, edge, rev),
        1,
        [
            pltpu.VMEM((512, 512), BF), pltpu.VMEM((1024, 1024), BF), pltpu.VMEM((128, 1024), BF),
            pltpu.VMEM((256, 1024), F32), pltpu.VMEM((256, 1024), F32), pltpu.VMEM((256, 1024), BF),
            pltpu.VMEM((256, 1024), BF), pltpu.VMEM((768, 128), F32), pltpu.VMEM((64, 4096), BF),
            pltpu.VMEM((128, 1024), BF),
        ],
        name="main",
    )
    rback = swap(back)
    rims = plane(pay)
    outgoing = call(
        route_rims_kernel,
        ((8, 176, 128), BF),
        (codes, rims),
        1,
        [pltpu.VMEM((1024, 128), F32)],
        name="route_rims",
    )
    ret = octet(outgoing)
    gin, lev, wrep = call(
        final_kernel,
        [((2, 32, 4096), BF), ((2, 64, 1024), BF), ((16, 24, 128), F32)],
        (glue, ret, keep, rback, perm, edge, rev),
        1,
        [pltpu.VMEM((64, 4096), BF), pltpu.VMEM((512, 512), BF)],
        name="final",
    )
    wall = plane(wrep)
    gc, gl = call(
        unpack_kernel, [((9, 32, 64), F32), ((4, 32, 128), F32)], (wall,), 0, name="unpack"
    )
    grad_conv = jnp.transpose(gc.reshape(3, 3, 32, 64), (3, 2, 0, 1))
    grad_level = jnp.transpose(gl.reshape(2, 2, 32, 128), (3, 2, 0, 1))
    return lev, gin, grad_conv, grad_level


def solution(mesh):
    fine = Mesh(mesh.devices.reshape(4, 4, 2, 2, 2), ("z", "x", "l", "c", "h"))
    tile = ("z", "x", "l", "c")
    return jax.shard_map(
        on_device,
        mesh=fine,
        in_specs=(
            P(tile, "h", None),
            P(tile, None, None),
            P(),
            P(),
            P(tile, "h", None),
        ),
        out_specs=(
            P(tile, "h", None),
            P(tile, "h", None),
            P(None, "h", None, None),
            P(None, "h", None, None),
        ),
        check_vma=False,
    )
```

time: 114 us -> 102 us (0.89)
  starting transfers between devices: 46.5 us -> 28.1 us
  blocking collectives: 0 us -> 12.1 us
  waiting for transfers between devices: 26.9 us -> 33.2 us
  Pallas kernels: 28.9 us -> 22.6 us
  local copies, waits for them, and re-layouts: 9.32 us -> 4.57 us
    ppermute x29 -> x0, starting transfers between devices: 40.5 us -> none  [the longest x14 22.6 us: octet(): return lax.ppermute(v, ('l', 'c', 'h'), [(i, i ^ k) for i in range(8)])]
    all_to_all x0 -> x4, waiting for transfers between devices: none -> 33.2 us  [the longest x2 22.5 us: plane(): return lax.all_to_all(v, ('z', 'x'), 0, 0)]
    ppermute x29 -> x0, waiting for transfers between devices: 26.9 us -> none  [the longest x15 22.7 us: ring(): return lax.ppermute(v, axis, [(i, (i + k) % 4) for i in range(4)])]
    all_to_all x0 -> x4, starting transfers between devices: none -> 24.3 us  [the longest x2 12.3 us: plane(): return lax.all_to_all(v, ('z', 'x'), 0, 0)]
    all_to_all x0 -> x1, blocking collectives: none -> 12.1 us  [plane(): return lax.all_to_all(v, ('z', 'x'), 0, 0)]
    pallas_call x9 -> x7, Pallas kernels: 28.9 us -> 22.6 us  [call(): pl.pallas_call(kernel, out_shape=[jax.ShapeDtypeStruct(s, d) for s, d in...]
    unnamed x69 -> x16, local copies, waits for them, and re-layouts: 4.96 us -> 2.38 us
    ppermute x4 -> x2, starting transfers between devices: 5.94 us -> 3.78 us  [swap(): return lax.ppermute(v, 'h', [(0, 1), (1, 0)])]
  transfers between devices with their start and end apart: 33 -> 6, of which waited for: 13 -> 4; matrix products, arithmetic and copies ran while one was open for 3% -> 1% of each run, Pallas kernels for 9% -> 8%
where the time goes in v2:
time: 102 us; the launch traced here: 101 us
  waiting for transfers between devices  33.2 us (33%)
  starting transfers between devices  28.1 us (28%)
  Pallas kernels  22.6 us (22%)
  blocking collectives  12.1 us (12%)
  local copies, waits for them, and re-layouts  4.57 us (4%)
    pallas_call x7, Pallas kernels, call(): pl.pallas_call(kernel, out_shape=[jax.ShapeDtypeStruct(s, d) for s, d in...  22.6 us
    all_to_all x2, waiting for transfers between devices, plane(): return lax.all_to_all(v, ('z', 'x'), 0, 0)  22.5 us
    all_to_all x2, starting transfers between devices, plane(): return lax.all_to_all(v, ('z', 'x'), 0, 0)  12.3 us
    all_to_all x1, blocking collectives, plane(): return lax.all_to_all(v, ('z', 'x'), 0, 0)  12.1 us
    all_to_all x2, starting transfers between devices, octet(): return lax.all_to_all(v, ('l', 'c', 'h'), 0, 0)  12 us
    all_to_all x2, waiting for transfers between devices, octet(): return lax.all_to_all(v, ('l', 'c', 'h'), 0, 0)  10.6 us
    ppermute x2, starting transfers between devices, swap(): return lax.ppermute(v, 'h', [(0, 1), (1, 0)])  3.78 us
    unnamed x16, local copies, waits for them, and re-layouts  2.38 us
  transfers between devices with their start and end apart: 6, of which 4 were waited for; matrix products, arithmetic and copies ran while one was open for 1% of the time, Pallas kernels for 8%

profile of v2, /device:TPU:1, one launch (start us, length us, event | category | flops | bytes accessed | tf_op | source)
XLA Modules:
  0.0 101.3 jit_solution(8597737833211346196)
XLA Ops:
  0.6 2.7 %strips.1 = (bf16[16,144,128]{2,1,0:T(8,128)(2,1)}, bf16[32,6144]{1,0:T(8,128)(2,1)}) custom-call(s32[3,2,4]{2,1,0:T(2,128)} %bitcast.16, bf16[2,32,4096]{2,1,0:T(8,128)(2,1)} %inp.3, bf16[2,64,1024]{2,1,0:T(8,128)(2,1)} %cot.3, bf16[4096,128]{1,0:T(8,128)(2,1)} %constant.26.clone.pick, bf16[256,128]{1,0:T(8,128)(2,1)} %constant.27.clone.ends), custom_call_target="tpu_custom_call" | custom-call | tf_op jit(solution)/shard_map/strips/pallas_call | solution.py:380
  3.3 0.0 copy-start.6
  3.3 8.5 %all-to-all-start = ((bf16[16,144,128]{2,1,0:T(8,128)(2,1)}), bf16[16,144,128]{2,1,0:T(8,128)(2,1)S(1)}, u32[]{:S(2)}, u32[]{:S(2)}) async-start(bf16[16,144,128]{2,1,0:T(8,128)(2,1)} %get-tuple-element.18), calls=%async_computation | async-start | bytes 1179648 | tf_op jit(solution)/shard_map/all_to_all | solution.py:397
  11.9 0.0 copy-done.6
  11.9 3.0 %collective-permute-start = (bf16[32,6144]{1,0:T(8,128)(2,1)S(1)}, bf16[32,6144]{1,0:T(8,128)(2,1)S(1)}, u32[]{:S(2)}, u32[]{:S(2)}) collective-permute-start(bf16[32,6144]{1,0:T(8,128)(2,1)S(1)} %copy-done.6), channel_id=1, source_target_pairs={{0,1},{1,0},{2,3},{3,2},{4,5},{5,4},{6,7},{7,6},{8,9},{9,8},{10,11... | collective-permute-start | bytes 1179656 | tf_op jit(solution)/shard_map/ppermute | solution.py:393
  14.9 8.1 %all-to-all-done.got = bf16[16,144,128]{2,1,0:T(8,128)(2,1)S(1)} async-done(((bf16[16,144,128]{2,1,0:T(8,128)(2,1)}), bf16[16,144,128]{2,1,0:T(8,128)(2,1)S(1)}, u32[]{:S(2)}, u32[]{:S(2)}) %all-to-all-start) | async-done | bytes 589856 | tf_op jit(solution)/shard_map/all_to_all | solution.py:397
  23.0 0.0 copy-start.1
  23.0 0.1 fusion.1
  23.1 0.7 reshape.29.codes
  23.8 0.0 copy-done.1
  23.9 3.0 %route_strips.1 = bf16[8,64,128]{2,1,0:T(8,128)(2,1)} custom-call(s32[128]{0:T(128)} %reshape.29.codes, bf16[16,144,128]{2,1,0:T(8,128)(2,1)} %copy-done.1), custom_call_target="tpu_custom_call" | custom-call | tf_op jit(solution)/shard_map/route_strips/pallas_call | solution.py:380
  26.9 6.8 %all-to-all-start.1 = ((bf16[8,64,128]{2,1,0:T(8,128)(2,1)}), bf16[8,64,128]{2,1,0:T(8,128)(2,1)S(1)}, u32[]{:S(2)}, u32[]{:S(2)}) async-start(bf16[8,64,128]{2,1,0:T(8,128)(2,1)} %route_strips.1), calls=%async_computation.1 | async-start | bytes 262144 | tf_op jit(solution)/shard_map/all_to_all | solution.py:401
  33.7 2.2 %weights.1 = (bf16[256,1024]{1,0:T(8,128)(2,1)}, bf16[1024,256]{1,0:T(8,128)(2,1)}, bf16[128,256]{1,0:T(8,128)(2,1)}, bf16[256,128]{1,0:T(8,128)(2,1)}) custom-call(bf16[3,3,64,64]{3,2,1,0:T(8,128)(2,1)} %bitcast.12, bf16[256,128]{1,0:T(8,128)(2,1)} %bitcast.13), custom_call_target="tpu_custom_call" | custom-call | tf_op jit(solution)/shard_map/weights/pallas_call | solution.py:380
  35.9 0.0 collective-permute-done.rcv
  35.9 0.0 copy-start.4
  35.9 3.0 %all-to-all-done.1.halo = bf16[8,64,128]{2,1,0:T(8,128)(2,1)S(1)} async-done(((bf16[8,64,128]{2,1,0:T(8,128)(2,1)}), bf16[8,64,128]{2,1,0:T(8,128)(2,1)S(1)}, u32[]{:S(2)}, u32[]{:S(2)}) %all-to-all-start.1) | async-done | bytes 131104 | tf_op jit(solution)/shard_map/all_to_all | solution.py:401
  38.9 0.0 copy-start.3
  38.9 0.0 copy-done.4
  38.9 0.7 copy-done.3
  39.6 7.0 %main.1 = (bf16[32,6144]{1,0:T(8,128)(2,1)}, bf16[32,6144]{1,0:T(8,128)(2,1)}, bf16[16,224,128]{2,1,0:T(8,128)(2,1)}) custom-call(s32[3,2,4]{2,1,0:T(2,128)} %bitcast.17, bf16[2,32,4096]{2,1,0:T(8,128)(2,1)} %inp.3, bf16[32,6144]{1,0:T(8,128)(2,1)} %copy-done.4, bf16[2,64,1024]{2,1,0:T(8,128)(2,1)} %cot.3, bf16[8,64,128]{2,1,0:T(8,128)(2,1)} %copy-done.3, ...), custom_call_target="tpu_custom_call" | custom-call | tf_op jit(solution)/shard_map/main/pallas_call | solution.py:380
  46.6 0.0 copy-start.7
  46.6 3.8 %all-to-all-start.2 = ((bf16[16,224,128]{2,1,0:T(8,128)(2,1)}), bf16[16,224,128]{2,1,0:T(8,128)(2,1)S(1)}, u32[]{:S(2)}, u32[]{:S(2)}) async-start(bf16[16,224,128]{2,1,0:T(8,128)(2,1)} %get-tuple-element.24), calls=%async_computation.2 | async-start | bytes 1835008 | tf_op jit(solution)/shard_map/all_to_all | solution.py:397
  50.4 0.0 copy-done.7
  50.4 0.8 collective-permute-start.1
  51.2 14.4 %all-to-all-done.2.got = bf16[16,224,128]{2,1,0:T(8,128)(2,1)S(1)} async-done(((bf16[16,224,128]{2,1,0:T(8,128)(2,1)}), bf16[16,224,128]{2,1,0:T(8,128)(2,1)S(1)}, u32[]{:S(2)}, u32[]{:S(2)}) %all-to-all-start.2) | async-done | bytes 917536 | tf_op jit(solution)/shard_map/all_to_all | solution.py:397
  65.6 0.0 copy-start
  65.6 0.9 copy-done
  66.5 2.7 %route_rims.1 = bf16[8,176,128]{2,1,0:T(8,128)(2,1)} custom-call(s32[128]{0:T(128)} %reshape.29.codes, bf16[16,224,128]{2,1,0:T(8,128)(2,1)} %copy-done), custom_call_target="tpu_custom_call" | custom-call | tf_op jit(solution)/shard_map/route_rims/pallas_call | solution.py:380
  69.3 5.2 %all-to-all-start.3 = ((bf16[8,176,128]{2,1,0:T(8,128)(2,1)}), bf16[8,176,128]{2,1,0:T(8,128)(2,1)S(1)}, u32[]{:S(2)}, u32[]{:S(2)}) async-start(bf16[8,176,128]{2,1,0:T(8,128)(2,1)} %route_rims.1), calls=%async_computation.3 | async-start | bytes 720896 | tf_op jit(solution)/shard_map/all_to_all | solution.py:401
  74.4 0.0 collective-permute-done.1.rcv
  74.4 0.0 copy-start.5
  74.4 7.6 %all-to-all-done.3.ret = bf16[8,176,128]{2,1,0:T(8,128)(2,1)S(1)} async-done(((bf16[8,176,128]{2,1,0:T(8,128)(2,1)}), bf16[8,176,128]{2,1,0:T(8,128)(2,1)S(1)}, u32[]{:S(2)}, u32[]{:S(2)}) %all-to-all-start.3) | async-done | bytes 360480 | tf_op jit(solution)/shard_map/all_to_all | solution.py:401
  82.0 0.0 copy-start.2
  82.0 0.0 copy-done.5
  82.1 0.7 copy-done.2
  82.8 3.2 %final.1 = (bf16[2,32,4096]{2,1,0:T(8,128)(2,1)}, bf16[2,64,1024]{2,1,0:T(8,128)(2,1)}, f32[16,24,128]{2,1,0:T(8,128)}) custom-call(s32[3,2,4]{2,1,0:T(2,128)} %bitcast.18, bf16[8,176,128]{2,1,0:T(8,128)(2,1)} %copy-done.2, bf16[32,6144]{1,0:T(8,128)(2,1)} %get-tuple-element.25.keep, bf16[32,6144]{1,0:T(8,128)(2,1)} %copy-done.5, ...), custom_call_target="tpu_custom_call" | custom-call | tf_op jit(solution)/shard_map/final/pallas_call | solution.py:380
  86.0 12.1 %all_to_all.25.ws = f32[16,24,128]{2,1,0:T(8,128)} all-to-all(f32[16,24,128]{2,1,0:T(8,128)} %get-tuple-element.29), channel_id=1, replica_groups=mesh['z'=4,'x'=4,'l'=2,'c'=2,'h'=2] {'z','x'}, dimensions={0} | all-to-all | bytes 393216 | tf_op jit(solution)/shard_map/all_to_all | solution.py:397
  98.1 1.7 %unpack.1 = (f32[9,32,64]{2,1,0:T(8,128)}, f32[4,32,128]{2,1,0:T(8,128)}) custom-call(f32[16,24,128]{2,1,0:T(8,128)} %all_to_all.25.ws), custom_call_target="tpu_custom_call" | custom-call | tf_op jit(solution)/shard_map/unpack/pallas_call | solution.py:380
  99.8 1.5 %copy.17 = f32[2,2,32,128]{3,1,0,2:T(2,128)} copy(f32[2,2,32,128]{3,2,1,0:T(8,128)} %bitcast.15) | data formatting | bytes 131072 | tf_op jit(solution)/shard_map/reshape | solution.py:473
Async XLA Ops:
  3.3 8.6 %copy-start.6 = (bf16[32,6144]{1,0:T(8,128)(2,1)S(1)}, bf16[32,6144]{1,0:T(8,128)(2,1)}, u32[]{:S(2)}) copy-start(bf16[32,6144]{1,0:T(8,128)(2,1)} %get-tuple-element.19) | copy-start | bytes 1179652
  3.3 19.7 %all-to-all-start = ((bf16[16,144,128]{2,1,0:T(8,128)(2,1)}), bf16[16,144,128]{2,1,0:T(8,128)(2,1)S(1)}, u32[]{:S(2)}, u32[]{:S(2)}) async-start(bf16[16,144,128]{2,1,0:T(8,128)(2,1)} %get-tuple-element.18), calls=%async_computation | async-start | bytes 1179648 | tf_op jit(solution)/shard_map/all_to_all | solution.py:397
  11.9 24.0 %collective-permute-start = (bf16[32,6144]{1,0:T(8,128)(2,1)S(1)}, bf16[32,6144]{1,0:T(8,128)(2,1)S(1)}, u32[]{:S(2)}, u32[]{:S(2)}) collective-permute-start(bf16[32,6144]{1,0:T(8,128)(2,1)S(1)} %copy-done.6), channel_id=1, source_target_pairs={{0,1},{1,0},{2,3},{3,2},{4,5},{5,4},{6,7},{7,6},{8,9},{9,8},{10,11... | collective-permute-start | bytes 1179656 | tf_op jit(solution)/shard_map/ppermute | solution.py:393
  23.0 0.8 copy-start.1
  26.9 12.1 %all-to-all-start.1 = ((bf16[8,64,128]{2,1,0:T(8,128)(2,1)}), bf16[8,64,128]{2,1,0:T(8,128)(2,1)S(1)}, u32[]{:S(2)}, u32[]{:S(2)}) async-start(bf16[8,64,128]{2,1,0:T(8,128)(2,1)} %route_strips.1), calls=%async_computation.1 | async-start | bytes 262144 | tf_op jit(solution)/shard_map/all_to_all | solution.py:401
  35.9 3.0 %copy-start.4 = (bf16[32,6144]{1,0:T(8,128)(2,1)}, bf16[32,6144]{1,0:T(8,128)(2,1)S(1)}, u32[]{:S(2)}) copy-start(bf16[32,6144]{1,0:T(8,128)(2,1)S(1)} %collective-permute-done.rcv) | copy-start | bytes 1179652
  38.9 0.7 copy-start.3
  46.6 3.8 %copy-start.7 = (bf16[32,6144]{1,0:T(8,128)(2,1)S(1)}, bf16[32,6144]{1,0:T(8,128)(2,1)}, u32[]{:S(2)}) copy-start(bf16[32,6144]{1,0:T(8,128)(2,1)} %get-tuple-element.26) | copy-start | bytes 1179652
  46.6 19.0 %all-to-all-start.2 = ((bf16[16,224,128]{2,1,0:T(8,128)(2,1)}), bf16[16,224,128]{2,1,0:T(8,128)(2,1)S(1)}, u32[]{:S(2)}, u32[]{:S(2)}) async-start(bf16[16,224,128]{2,1,0:T(8,128)(2,1)} %get-tuple-element.24), calls=%async_computation.2 | async-start | bytes 1835008 | tf_op jit(solution)/shard_map/all_to_all | solution.py:397
  50.4 24.1 %collective-permute-start.1 = (bf16[32,6144]{1,0:T(8,128)(2,1)S(1)}, bf16[32,6144]{1,0:T(8,128)(2,1)S(1)}, u32[]{:S(2)}, u32[]{:S(2)}) collective-permute-start(bf16[32,6144]{1,0:T(8,128)(2,1)S(1)} %copy-done.7), channel_id=1, source_target_pairs={{0,1},{1,0},{2,3},{3,2},{4,5},{5,4},{6,7},{7,6},{8,9},{9,8},{10,11... | collective-permute-start | bytes 1179656 | tf_op jit(solution)/shard_map/ppermute | solution.py:393
  65.6 0.9 copy-start
  69.3 12.8 %all-to-all-start.3 = ((bf16[8,176,128]{2,1,0:T(8,128)(2,1)}), bf16[8,176,128]{2,1,0:T(8,128)(2,1)S(1)}, u32[]{:S(2)}, u32[]{:S(2)}) async-start(bf16[8,176,128]{2,1,0:T(8,128)(2,1)} %route_rims.1), calls=%async_computation.3 | async-start | bytes 720896 | tf_op jit(solution)/shard_map/all_to_all | solution.py:401
  74.4 7.6 %copy-start.5 = (bf16[32,6144]{1,0:T(8,128)(2,1)}, bf16[32,6144]{1,0:T(8,128)(2,1)S(1)}, u32[]{:S(2)}) copy-start(bf16[32,6144]{1,0:T(8,128)(2,1)S(1)} %collective-permute-done.1.rcv) | copy-start | bytes 1179652
  82.0 0.7 copy-start.2

commit v3 on v2

--- a/solution.py
+++ b/solution.py
@@ -52,15 +52,10 @@
     return pl.multiple_of(v, m)
 
 
-def split(v):
-    hi = v.astype(BF)
-    return hi, (v - hi.astype(F32)).astype(BF)
-
-
 def strips_kernel(glue, inp, cot, pick, ends, out, send):
-    both = inp[...].reshape(64, 4096)
-    lr = dot(both, pick[...]).astype(BF)
-    tb = dot(jnp.concatenate([both[:, :128], both[:, 3968:]], axis=1), ends[...]).astype(BF)
+    pix = inp[...].reshape(64, 4096)
+    lr = dot(pix, pick[...]).astype(BF)
+    tb = dot(jnp.concatenate([pix[:, :128], pix[:, 3968:]], axis=1), ends[...]).astype(BF)
     lane = lax.broadcasted_iota(jnp.int32, (16, 128), 1)
     codes = jnp.zeros((16, 128), jnp.int32)
     for tile in range(2):
@@ -133,7 +128,7 @@
 
 def main_kernel(
     glue, inp, rcv, cot, halo, wb, wbt, lw, lwt, perm, edge, rev,
-    keep, send, pay,
+    keep, send, pay, c0, c1, c2, c3, c4, c5, c6, c7,
     xs, pt, ct, pre_s, gh_s, hd, gp, wh, gs, lv_s,
 ):
     h = lax.axis_index("h")
@@ -256,18 +251,16 @@
         else:
             packed[-1] = jnp.where(l1 < 64, packed[-1], v + pltpu.roll(u, 64, 1))
     for hh in range(2):
-        base = hh * 384
+        base = hh * 288
         for q in range(5):
             wh[base + q * 32 : base + q * 32 + 32, :] = packed[q][hh * 32 : hh * 32 + 32]
         for ab in range(4):
             row = base + 160 + ab * 32
             wh[row : row + 32, :] = dl[ab * 64 + hh * 32 : ab * 64 + hh * 32 + 32]
-        wh[base + 288 : base + 384, :] = jnp.zeros((96, 128), F32)
-    for d in range(16):
-        chunk = jnp.concatenate([wh[d * 24 : d * 24 + 24, :], wh[384 + d * 24 : 408 + d * 24, :]], axis=0)
-        hi, lo = split(chunk)
-        pay[d, 128:176, :] = hi
-        pay[d, 176:224, :] = lo
+    lch = lax.axis_index("l") * 4 + lax.axis_index("c") * 2 + h
+    for k, ref in enumerate((c0, c1, c2, c3, c4, c5, c6, c7)):
+        d = lch ^ k
+        ref[...] = wh[pl.ds(al((d & 1) * 288 + (d >> 1) * 72, 8), 72), :]
     lv_s[...] = dot(lw[...], hd[...]).astype(BF)
     for b in range(2):
         gs[:, b * 1024 : b * 1024 + 1024] = (qs[1][b] + down(qs[3][b])).astype(BF)
@@ -297,30 +290,15 @@
                     dst = ((t & 6) | hh) * 128 + (t & 1) * 64 + (s >> 1) * 32
                     place(acc, al(dst, 32), v, (r ^ s) & 1, s, half)
 
-    w = None
-    for i in range(16):
-        v = got[i, 128:176, :].astype(F32) + got[i, 176:224, :].astype(F32)
-        w = v if w is None else w + v
-    pieces = []
-    for q in range(2):
-        hi, lo = split(w[q * 24 : q * 24 + 24])
-        pieces.append(jnp.concatenate([hi.astype(F32), lo.astype(F32)], axis=0).astype(BF))
     for k in range(8):
-        out[k, 0:128, :] = acc[k * 128 : k * 128 + 128, :].astype(BF)
-        out[k, 128:176, :] = pieces[k & 1]
-
-
-def final_kernel(glue, ret, keep, rcv, perm, edge, rev, gin, lev, wout, gs, xs):
+        out[k] = acc[k * 128 : k * 128 + 128, :].astype(BF)
+
+
+def final_kernel(glue, ret, keep, rcv, perm, edge, rev, gin, lev, gs, xs):
     h = lax.axis_index("h")
-    acc = w = None
-    for k in range(8):
-        v = ret[k, 0:128, :].astype(F32)
-        p = ret[k, 128:176, :].astype(F32)
-        p = p[0:24] + p[24:48]
-        acc = v if acc is None else acc + v
-        w = p if w is None else w + p
-    for d in range(16):
-        wout[d] = w
+    acc = ret[0].astype(F32)
+    for k in range(1, 8):
+        acc = acc + ret[k].astype(F32)
     lane = lax.broadcasted_iota(jnp.int32, (128, 128), 1)
     row = lax.broadcasted_iota(jnp.int32, (128, 128), 0)
     flag = jnp.zeros((128, 128), jnp.int32)
@@ -360,15 +338,17 @@
         lev[tile, 32:] = src[:, 5120:]
 
 
-def unpack_kernel(ws, gc, gl):
-    w = ws[...].reshape(384, 128)
+def unpack_kernel(w0, w1, w2, w3, gc, gl, w):
+    q = lax.axis_index("l") * 2 + lax.axis_index("c")
+    for k, ref in enumerate((w0, w1, w2, w3)):
+        w[pl.ds(al((q ^ k) * 72, 8), 72), :] = ref[...]
     for ij in range(9):
         v = w[(ij // 2) * 32 : (ij // 2) * 32 + 32, :]
         if ij % 2:
             v = pltpu.roll(v, 64, 1)
         gc[ij] = v[:, :64]
     for ab in range(4):
-        gl[ab] = w[160 + ab * 32 : 192 + ab * 32, :]
+        gl[:, ab // 2, ab % 2, :] = w[160 + ab * 32 : 192 + ab * 32, :]
 
 
 def call(kernel, outs, args, smem, scratch=(), name=None):
@@ -393,6 +373,20 @@
     return lax.ppermute(v, "h", [(0, 1), (1, 0)])
 
 
+def hop(v, axes, n, k):
+    return lax.ppermute(v, axes, [(i, i ^ k) for i in range(n)]) if k else v
+
+
+def ring(v, axis, k):
+    return lax.ppermute(v, axis, [(i, (i + k) % 4) for i in range(4)]) if k else v
+
+
+def total(parts):
+    while len(parts) > 1:
+        parts = [a + b for a, b in zip(parts[::2], parts[1::2])]
+    return parts[0]
+
+
 def plane(v):
     return lax.all_to_all(v, ("z", "x"), 0, 0)
 
@@ -433,44 +427,53 @@
         0,
         name="weights",
     )
-    keep, back, pay = call(
+    keep, back, pay, *chunks = call(
         main_kernel,
-        [((32, 6144), BF), ((32, 6144), BF), ((16, 224, 128), BF)],
+        [((32, 6144), BF), ((32, 6144), BF), ((16, 128, 128), BF)]
+        + [((72, 128), F32)] * 8,
         (glue, inputs, rcv, cotangent, halos, wb, wbt, lw, lwt, perm, edge, rev),
         1,
         [
             pltpu.VMEM((512, 512), BF), pltpu.VMEM((1024, 1024), BF), pltpu.VMEM((128, 1024), BF),
             pltpu.VMEM((256, 1024), F32), pltpu.VMEM((256, 1024), F32), pltpu.VMEM((256, 1024), BF),
-            pltpu.VMEM((256, 1024), BF), pltpu.VMEM((768, 128), F32), pltpu.VMEM((64, 4096), BF),
+            pltpu.VMEM((256, 1024), BF), pltpu.VMEM((576, 128), F32), pltpu.VMEM((64, 4096), BF),
             pltpu.VMEM((128, 1024), BF),
         ],
         name="main",
     )
+    rims = plane(pay)
     rback = swap(back)
-    rims = plane(pay)
+    w = total([hop(chunks[k], ("l", "c", "h"), 8, k) for k in range(8)])
+    w = total([ring(w, "z", k) for k in range(4)])
+    w = total([ring(w, "x", k) for k in range(4)])
+    parts = [hop(w, ("l", "c"), 4, k) for k in range(4)]
     outgoing = call(
         route_rims_kernel,
-        ((8, 176, 128), BF),
+        ((8, 128, 128), BF),
         (codes, rims),
         1,
         [pltpu.VMEM((1024, 128), F32)],
         name="route_rims",
     )
     ret = octet(outgoing)
-    gin, lev, wrep = call(
+    gin, lev = call(
         final_kernel,
-        [((2, 32, 4096), BF), ((2, 64, 1024), BF), ((16, 24, 128), F32)],
+        [((2, 32, 4096), BF), ((2, 64, 1024), BF)],
         (glue, ret, keep, rback, perm, edge, rev),
         1,
         [pltpu.VMEM((64, 4096), BF), pltpu.VMEM((512, 512), BF)],
         name="final",
     )
-    wall = plane(wrep)
     gc, gl = call(
-        unpack_kernel, [((9, 32, 64), F32), ((4, 32, 128), F32)], (wall,), 0, name="unpack"
+        unpack_kernel,
+        [((9, 32, 64), F32), ((32, 2, 2, 128), F32)],
+        tuple(parts),
+        0,
+        [pltpu.VMEM((288, 128), F32)],
+        name="unpack",
     )
     grad_conv = jnp.transpose(gc.reshape(3, 3, 32, 64), (3, 2, 0, 1))
-    grad_level = jnp.transpose(gl.reshape(2, 2, 32, 128), (3, 2, 0, 1))
+    grad_level = jnp.transpose(gl, (3, 0, 1, 2))
     return lev, gin, grad_conv, grad_level
 
 

time: 102 us -> 94.8 us (0.929)
  starting transfers between devices: 28.1 us -> 44.3 us
  blocking collectives: 12.1 us -> 0 us
  waiting for transfers between devices: 33.2 us -> 22.2 us
    ppermute x0 -> x16, starting transfers between devices: none -> 16.5 us  [the longest x10 9.77 us: hop(): return lax.ppermute(v, axes, [(i, i ^ k) for i in range(n)]) if k else v]
    all_to_all x2, waiting for transfers between devices: 22.5 us -> 8.13 us  [plane(): return lax.all_to_all(v, ('z', 'x'), 0, 0)]
    all_to_all x1 -> x0, blocking collectives: 12.1 us -> none  [plane(): return lax.all_to_all(v, ('z', 'x'), 0, 0)]
    ppermute x0 -> x16, waiting for transfers between devices: none -> 11 us  [the longest x6 6.58 us: ring(): lax.ppermute(v, axis, [(i, (i + k) % 4) for i in range(4)])]
    all_to_all x2, waiting for transfers between devices: 10.6 us -> 3.05 us  [octet(): return lax.all_to_all(v, ('l', 'c', 'h'), 0, 0)]
    reshape x1 -> x0, local copies, waits for them, and re-layouts: 1.52 us -> none  [on_device(): grad_level = jnp.transpose(gl.reshape(2, 2, 32, 128), (3, 2, 0, 1))]
    unnamed x16 -> x26, local copies, waits for them, and re-layouts: 2.38 us -> 3.57 us
  transfers between devices with their start and end apart: 6 -> 22, of which waited for: 4 -> 6; matrix products, arithmetic and copies ran while one was open for 1% -> 1% of each run, Pallas kernels for 8% -> 10%
where the time goes in v3:
time: 94.8 us; the launch traced here: 93.9 us
  starting transfers between devices  44.3 us (47%)
  Pallas kernels  22.3 us (24%)
  waiting for transfers between devices  22.2 us (23%)
  local copies, waits for them, and re-layouts  4.22 us (4%)
    pallas_call x7, Pallas kernels, call(): pl.pallas_call(kernel, out_shape=[jax.ShapeDtypeStruct(s, d) for s, d in...  22.3 us
    all_to_all x2, starting transfers between devices, plane(): return lax.all_to_all(v, ('z', 'x'), 0, 0)  12.3 us
    all_to_all x2, starting transfers between devices, octet(): return lax.all_to_all(v, ('l', 'c', 'h'), 0, 0)  11.4 us
    ppermute x10, starting transfers between devices, hop(): return lax.ppermute(v, axes, [(i, i ^ k) for i in range(n)]) if k else v  9.77 us
    all_to_all x2, waiting for transfers between devices, plane(): return lax.all_to_all(v, ('z', 'x'), 0, 0)  8.13 us
    ppermute x6, starting transfers between devices, ring(): lax.ppermute(v, axis, [(i, (i + k) % 4) for i in range(4)])  6.72 us
    ppermute x6, waiting for transfers between devices, ring(): lax.ppermute(v, axis, [(i, (i + k) % 4) for i in range(4)])  6.58 us
    ppermute x10, waiting for transfers between devices, hop(): return lax.ppermute(v, axes, [(i, i ^ k) for i in range(n)]) if k else v  4.38 us
  transfers between devices with their start and end apart: 22, of which 6 were waited for; matrix products, arithmetic and copies ran while one was open for 1% of the time, Pallas kernels for 10%

profile of v3, /device:TPU:1, one launch (start us, length us, event | category | flops | bytes accessed | tf_op | source)
XLA Modules:
  0.0 93.9 jit_solution(7139546405066015117)
XLA Ops:
  0.6 2.7 %strips.1 = (bf16[16,144,128]{2,1,0:T(8,128)(2,1)}, bf16[32,6144]{1,0:T(8,128)(2,1)}) custom-call(s32[3,2,4]{2,1,0:T(2,128)} %bitcast.11, bf16[2,32,4096]{2,1,0:T(8,128)(2,1)} %inp.3, bf16[2,64,1024]{2,1,0:T(8,128)(2,1)} %cot.3, bf16[4096,128]{1,0:T(8,128)(2,1)} %constant.26.clone.pick, bf16[256,128]{1,0:T(8,128)(2,1)} %constant.27.clone.ends), custom_call_target="tpu_custom_call" | custom-call | tf_op jit(solution)/shard_map/strips/pallas_call | solution.py:360
  3.3 8.5 %all-to-all-start = ((bf16[16,144,128]{2,1,0:T(8,128)(2,1)}), bf16[16,144,128]{2,1,0:T(8,128)(2,1)S(1)}, u32[]{:S(2)}, u32[]{:S(2)}) async-start(bf16[16,144,128]{2,1,0:T(8,128)(2,1)} %get-tuple-element.25), calls=%async_computation | async-start | bytes 1179648 | tf_op jit(solution)/shard_map/all_to_all | solution.py:391
  11.9 3.0 %collective-permute-start = (bf16[32,6144]{1,0:T(8,128)(2,1)S(1)}, bf16[32,6144]{1,0:T(8,128)(2,1)S(1)}, u32[]{:S(2)}, u32[]{:S(2)}) collective-permute-start(bf16[32,6144]{1,0:T(8,128)(2,1)S(1)} %copy-done.12), channel_id=1, source_target_pairs={{0,1},{1,0},{2,3},{3,2},{4,5},{5,4},{6,7},{7,6},{8,9},{9,8},{10,11... | collective-permute-start | bytes 1179656 | tf_op jit(solution)/shard_map/ppermute | solution.py:373
  14.9 8.1 %all-to-all-done.got = bf16[16,144,128]{2,1,0:T(8,128)(2,1)S(1)} async-done(((bf16[16,144,128]{2,1,0:T(8,128)(2,1)}), bf16[16,144,128]{2,1,0:T(8,128)(2,1)S(1)}, u32[]{:S(2)}, u32[]{:S(2)}) %all-to-all-start) | async-done | bytes 589856 | tf_op jit(solution)/shard_map/all_to_all | solution.py:391
  23.0 0.1 fusion.1
  23.1 0.7 reshape.25.codes
  23.8 0.1 copy-done
  23.8 3.1 %route_strips.1 = bf16[8,64,128]{2,1,0:T(8,128)(2,1)} custom-call(s32[128]{0:T(128)} %reshape.25.codes, bf16[16,144,128]{2,1,0:T(8,128)(2,1)} %copy-done), custom_call_target="tpu_custom_call" | custom-call | tf_op jit(solution)/shard_map/route_strips/pallas_call | solution.py:360
  27.0 6.5 %all-to-all-start.1 = ((bf16[8,64,128]{2,1,0:T(8,128)(2,1)}), bf16[8,64,128]{2,1,0:T(8,128)(2,1)S(1)}, u32[]{:S(2)}, u32[]{:S(2)}) async-start(bf16[8,64,128]{2,1,0:T(8,128)(2,1)} %route_strips.1), calls=%async_computation.1 | async-start | bytes 262144 | tf_op jit(solution)/shard_map/all_to_all | solution.py:395
  33.4 2.2 %weights.1 = (bf16[256,1024]{1,0:T(8,128)(2,1)}, bf16[1024,256]{1,0:T(8,128)(2,1)}, bf16[128,256]{1,0:T(8,128)(2,1)}, bf16[256,128]{1,0:T(8,128)(2,1)}) custom-call(bf16[3,3,64,64]{3,2,1,0:T(8,128)(2,1)} %bitcast.9, bf16[256,128]{1,0:T(8,128)(2,1)} %bitcast.10), custom_call_target="tpu_custom_call" | custom-call | tf_op jit(solution)/shard_map/weights/pallas_call | solution.py:360
  35.6 0.0 collective-permute-done.rcv
  35.6 3.0 %all-to-all-done.1.halo = bf16[8,64,128]{2,1,0:T(8,128)(2,1)S(1)} async-done(((bf16[8,64,128]{2,1,0:T(8,128)(2,1)}), bf16[8,64,128]{2,1,0:T(8,128)(2,1)S(1)}, u32[]{:S(2)}, u32[]{:S(2)}) %all-to-all-start.1) | async-done | bytes 131104 | tf_op jit(solution)/shard_map/all_to_all | solution.py:395
  38.7 0.7 copy-done.3
  39.3 7.0 %main.1 = (bf16[32,6144]{1,0:T(8,128)(2,1)}, bf16[32,6144]{1,0:T(8,128)(2,1)}, bf16[16,128,128]{2,1,0:T(8,128)(2,1)}, f32[72,128]{1,0:T(8,128)}, f32[72,128]{1,0...) custom-call(s32[3,2,4]{2,1,0:T(2,128)} %bitcast.12, ...), custom_call_target="tpu_custom_call" | custom-call | tf_op jit(solution)/shard_map/main/pallas_call | solution.py:360
  46.4 0.8 collective-permute-start.2
  47.2 1.3 %collective-permute-start.3 = (f32[72,128]{1,0:T(8,128)}, f32[72,128]{1,0:T(8,128)S(1)}, u32[]{:S(2)}, u32[]{:S(2)}) collective-permute-start(f32[72,128]{1,0:T(8,128)} %get-tuple-element.38), channel_id=1, source_target_pairs={{0,2},{1,3},{2,0},{3,1},{4,6},{5,7},{6,4},{7,5},{8,10},{9,11},{10,... | collective-permute-start | bytes 110600 | tf_op jit(solution)/shard_map/ppermute | solution.py:377
  48.5 1.4 %collective-permute-start.4 = (f32[72,128]{1,0:T(8,128)}, f32[72,128]{1,0:T(8,128)S(1)}, u32[]{:S(2)}, u32[]{:S(2)}) collective-permute-start(f32[72,128]{1,0:T(8,128)} %get-tuple-element.39), channel_id=1, source_target_pairs={{0,3},{1,2},{2,1},{3,0},{4,7},{5,6},{6,5},{7,4},{8,11},{9,10},{10,... | collective-permute-start | bytes 110600 | tf_op jit(solution)/shard_map/ppermute | solution.py:377
  49.9 0.3 collective-permute-start.5
  50.2 1.4 %collective-permute-start.6 = (f32[72,128]{1,0:T(8,128)}, f32[72,128]{1,0:T(8,128)S(1)}, u32[]{:S(2)}, u32[]{:S(2)}) collective-permute-start(f32[72,128]{1,0:T(8,128)} %get-tuple-element.41), channel_id=1, source_target_pairs={{0,5},{1,4},{2,7},{3,6},{4,1},{5,0},{6,3},{7,2},{8,13},{9,12},{10,... | collective-permute-start | bytes 110600 | tf_op jit(solution)/shard_map/ppermute | solution.py:377
  51.6 0.0 collective-permute-done.2
  51.6 1.3 %collective-permute-start.7 = (f32[72,128]{1,0:T(8,128)}, f32[72,128]{1,0:T(8,128)S(1)}, u32[]{:S(2)}, u32[]{:S(2)}) collective-permute-start(f32[72,128]{1,0:T(8,128)} %get-tuple-element.42), channel_id=1, source_target_pairs={{0,6},{1,7},{2,4},{3,5},{4,2},{5,3},{6,0},{7,1},{8,14},{9,15},{10,... | collective-permute-start | bytes 110600 | tf_op jit(solution)/shard_map/ppermute | solution.py:377
  53.0 0.0 collective-permute-done.3
  53.0 0.9 %collective-permute-start.8 = (f32[72,128]{1,0:T(8,128)}, f32[72,128]{1,0:T(8,128)S(1)}, u32[]{:S(2)}, u32[]{:S(2)}) collective-permute-start(f32[72,128]{1,0:T(8,128)} %get-tuple-element.43), channel_id=1, source_target_pairs={{0,7},{1,6},{2,5},{3,4},{4,3},{5,2},{6,1},{7,0},{8,15},{9,14},{10,... | collective-permute-start | bytes 110600 | tf_op jit(solution)/shard_map/ppermute | solution.py:377
  53.9 3.7 %all-to-all-start.2 = ((bf16[16,128,128]{2,1,0:T(8,128)(2,1)}), bf16[16,128,128]{2,1,0:T(8,128)(2,1)S(1)}, u32[]{:S(2)}, u32[]{:S(2)}) async-start(bf16[16,128,128]{2,1,0:T(8,128)(2,1)} %get-tuple-element.31), calls=%async_computation.2 | async-start | bytes 1048576 | tf_op jit(solution)/shard_map/all_to_all | solution.py:391
  57.7 0.1 collective-permute-done.8
  57.8 2.5 %collective-permute-start.11 = (f32[72,128]{1,0:T(8,128)S(1)}, f32[72,128]{1,0:T(8,128)S(1)}, u32[]{:S(2)}, u32[]{:S(2)}) collective-permute-start(f32[72,128]{1,0:T(8,128)S(1)} %add_add_fusion.2), channel_id=1, source_target_pairs={{0,96},{32,0},{64,32},{96,64},{1,97},{33,1},{65,33},{97,65},{2,98}... | collective-permute-start | bytes 110600 | tf_op jit(solution)/shard_map/ppermute | solution.py:381
  60.3 0.5 collective-permute-start.10
  60.9 0.6 collective-permute-start.9
  61.5 1.2 %collective-permute-start.1 = (bf16[32,6144]{1,0:T(8,128)(2,1)S(1)}, bf16[32,6144]{1,0:T(8,128)(2,1)S(1)}, u32[]{:S(2)}, u32[]{:S(2)}) collective-permute-start(bf16[32,6144]{1,0:T(8,128)(2,1)S(1)} %copy-done.11), channel_id=1, source_target_pairs={{0,1},{1,0},{2,3},{3,2},{4,5},{5,4},{6,7},{7,6},{8,9},{9,8},{10,11... | collective-permute-start | bytes 1179656 | tf_op jit(solution)/shard_map/ppermute | solution.py:373
  62.7 5.7 %collective-permute-done.10 = f32[72,128]{1,0:T(8,128)S(1)} collective-permute-done((f32[72,128]{1,0:T(8,128)S(1)}, f32[72,128]{1,0:T(8,128)S(1)}, u32[]{:S(2)}, u32[]{:S(2)}) %collective-permute-start.10) | collective-permute-done | bytes 36896 | tf_op jit(solution)/shard_map/ppermute | solution.py:381
  68.5 0.8 collective-permute-done.9
  69.3 2.0 %collective-permute-start.14 = (f32[72,128]{1,0:T(8,128)S(1)}, f32[72,128]{1,0:T(8,128)S(1)}, u32[]{:S(2)}, u32[]{:S(2)}) collective-permute-start(f32[72,128]{1,0:T(8,128)S(1)} %add_add_fusion.1), channel_id=1, source_target_pairs={{0,24},{8,0},{16,8},{24,16},{1,25},{9,1},{17,9},{25,17},{2,26},{10... | collective-permute-start | bytes 110600 | tf_op jit(solution)/shard_map/ppermute | solution.py:381
  71.3 0.7 collective-permute-start.13
  72.0 0.4 collective-permute-start.12
  72.4 0.8 copy-done.1
  73.2 2.5 %route_rims.1 = bf16[8,128,128]{2,1,0:T(8,128)(2,1)} custom-call(s32[128]{0:T(128)} %reshape.25.codes, bf16[16,128,128]{2,1,0:T(8,128)(2,1)} %copy-done.1), custom_call_target="tpu_custom_call" | custom-call | tf_op jit(solution)/shard_map/route_rims/pallas_call | solution.py:360
  75.7 4.9 %all-to-all-start.3 = ((bf16[8,128,128]{2,1,0:T(8,128)(2,1)}), bf16[8,128,128]{2,1,0:T(8,128)(2,1)S(1)}, u32[]{:S(2)}, u32[]{:S(2)}) async-start(bf16[8,128,128]{2,1,0:T(8,128)(2,1)} %route_rims.1), calls=%async_computation.3 | async-start | bytes 524288 | tf_op jit(solution)/shard_map/all_to_all | solution.py:395
  80.6 0.0 copy-start.6
  80.7 1.7 %collective-permute-start.17 = (f32[72,128]{1,0:T(8,128)S(1)}, f32[72,128]{1,0:T(8,128)S(1)}, u32[]{:S(2)}, u32[]{:S(2)}) collective-permute-start(f32[72,128]{1,0:T(8,128)S(1)} %add_add_fusion.w0), channel_id=1, source_target_pairs={{0,6},{2,4},{4,2},{6,0},{1,7},{3,5},{5,3},{7,1},{8,14},{10,12},{12... | collective-permute-start | bytes 110600 | tf_op jit(solution)/shard_map/ppermute | solution.py:377
  82.4 0.5 collective-permute-start.15
  82.9 4.3 %collective-permute-done.17.w3 = f32[72,128]{1,0:T(8,128)S(1)} collective-permute-done((f32[72,128]{1,0:T(8,128)S(1)}, f32[72,128]{1,0:T(8,128)S(1)}, u32[]{:S(2)}, u32[]{:S(2)}) %collective-permute-start.17) | collective-permute-done | bytes 36896 | tf_op jit(solution)/shard_map/ppermute | solution.py:377
  87.2 0.6 copy-done.8
  87.7 0.0 copy-done.9
  87.8 0.6 copy-done.10
  88.4 1.6 %unpack.1 = (f32[9,32,64]{2,1,0:T(8,128)}, f32[32,2,2,128]{3,2,1,0:T(2,128)}) custom-call(f32[72,128]{1,0:T(8,128)} %copy-done.6, f32[72,128]{1,0:T(8,128)} %copy-done.10, f32[72,128]{1,0:T(8,128)} %copy-done.9, f32[72,128]{1,0:T(8,128)} %copy-done.8), custom_call_target="tpu_custom_call" | custom-call | tf_op jit(solution)/shard_map/unpack/pallas_call | solution.py:360
  90.0 0.7 copy-done.4
  90.7 0.1 copy-done.2
  90.8 3.1 %final.1 = (bf16[2,32,4096]{2,1,0:T(8,128)(2,1)}, bf16[2,64,1024]{2,1,0:T(8,128)(2,1)}) custom-call(s32[3,2,4]{2,1,0:T(2,128)} %bitcast.13, bf16[8,128,128]{2,1,0:T(8,128)(2,1)} %copy-done.2, bf16[32,6144]{1,0:T(8,128)(2,1)} %get-tuple-element.32.keep, bf16[32,6144]{1,0:T(8,128)(2,1)} %copy-done.4, bf16[512,512]{1,0:T(8,128)(2,1)} %constant.24.clone.perm, ...), custom_call_target="tpu_custom_call" | custom-call | tf_op jit(solution)/shard_map/final/pallas_call | solution.py:360
  (34 shorter events, 0.1 us)
Async XLA Ops:
  3.3 8.6 %copy-start.12 = (bf16[32,6144]{1,0:T(8,128)(2,1)S(1)}, bf16[32,6144]{1,0:T(8,128)(2,1)}, u32[]{:S(2)}) copy-start(bf16[32,6144]{1,0:T(8,128)(2,1)} %get-tuple-element.26) | copy-start | bytes 1179652
  3.3 19.7 %all-to-all-start = ((bf16[16,144,128]{2,1,0:T(8,128)(2,1)}), bf16[16,144,128]{2,1,0:T(8,128)(2,1)S(1)}, u32[]{:S(2)}, u32[]{:S(2)}) async-start(bf16[16,144,128]{2,1,0:T(8,128)(2,1)} %get-tuple-element.25), calls=%async_computation | async-start | bytes 1179648 | tf_op jit(solution)/shard_map/all_to_all | solution.py:391
  11.9 23.7 %collective-permute-start = (bf16[32,6144]{1,0:T(8,128)(2,1)S(1)}, bf16[32,6144]{1,0:T(8,128)(2,1)S(1)}, u32[]{:S(2)}, u32[]{:S(2)}) collective-permute-start(bf16[32,6144]{1,0:T(8,128)(2,1)S(1)} %copy-done.12), channel_id=1, source_target_pairs={{0,1},{1,0},{2,3},{3,2},{4,5},{5,4},{6,7},{7,6},{8,9},{9,8},{10,11... | collective-permute-start | bytes 1179656 | tf_op jit(solution)/shard_map/ppermute | solution.py:373
  23.0 0.8 copy-start
  27.0 11.7 %all-to-all-start.1 = ((bf16[8,64,128]{2,1,0:T(8,128)(2,1)}), bf16[8,64,128]{2,1,0:T(8,128)(2,1)S(1)}, u32[]{:S(2)}, u32[]{:S(2)}) async-start(bf16[8,64,128]{2,1,0:T(8,128)(2,1)} %route_strips.1), calls=%async_computation.1 | async-start | bytes 262144 | tf_op jit(solution)/shard_map/all_to_all | solution.py:395
  35.6 3.1 %copy-start.5 = (bf16[32,6144]{1,0:T(8,128)(2,1)}, bf16[32,6144]{1,0:T(8,128)(2,1)S(1)}, u32[]{:S(2)}) copy-start(bf16[32,6144]{1,0:T(8,128)(2,1)S(1)} %collective-permute-done.rcv) | copy-start | bytes 1179652
  38.7 0.7 copy-start.3
  46.4 5.3 %collective-permute-start.2 = (f32[72,128]{1,0:T(8,128)}, f32[72,128]{1,0:T(8,128)S(1)}, u32[]{:S(2)}, u32[]{:S(2)}) collective-permute-start(f32[72,128]{1,0:T(8,128)} %get-tuple-element.37), channel_id=1, source_target_pairs={{0,1},{1,0},{2,3},{3,2},{4,5},{5,4},{6,7},{7,6},{8,9},{9,8},{10,11... | collective-permute-start | bytes 110600 | tf_op jit(solution)/shard_map/ppermute | solution.py:377
  47.2 5.8 %collective-permute-start.3 = (f32[72,128]{1,0:T(8,128)}, f32[72,128]{1,0:T(8,128)S(1)}, u32[]{:S(2)}, u32[]{:S(2)}) collective-permute-start(f32[72,128]{1,0:T(8,128)} %get-tuple-element.38), channel_id=1, source_target_pairs={{0,2},{1,3},{2,0},{3,1},{4,6},{5,7},{6,4},{7,5},{8,10},{9,11},{10,... | collective-permute-start | bytes 110600 | tf_op jit(solution)/shard_map/ppermute | solution.py:377
  48.5 9.2 %collective-permute-start.4 = (f32[72,128]{1,0:T(8,128)}, f32[72,128]{1,0:T(8,128)S(1)}, u32[]{:S(2)}, u32[]{:S(2)}) collective-permute-start(f32[72,128]{1,0:T(8,128)} %get-tuple-element.39), channel_id=1, source_target_pairs={{0,3},{1,2},{2,1},{3,0},{4,7},{5,6},{6,5},{7,4},{8,11},{9,10},{10,... | collective-permute-start | bytes 110600 | tf_op jit(solution)/shard_map/ppermute | solution.py:377
  49.9 7.7 %collective-permute-start.5 = (f32[72,128]{1,0:T(8,128)}, f32[72,128]{1,0:T(8,128)S(1)}, u32[]{:S(2)}, u32[]{:S(2)}) collective-permute-start(f32[72,128]{1,0:T(8,128)} %get-tuple-element.40), channel_id=1, source_target_pairs={{0,4},{1,5},{2,6},{3,7},{4,0},{5,1},{6,2},{7,3},{8,12},{9,13},{10,... | collective-permute-start | bytes 110600 | tf_op jit(solution)/shard_map/ppermute | solution.py:377
  50.2 7.5 %collective-permute-start.6 = (f32[72,128]{1,0:T(8,128)}, f32[72,128]{1,0:T(8,128)S(1)}, u32[]{:S(2)}, u32[]{:S(2)}) collective-permute-start(f32[72,128]{1,0:T(8,128)} %get-tuple-element.41), channel_id=1, source_target_pairs={{0,5},{1,4},{2,7},{3,6},{4,1},{5,0},{6,3},{7,2},{8,13},{9,12},{10,... | collective-permute-start | bytes 110600 | tf_op jit(solution)/shard_map/ppermute | solution.py:377
  51.6 6.0 %collective-permute-start.7 = (f32[72,128]{1,0:T(8,128)}, f32[72,128]{1,0:T(8,128)S(1)}, u32[]{:S(2)}, u32[]{:S(2)}) collective-permute-start(f32[72,128]{1,0:T(8,128)} %get-tuple-element.42), channel_id=1, source_target_pairs={{0,6},{1,7},{2,4},{3,5},{4,2},{5,3},{6,0},{7,1},{8,14},{9,15},{10,... | collective-permute-start | bytes 110600 | tf_op jit(solution)/shard_map/ppermute | solution.py:377
  53.0 4.8 %collective-permute-start.8 = (f32[72,128]{1,0:T(8,128)}, f32[72,128]{1,0:T(8,128)S(1)}, u32[]{:S(2)}, u32[]{:S(2)}) collective-permute-start(f32[72,128]{1,0:T(8,128)} %get-tuple-element.43), channel_id=1, source_target_pairs={{0,7},{1,6},{2,5},{3,4},{4,3},{5,2},{6,1},{7,0},{8,15},{9,14},{10,... | collective-permute-start | bytes 110600 | tf_op jit(solution)/shard_map/ppermute | solution.py:377
  53.9 3.9 %copy-start.7 = (f32[72,128]{1,0:T(8,128)S(1)}, f32[72,128]{1,0:T(8,128)}, u32[]{:S(2)}) copy-start(f32[72,128]{1,0:T(8,128)} %get-tuple-element.36) | copy-start | bytes 110596
  53.9 7.5 %copy-start.11 = (bf16[32,6144]{1,0:T(8,128)(2,1)S(1)}, bf16[32,6144]{1,0:T(8,128)(2,1)}, u32[]{:S(2)}) copy-start(bf16[32,6144]{1,0:T(8,128)(2,1)} %get-tuple-element.33) | copy-start | bytes 1179652
  53.9 18.4 %all-to-all-start.2 = ((bf16[16,128,128]{2,1,0:T(8,128)(2,1)}), bf16[16,128,128]{2,1,0:T(8,128)(2,1)S(1)}, u32[]{:S(2)}, u32[]{:S(2)}) async-start(bf16[16,128,128]{2,1,0:T(8,128)(2,1)} %get-tuple-element.31), calls=%async_computation.2 | async-start | bytes 1048576 | tf_op jit(solution)/shard_map/all_to_all | solution.py:391
  57.8 4.9 %collective-permute-start.11 = (f32[72,128]{1,0:T(8,128)S(1)}, f32[72,128]{1,0:T(8,128)S(1)}, u32[]{:S(2)}, u32[]{:S(2)}) collective-permute-start(f32[72,128]{1,0:T(8,128)S(1)} %add_add_fusion.2), channel_id=1, source_target_pairs={{0,96},{32,0},{64,32},{96,64},{1,97},{33,1},{65,33},{97,65},{2,98}... | collective-permute-start | bytes 110600 | tf_op jit(solution)/shard_map/ppermute | solution.py:381
  60.3 8.1 %collective-permute-start.10 = (f32[72,128]{1,0:T(8,128)S(1)}, f32[72,128]{1,0:T(8,128)S(1)}, u32[]{:S(2)}, u32[]{:S(2)}) collective-permute-start(f32[72,128]{1,0:T(8,128)S(1)} %add_add_fusion.2), channel_id=1, source_target_pairs={{0,64},{32,96},{64,0},{96,32},{1,65},{33,97},{65,1},{97,33},{2,66}... | collective-permute-start | bytes 110600 | tf_op jit(solution)/shard_map/ppermute | solution.py:381
  60.9 8.4 %collective-permute-start.9 = (f32[72,128]{1,0:T(8,128)S(1)}, f32[72,128]{1,0:T(8,128)S(1)}, u32[]{:S(2)}, u32[]{:S(2)}) collective-permute-start(f32[72,128]{1,0:T(8,128)S(1)} %add_add_fusion.2), channel_id=1, source_target_pairs={{0,32},{32,64},{64,96},{96,0},{1,33},{33,65},{65,97},{97,1},{2,34}... | collective-permute-start | bytes 110600 | tf_op jit(solution)/shard_map/ppermute | solution.py:381
  61.5 28.5 %collective-permute-start.1 = (bf16[32,6144]{1,0:T(8,128)(2,1)S(1)}, bf16[32,6144]{1,0:T(8,128)(2,1)S(1)}, u32[]{:S(2)}, u32[]{:S(2)}) collective-permute-start(bf16[32,6144]{1,0:T(8,128)(2,1)S(1)} %copy-done.11), channel_id=1, source_target_pairs={{0,1},{1,0},{2,3},{3,2},{4,5},{5,4},{6,7},{7,6},{8,9},{9,8},{10,11... | collective-permute-start | bytes 1179656 | tf_op jit(solution)/shard_map/ppermute | solution.py:373
  69.3 11.3 %collective-permute-start.14 = (f32[72,128]{1,0:T(8,128)S(1)}, f32[72,128]{1,0:T(8,128)S(1)}, u32[]{:S(2)}, u32[]{:S(2)}) collective-permute-start(f32[72,128]{1,0:T(8,128)S(1)} %add_add_fusion.1), channel_id=1, source_target_pairs={{0,24},{8,0},{16,8},{24,16},{1,25},{9,1},{17,9},{25,17},{2,26},{10... | collective-permute-start | bytes 110600 | tf_op jit(solution)/shard_map/ppermute | solution.py:381
  71.3 9.3 %collective-permute-start.13 = (f32[72,128]{1,0:T(8,128)S(1)}, f32[72,128]{1,0:T(8,128)S(1)}, u32[]{:S(2)}, u32[]{:S(2)}) collective-permute-start(f32[72,128]{1,0:T(8,128)S(1)} %add_add_fusion.1), channel_id=1, source_target_pairs={{0,16},{8,24},{16,0},{24,8},{1,17},{9,25},{17,1},{25,9},{2,18},{10... | collective-permute-start | bytes 110600 | tf_op jit(solution)/shard_map/ppermute | solution.py:381
  72.0 8.6 %collective-permute-start.12 = (f32[72,128]{1,0:T(8,128)S(1)}, f32[72,128]{1,0:T(8,128)S(1)}, u32[]{:S(2)}, u32[]{:S(2)}) collective-permute-start(f32[72,128]{1,0:T(8,128)S(1)} %add_add_fusion.1), channel_id=1, source_target_pairs={{0,8},{8,16},{16,24},{24,0},{1,9},{9,17},{17,25},{25,1},{2,10},{10... | collective-permute-start | bytes 110600 | tf_op jit(solution)/shard_map/ppermute | solution.py:381
  72.4 0.8 copy-start.1
  75.7 14.3 %all-to-all-start.3 = ((bf16[8,128,128]{2,1,0:T(8,128)(2,1)}), bf16[8,128,128]{2,1,0:T(8,128)(2,1)S(1)}, u32[]{:S(2)}, u32[]{:S(2)}) async-start(bf16[8,128,128]{2,1,0:T(8,128)(2,1)} %route_rims.1), calls=%async_computation.3 | async-start | bytes 524288 | tf_op jit(solution)/shard_map/all_to_all | solution.py:395
  80.6 6.5 %copy-start.6 = (f32[72,128]{1,0:T(8,128)}, f32[72,128]{1,0:T(8,128)S(1)}, u32[]{:S(2)}) copy-start(f32[72,128]{1,0:T(8,128)S(1)} %add_add_fusion.w0) | copy-start | bytes 110596
  80.7 6.5 %collective-permute-start.17 = (f32[72,128]{1,0:T(8,128)S(1)}, f32[72,128]{1,0:T(8,128)S(1)}, u32[]{:S(2)}, u32[]{:S(2)}) collective-permute-start(f32[72,128]{1,0:T(8,128)S(1)} %add_add_fusion.w0), channel_id=1, source_target_pairs={{0,6},{2,4},{4,2},{6,0},{1,7},{3,5},{5,3},{7,1},{8,14},{10,12},{12... | collective-permute-start | bytes 110600 | tf_op jit(solution)/shard_map/ppermute | solution.py:377
  82.4 4.8 %collective-permute-start.16 = (f32[72,128]{1,0:T(8,128)S(1)}, f32[72,128]{1,0:T(8,128)S(1)}, u32[]{:S(2)}, u32[]{:S(2)}) collective-permute-start(f32[72,128]{1,0:T(8,128)S(1)} %add_add_fusion.w0), channel_id=1, source_target_pairs={{0,4},{2,6},{4,0},{6,2},{1,5},{3,7},{5,1},{7,3},{8,12},{10,14},{12... | collective-permute-start | bytes 110600 | tf_op jit(solution)/shard_map/ppermute | solution.py:377
  82.4 4.8 %collective-permute-start.15 = (f32[72,128]{1,0:T(8,128)S(1)}, f32[72,128]{1,0:T(8,128)S(1)}, u32[]{:S(2)}, u32[]{:S(2)}) collective-permute-start(f32[72,128]{1,0:T(8,128)S(1)} %add_add_fusion.w0), channel_id=1, source_target_pairs={{0,2},{2,0},{4,6},{6,4},{1,3},{3,1},{5,7},{7,5},{8,10},{10,8},{12,... | collective-permute-start | bytes 110600 | tf_op jit(solution)/shard_map/ppermute | solution.py:377
  87.1 0.6 copy-start.8
  87.1 0.6 copy-start.9
  87.8 0.6 copy-start.10
  90.0 0.7 copy-start.4
  90.0 0.8 copy-start.2

commit v4 on v3

--- a/solution.py
+++ b/solution.py
@@ -1,5 +1,3 @@
-import functools
-
 import jax
 import jax.numpy as jnp
 import numpy as np
@@ -198,10 +196,10 @@
         rows = slice(q * 32, q * 32 + 32)
         v = pre_s[rows, :]
         v2 = v * v
-        th = jnp.tanh(SQ * (v + 0.044715 * (v2 * v)))
-        half = 0.5 * (1.0 + th)
-        hd[rows, :] = (v * half).astype(BF)
-        d = half + 0.5 * v * (1.0 - th * th) * (SQ * (1.0 + 3 * 0.044715 * v2))
+        half = 0.5 + 0.5 * jnp.tanh(v * (SQ + (SQ * 0.044715) * v2))
+        act = v * half
+        hd[rows, :] = act.astype(BF)
+        d = half + act * (1.0 - half) * (2 * SQ + (6 * SQ * 0.044715) * v2)
         gp[rows, :] = (gh_s[rows, :] * d).astype(BF)
     gx = dot(wbt[...], gp[...])
 
@@ -351,7 +349,7 @@
         gl[:, ab // 2, ab % 2, :] = w[160 + ab * 32 : 192 + ab * 32, :]
 
 
-def call(kernel, outs, args, smem, scratch=(), name=None):
+def call(kernel, outs, args, smem, scratch=(), mib=8):
     specs = [
         pl.BlockSpec(memory_space=pltpu.SMEM if i < smem else pltpu.VMEM) for i in range(len(args))
     ]
@@ -363,8 +361,7 @@
         in_specs=specs,
         out_specs=[pl.BlockSpec(memory_space=pltpu.VMEM) for _ in shapes],
         scratch_shapes=list(scratch),
-        compiler_params=pltpu.CompilerParams(vmem_limit_bytes=58 << 20),
-        name=name,
+        compiler_params=pltpu.CompilerParams(vmem_limit_bytes=mib << 20),
     )(*args)
     return res[0] if single else res
 
@@ -395,7 +392,7 @@
     return lax.all_to_all(v, ("l", "c", "h"), 0, 0)
 
 
-def on_device(inputs, gluing, conv_weight, level_weight, cotangent):
+def level_step(inputs, gluing, conv_weight, level_weight, cotangent):
     perm, edge, pick, ends, rev = constants()
     glue = jnp.transpose(gluing, (2, 0, 1))
     strips, send = call(
@@ -403,19 +400,14 @@
         [((16, 144, 128), BF), ((32, 6144), BF)],
         (glue, inputs, cotangent, pick, ends),
         1,
-        name="strips",
+        mib=58,
     )
     rcv = swap(send)
     got = plane(strips)
     here = (lax.axis_index("z") * 4 + lax.axis_index("x")).astype(BF)
     codes = jnp.where(got[:, 128, :8] == here, got[:, 128, 8:16], -1).astype(jnp.int32).reshape(128)
     routed = call(
-        route_strips_kernel,
-        ((8, 64, 128), BF),
-        (codes, got),
-        1,
-        [pltpu.VMEM((512, 128), F32)],
-        name="route_strips",
+        route_strips_kernel, ((8, 64, 128), BF), (codes, got), 1, [pltpu.VMEM((512, 128), F32)]
     )
     halos = octet(routed)
     w9 = jnp.transpose(conv_weight, (2, 3, 0, 1))
@@ -425,7 +417,7 @@
         [((256, 1024), BF), ((1024, 256), BF), ((128, 256), BF), ((256, 128), BF)],
         (w9, lwc),
         0,
-        name="weights",
+        mib=58,
     )
     keep, back, pay, *chunks = call(
         main_kernel,
@@ -439,21 +431,19 @@
             pltpu.VMEM((256, 1024), BF), pltpu.VMEM((576, 128), F32), pltpu.VMEM((64, 4096), BF),
             pltpu.VMEM((128, 1024), BF),
         ],
-        name="main",
+        mib=58,
     )
     rims = plane(pay)
     rback = swap(back)
-    w = total([hop(chunks[k], ("l", "c", "h"), 8, k) for k in range(8)])
-    w = total([ring(w, "z", k) for k in range(4)])
-    w = total([ring(w, "x", k) for k in range(4)])
+    near = [hop(chunks[k], ("l", "c", "h"), 8, k) for k in range(8)]
+    w = total(near)
+    near = [ring(w, "z", k) for k in range(4)]
+    w = total(near)
+    near = [ring(w, "x", k) for k in range(4)]
+    w = total(near)
     parts = [hop(w, ("l", "c"), 4, k) for k in range(4)]
     outgoing = call(
-        route_rims_kernel,
-        ((8, 128, 128), BF),
-        (codes, rims),
-        1,
-        [pltpu.VMEM((1024, 128), F32)],
-        name="route_rims",
+        route_rims_kernel, ((8, 128, 128), BF), (codes, rims), 1, [pltpu.VMEM((1024, 128), F32)]
     )
     ret = octet(outgoing)
     gin, lev = call(
@@ -462,7 +452,6 @@
         (glue, ret, keep, rback, perm, edge, rev),
         1,
         [pltpu.VMEM((64, 4096), BF), pltpu.VMEM((512, 512), BF)],
-        name="final",
     )
     gc, gl = call(
         unpack_kernel,
@@ -470,7 +459,6 @@
         tuple(parts),
         0,
         [pltpu.VMEM((288, 128), F32)],
-        name="unpack",
     )
     grad_conv = jnp.transpose(gc.reshape(3, 3, 32, 64), (3, 2, 0, 1))
     grad_level = jnp.transpose(gl, (3, 0, 1, 2))
@@ -481,7 +469,7 @@
     fine = Mesh(mesh.devices.reshape(4, 4, 2, 2, 2), ("z", "x", "l", "c", "h"))
     tile = ("z", "x", "l", "c")
     return jax.shard_map(
-        on_device,
+        level_step,
         mesh=fine,
         in_specs=(
             P(tile, "h", None),

time: 94.8 us -> 88.8 us (0.937)
  local copies, waits for them, and re-layouts: 4.22 us -> 0.77 us
  Pallas kernels: 22.3 us -> 19.6 us
    unnamed x26 -> x20, local copies, waits for them, and re-layouts: 3.57 us -> 0.69 us
    pallas_call x7, Pallas kernels: 22.3 us -> 19.6 us  [call(): pl.pallas_call(kernel, out_shape=[jax.ShapeDtypeStruct(s, d) for s, d in...]
  transfers between devices with their start and end apart: 22 -> 22, of which waited for: 6 -> 6; matrix products, arithmetic and copies ran while one was open for 1% -> 0% of each run, Pallas kernels for 10% -> 9%
where the time goes in v4:
time: 88.8 us; the launch traced here: 88.2 us
  starting transfers between devices  44.7 us (50%)
  waiting for transfers between devices  22.2 us (25%)
  Pallas kernels  19.6 us (22%)
    pallas_call x7, Pallas kernels, call(): pl.pallas_call(kernel, out_shape=[jax.ShapeDtypeStruct(s, d) for s, d in...  19.6 us
    all_to_all x2, starting transfers between devices, plane(): return lax.all_to_all(v, ('z', 'x'), 0, 0)  12.3 us
    all_to_all x2, starting transfers between devices, octet(): return lax.all_to_all(v, ('l', 'c', 'h'), 0, 0)  11.7 us
    ppermute x10, starting transfers between devices, hop(): return lax.ppermute(v, axes, [(i, i ^ k) for i in range(n)]) if k else v  9.76 us
    all_to_all x2, waiting for transfers between devices, plane(): return lax.all_to_all(v, ('z', 'x'), 0, 0)  8.13 us
    ppermute x6, starting transfers between devices, ring(): lax.ppermute(v, axis, [(i, (i + k) % 4) for i in range(4)])  6.72 us
    ppermute x6, waiting for transfers between devices, ring(): lax.ppermute(v, axis, [(i, (i + k) % 4) for i in range(4)])  6.59 us
    ppermute x10, waiting for transfers between devices, hop(): return lax.ppermute(v, axes, [(i, i ^ k) for i in range(n)]) if k else v  4.39 us
  transfers between devices with their start and end apart: 22, of which 6 were waited for; matrix products, arithmetic and copies ran while one was open for 0% of the time, Pallas kernels for 9%

profile of v4, /device:TPU:1, one launch (start us, length us, event | category | flops | bytes accessed | tf_op | source)
XLA Modules:
  0.0 88.2 jit_solution(9014176923722457018)
XLA Ops:
  0.6 2.7 %shard_map.129 = (bf16[16,144,128]{2,1,0:T(8,128)(2,1)}, bf16[32,6144]{1,0:T(8,128)(2,1)}) custom-call(s32[3,2,4]{2,1,0:T(2,128)} %bitcast.9, bf16[2,32,4096]{2,1,0:T(8,128)(2,1)} %inp.3, bf16[2,64,1024]{2,1,0:T(8,128)(2,1)} %cot.3, bf16[4096,128]{1,0:T(8,128)(2,1)} %constant.26.clone.pick, bf16[256,128]{1,0:T(8,128)(2,1)} %constant.27.clone.ends), custom_call_target="tpu_custom_call" | custom-call | tf_op jit(solution)/shard_map/pallas_call | solution.py:358
  3.3 8.5 %all-to-all-start = ((bf16[16,144,128]{2,1,0:T(8,128)(2,1)}), bf16[16,144,128]{2,1,0:T(8,128)(2,1)S(1)}, u32[]{:S(2)}, u32[]{:S(2)}) async-start(bf16[16,144,128]{2,1,0:T(8,128)(2,1)} %get-tuple-element.25), calls=%async_computation | async-start | bytes 1179648 | tf_op jit(solution)/shard_map/all_to_all | solution.py:388
  11.9 3.0 %collective-permute-start = (bf16[32,6144]{1,0:T(8,128)(2,1)S(1)}, bf16[32,6144]{1,0:T(8,128)(2,1)S(1)}, u32[]{:S(2)}, u32[]{:S(2)}) collective-permute-start(bf16[32,6144]{1,0:T(8,128)(2,1)S(1)} %copy-done.9), channel_id=1, source_target_pairs={{0,1},{1,0},{2,3},{3,2},{4,5},{5,4},{6,7},{7,6},{8,9},{9,8},{10,11... | collective-permute-start | bytes 1179656 | tf_op jit(solution)/shard_map/ppermute | solution.py:370
  14.9 8.1 %all-to-all-done.got = bf16[16,144,128]{2,1,0:T(8,128)(2,1)S(1)} async-done(((bf16[16,144,128]{2,1,0:T(8,128)(2,1)}), bf16[16,144,128]{2,1,0:T(8,128)(2,1)S(1)}, u32[]{:S(2)}, u32[]{:S(2)}) %all-to-all-start) | async-done | bytes 589856 | tf_op jit(solution)/shard_map/all_to_all | solution.py:388
  23.0 0.1 fusion.1
  23.1 0.1 reshape.25.codes
  23.2 2.6 %shard_map.130 = bf16[8,64,128]{2,1,0:T(8,128)(2,1)} custom-call(s32[128]{0:T(128)S(1)} %reshape.25.codes, bf16[16,144,128]{2,1,0:T(8,128)(2,1)S(1)} %all-to-all-done.got), custom_call_target="tpu_custom_call" | custom-call | tf_op jit(solution)/shard_map/pallas_call | solution.py:358
  25.8 6.7 %all-to-all-start.1 = ((bf16[8,64,128]{2,1,0:T(8,128)(2,1)}), bf16[8,64,128]{2,1,0:T(8,128)(2,1)S(1)}, u32[]{:S(2)}, u32[]{:S(2)}) async-start(bf16[8,64,128]{2,1,0:T(8,128)(2,1)} %shard_map.130), calls=%async_computation.1 | async-start | bytes 262144 | tf_op jit(solution)/shard_map/all_to_all | solution.py:392
  32.4 2.2 %shard_map.131 = (bf16[256,1024]{1,0:T(8,128)(2,1)}, bf16[1024,256]{1,0:T(8,128)(2,1)}, bf16[128,256]{1,0:T(8,128)(2,1)}, bf16[256,128]{1,0:T(8,128)(2,1)}) custom-call(bf16[3,3,64,64]{3,2,1,0:T(8,128)(2,1)} %bitcast.12, bf16[256,128]{1,0:T(8,128)(2,1)} %bitcast.13), custom_call_target="tpu_custom_call" | custom-call | tf_op jit(solution)/shard_map/pallas_call | solution.py:358
  34.6 0.0 collective-permute-done.rcv
  34.6 3.0 %all-to-all-done.1.halo = bf16[8,64,128]{2,1,0:T(8,128)(2,1)S(1)} async-done(((bf16[8,64,128]{2,1,0:T(8,128)(2,1)}), bf16[8,64,128]{2,1,0:T(8,128)(2,1)S(1)}, u32[]{:S(2)}, u32[]{:S(2)}) %all-to-all-start.1) | async-done | bytes 131104 | tf_op jit(solution)/shard_map/all_to_all | solution.py:392
  37.7 0.7 copy-done.5
  38.3 7.1 %shard_map.132 = (bf16[32,6144]{1,0:T(8,128)(2,1)}, bf16[32,6144]{1,0:T(8,128)(2,1)}, bf16[16,128,128]{2,1,0:T(8,128)(2,1)}, f32[72,128]{1,0:T(8,128)}, f32[72,1...) custom-call(s32[3,2,4]{2,1,0:T(2,128)} %bitcast.10, ...), custom_call_target="tpu_custom_call" | custom-call | tf_op jit(solution)/shard_map/pallas_call | solution.py:358
  45.4 0.8 collective-permute-start.2
  46.2 1.3 %collective-permute-start.3 = (f32[72,128]{1,0:T(8,128)}, f32[72,128]{1,0:T(8,128)S(1)}, u32[]{:S(2)}, u32[]{:S(2)}) collective-permute-start(f32[72,128]{1,0:T(8,128)} %get-tuple-element.38), channel_id=1, source_target_pairs={{0,2},{1,3},{2,0},{3,1},{4,6},{5,7},{6,4},{7,5},{8,10},{9,11},{10,... | collective-permute-start | bytes 110600 | tf_op jit(solution)/shard_map/ppermute | solution.py:374
  47.5 1.4 %collective-permute-start.4 = (f32[72,128]{1,0:T(8,128)}, f32[72,128]{1,0:T(8,128)S(1)}, u32[]{:S(2)}, u32[]{:S(2)}) collective-permute-start(f32[72,128]{1,0:T(8,128)} %get-tuple-element.39), channel_id=1, source_target_pairs={{0,3},{1,2},{2,1},{3,0},{4,7},{5,6},{6,5},{7,4},{8,11},{9,10},{10,... | collective-permute-start | bytes 110600 | tf_op jit(solution)/shard_map/ppermute | solution.py:374
  48.9 0.3 collective-permute-start.5
  49.2 1.4 %collective-permute-start.6 = (f32[72,128]{1,0:T(8,128)}, f32[72,128]{1,0:T(8,128)S(1)}, u32[]{:S(2)}, u32[]{:S(2)}) collective-permute-start(f32[72,128]{1,0:T(8,128)} %get-tuple-element.41), channel_id=1, source_target_pairs={{0,5},{1,4},{2,7},{3,6},{4,1},{5,0},{6,3},{7,2},{8,13},{9,12},{10,... | collective-permute-start | bytes 110600 | tf_op jit(solution)/shard_map/ppermute | solution.py:374
  50.7 0.0 collective-permute-done.2
  50.7 1.4 %collective-permute-start.7 = (f32[72,128]{1,0:T(8,128)}, f32[72,128]{1,0:T(8,128)S(1)}, u32[]{:S(2)}, u32[]{:S(2)}) collective-permute-start(f32[72,128]{1,0:T(8,128)} %get-tuple-element.42), channel_id=1, source_target_pairs={{0,6},{1,7},{2,4},{3,5},{4,2},{5,3},{6,0},{7,1},{8,14},{9,15},{10,... | collective-permute-start | bytes 110600 | tf_op jit(solution)/shard_map/ppermute | solution.py:374
  52.0 0.0 collective-permute-done.3
  52.0 0.9 %collective-permute-start.8 = (f32[72,128]{1,0:T(8,128)}, f32[72,128]{1,0:T(8,128)S(1)}, u32[]{:S(2)}, u32[]{:S(2)}) collective-permute-start(f32[72,128]{1,0:T(8,128)} %get-tuple-element.43), channel_id=1, source_target_pairs={{0,7},{1,6},{2,5},{3,4},{4,3},{5,2},{6,1},{7,0},{8,15},{9,14},{10,... | collective-permute-start | bytes 110600 | tf_op jit(solution)/shard_map/ppermute | solution.py:374
  53.0 3.7 %all-to-all-start.2 = ((bf16[16,128,128]{2,1,0:T(8,128)(2,1)}), bf16[16,128,128]{2,1,0:T(8,128)(2,1)S(1)}, u32[]{:S(2)}, u32[]{:S(2)}) async-start(bf16[16,128,128]{2,1,0:T(8,128)(2,1)} %get-tuple-element.31), calls=%async_computation.2 | async-start | bytes 1048576 | tf_op jit(solution)/shard_map/all_to_all | solution.py:388
  56.7 0.0 collective-permute-done.4
  56.7 0.0 collective-permute-done.5
  56.7 0.0 collective-permute-done.7
  56.7 0.1 collective-permute-done.8
  56.8 2.5 %collective-permute-start.11 = (f32[72,128]{1,0:T(8,128)S(1)}, f32[72,128]{1,0:T(8,128)S(1)}, u32[]{:S(2)}, u32[]{:S(2)}) collective-permute-start(f32[72,128]{1,0:T(8,128)S(1)} %add_add_fusion.2), channel_id=1, source_target_pairs={{0,96},{32,0},{64,32},{96,64},{1,97},{33,1},{65,33},{97,65},{2,98}... | collective-permute-start | bytes 110600 | tf_op jit(solution)/shard_map/ppermute | solution.py:378
  59.4 0.5 collective-permute-start.10
  59.9 0.6 collective-permute-start.9
  60.5 1.2 %collective-permute-start.1 = (bf16[32,6144]{1,0:T(8,128)(2,1)S(1)}, bf16[32,6144]{1,0:T(8,128)(2,1)S(1)}, u32[]{:S(2)}, u32[]{:S(2)}) collective-permute-start(bf16[32,6144]{1,0:T(8,128)(2,1)S(1)} %copy-done.8), channel_id=1, source_target_pairs={{0,1},{1,0},{2,3},{3,2},{4,5},{5,4},{6,7},{7,6},{8,9},{9,8},{10,11... | collective-permute-start | bytes 1179656 | tf_op jit(solution)/shard_map/ppermute | solution.py:370
  61.7 5.7 %collective-permute-done.10 = f32[72,128]{1,0:T(8,128)S(1)} collective-permute-done((f32[72,128]{1,0:T(8,128)S(1)}, f32[72,128]{1,0:T(8,128)S(1)}, u32[]{:S(2)}, u32[]{:S(2)}) %collective-permute-start.10) | collective-permute-done | bytes 36896 | tf_op jit(solution)/shard_map/ppermute | solution.py:378
  67.4 0.9 collective-permute-done.9
  68.3 2.0 %collective-permute-start.14 = (f32[72,128]{1,0:T(8,128)S(1)}, f32[72,128]{1,0:T(8,128)S(1)}, u32[]{:S(2)}, u32[]{:S(2)}) collective-permute-start(f32[72,128]{1,0:T(8,128)S(1)} %add_add_fusion.1), channel_id=1, source_target_pairs={{0,24},{8,0},{16,8},{24,16},{1,25},{9,1},{17,9},{25,17},{2,26},{10... | collective-permute-start | bytes 110600 | tf_op jit(solution)/shard_map/ppermute | solution.py:378
  70.3 0.7 collective-permute-start.13
  71.0 0.4 collective-permute-start.12
  71.4 2.1 %shard_map.133 = bf16[8,128,128]{2,1,0:T(8,128)(2,1)} custom-call(s32[128]{0:T(128)S(1)} %reshape.25.codes, bf16[16,128,128]{2,1,0:T(8,128)(2,1)S(1)} %all-to-all-done.2.got), custom_call_target="tpu_custom_call" | custom-call | tf_op jit(solution)/shard_map/pallas_call | solution.py:358
  73.5 5.1 %all-to-all-start.3 = ((bf16[8,128,128]{2,1,0:T(8,128)(2,1)}), bf16[8,128,128]{2,1,0:T(8,128)(2,1)S(1)}, u32[]{:S(2)}, u32[]{:S(2)}) async-start(bf16[8,128,128]{2,1,0:T(8,128)(2,1)} %shard_map.133), calls=%async_computation.3 | async-start | bytes 524288 | tf_op jit(solution)/shard_map/all_to_all | solution.py:392
  78.6 0.0 collective-permute-done.14
  78.6 0.0 collective-permute-done.13
  78.6 0.0 copy-start.3
  78.7 1.7 %collective-permute-start.17 = (f32[72,128]{1,0:T(8,128)S(1)}, f32[72,128]{1,0:T(8,128)S(1)}, u32[]{:S(2)}, u32[]{:S(2)}) collective-permute-start(f32[72,128]{1,0:T(8,128)S(1)} %add_add_fusion.w0), channel_id=1, source_target_pairs={{0,6},{2,4},{4,2},{6,0},{1,7},{3,5},{5,3},{7,1},{8,14},{10,12},{12... | collective-permute-start | bytes 110600 | tf_op jit(solution)/shard_map/ppermute | solution.py:374
  80.4 0.0 collective-permute-start.16
  80.4 0.5 collective-permute-start.15
  80.9 4.3 %collective-permute-done.17.w3 = f32[72,128]{1,0:T(8,128)S(1)} collective-permute-done((f32[72,128]{1,0:T(8,128)S(1)}, f32[72,128]{1,0:T(8,128)S(1)}, u32[]{:S(2)}, u32[]{:S(2)}) %collective-permute-start.17) | collective-permute-done | bytes 36896 | tf_op jit(solution)/shard_map/ppermute | solution.py:374
  85.1 0.0 collective-permute-done.16.w2
  85.1 0.8 shard_map.135
  86.0 2.2 %shard_map.134 = (bf16[2,32,4096]{2,1,0:T(8,128)(2,1)}, bf16[2,64,1024]{2,1,0:T(8,128)(2,1)}) custom-call(s32[3,2,4]{2,1,0:T(2,128)S(1)} %bitcast.11, bf16[8,128,128]{2,1,0:T(8,128)(2,1)S(1)} %all-to-all-done.3.ret, bf16[32,6144]{1,0:T(8,128)(2,1)S(1)} %copy-done.2, bf16[32,6144]{1,0:T(8,128)(2,1)S(1)} %collective-permute-done.1.rcv, ...), custom_call_target="tpu_custom_call" | custom-call | tf_op jit(solution)/shard_map/pallas_call | solution.py:358
  (28 shorter events, 0.1 us)
Async XLA Ops:
  3.3 8.6 %copy-start.9 = (bf16[32,6144]{1,0:T(8,128)(2,1)S(1)}, bf16[32,6144]{1,0:T(8,128)(2,1)}, u32[]{:S(2)}) copy-start(bf16[32,6144]{1,0:T(8,128)(2,1)} %get-tuple-element.26) | copy-start | bytes 1179652
  3.3 19.7 %all-to-all-start = ((bf16[16,144,128]{2,1,0:T(8,128)(2,1)}), bf16[16,144,128]{2,1,0:T(8,128)(2,1)S(1)}, u32[]{:S(2)}, u32[]{:S(2)}) async-start(bf16[16,144,128]{2,1,0:T(8,128)(2,1)} %get-tuple-element.25), calls=%async_computation | async-start | bytes 1179648 | tf_op jit(solution)/shard_map/all_to_all | solution.py:388
  11.9 22.7 %collective-permute-start = (bf16[32,6144]{1,0:T(8,128)(2,1)S(1)}, bf16[32,6144]{1,0:T(8,128)(2,1)S(1)}, u32[]{:S(2)}, u32[]{:S(2)}) collective-permute-start(bf16[32,6144]{1,0:T(8,128)(2,1)S(1)} %copy-done.9), channel_id=1, source_target_pairs={{0,1},{1,0},{2,3},{3,2},{4,5},{5,4},{6,7},{7,6},{8,9},{9,8},{10,11... | collective-permute-start | bytes 1179656 | tf_op jit(solution)/shard_map/ppermute | solution.py:370
  25.8 11.9 %all-to-all-start.1 = ((bf16[8,64,128]{2,1,0:T(8,128)(2,1)}), bf16[8,64,128]{2,1,0:T(8,128)(2,1)S(1)}, u32[]{:S(2)}, u32[]{:S(2)}) async-start(bf16[8,64,128]{2,1,0:T(8,128)(2,1)} %shard_map.130), calls=%async_computation.1 | async-start | bytes 262144 | tf_op jit(solution)/shard_map/all_to_all | solution.py:392
  34.6 3.1 %copy-start.6 = (bf16[32,6144]{1,0:T(8,128)(2,1)}, bf16[32,6144]{1,0:T(8,128)(2,1)S(1)}, u32[]{:S(2)}) copy-start(bf16[32,6144]{1,0:T(8,128)(2,1)S(1)} %collective-permute-done.rcv) | copy-start | bytes 1179652
  37.7 0.7 copy-start.5
  45.4 5.3 %collective-permute-start.2 = (f32[72,128]{1,0:T(8,128)}, f32[72,128]{1,0:T(8,128)S(1)}, u32[]{:S(2)}, u32[]{:S(2)}) collective-permute-start(f32[72,128]{1,0:T(8,128)} %get-tuple-element.37), channel_id=1, source_target_pairs={{0,1},{1,0},{2,3},{3,2},{4,5},{5,4},{6,7},{7,6},{8,9},{9,8},{10,11... | collective-permute-start | bytes 110600 | tf_op jit(solution)/shard_map/ppermute | solution.py:374
  46.2 5.8 %collective-permute-start.3 = (f32[72,128]{1,0:T(8,128)}, f32[72,128]{1,0:T(8,128)S(1)}, u32[]{:S(2)}, u32[]{:S(2)}) collective-permute-start(f32[72,128]{1,0:T(8,128)} %get-tuple-element.38), channel_id=1, source_target_pairs={{0,2},{1,3},{2,0},{3,1},{4,6},{5,7},{6,4},{7,5},{8,10},{9,11},{10,... | collective-permute-start | bytes 110600 | tf_op jit(solution)/shard_map/ppermute | solution.py:374
  47.5 9.2 %collective-permute-start.4 = (f32[72,128]{1,0:T(8,128)}, f32[72,128]{1,0:T(8,128)S(1)}, u32[]{:S(2)}, u32[]{:S(2)}) collective-permute-start(f32[72,128]{1,0:T(8,128)} %get-tuple-element.39), channel_id=1, source_target_pairs={{0,3},{1,2},{2,1},{3,0},{4,7},{5,6},{6,5},{7,4},{8,11},{9,10},{10,... | collective-permute-start | bytes 110600 | tf_op jit(solution)/shard_map/ppermute | solution.py:374
  48.9 7.7 %collective-permute-start.5 = (f32[72,128]{1,0:T(8,128)}, f32[72,128]{1,0:T(8,128)S(1)}, u32[]{:S(2)}, u32[]{:S(2)}) collective-permute-start(f32[72,128]{1,0:T(8,128)} %get-tuple-element.40), channel_id=1, source_target_pairs={{0,4},{1,5},{2,6},{3,7},{4,0},{5,1},{6,2},{7,3},{8,12},{9,13},{10,... | collective-permute-start | bytes 110600 | tf_op jit(solution)/shard_map/ppermute | solution.py:374
  49.2 7.5 %collective-permute-start.6 = (f32[72,128]{1,0:T(8,128)}, f32[72,128]{1,0:T(8,128)S(1)}, u32[]{:S(2)}, u32[]{:S(2)}) collective-permute-start(f32[72,128]{1,0:T(8,128)} %get-tuple-element.41), channel_id=1, source_target_pairs={{0,5},{1,4},{2,7},{3,6},{4,1},{5,0},{6,3},{7,2},{8,13},{9,12},{10,... | collective-permute-start | bytes 110600 | tf_op jit(solution)/shard_map/ppermute | solution.py:374
  50.7 6.0 %collective-permute-start.7 = (f32[72,128]{1,0:T(8,128)}, f32[72,128]{1,0:T(8,128)S(1)}, u32[]{:S(2)}, u32[]{:S(2)}) collective-permute-start(f32[72,128]{1,0:T(8,128)} %get-tuple-element.42), channel_id=1, source_target_pairs={{0,6},{1,7},{2,4},{3,5},{4,2},{5,3},{6,0},{7,1},{8,14},{9,15},{10,... | collective-permute-start | bytes 110600 | tf_op jit(solution)/shard_map/ppermute | solution.py:374
  52.0 4.8 %collective-permute-start.8 = (f32[72,128]{1,0:T(8,128)}, f32[72,128]{1,0:T(8,128)S(1)}, u32[]{:S(2)}, u32[]{:S(2)}) collective-permute-start(f32[72,128]{1,0:T(8,128)} %get-tuple-element.43), channel_id=1, source_target_pairs={{0,7},{1,6},{2,5},{3,4},{4,3},{5,2},{6,1},{7,0},{8,15},{9,14},{10,... | collective-permute-start | bytes 110600 | tf_op jit(solution)/shard_map/ppermute | solution.py:374
  53.0 3.9 %copy-start.7 = (f32[72,128]{1,0:T(8,128)S(1)}, f32[72,128]{1,0:T(8,128)}, u32[]{:S(2)}) copy-start(f32[72,128]{1,0:T(8,128)} %get-tuple-element.36) | copy-start | bytes 110596
  53.0 7.5 %copy-start.8 = (bf16[32,6144]{1,0:T(8,128)(2,1)S(1)}, bf16[32,6144]{1,0:T(8,128)(2,1)}, u32[]{:S(2)}) copy-start(bf16[32,6144]{1,0:T(8,128)(2,1)} %get-tuple-element.33) | copy-start | bytes 1179652
  53.0 18.4 %all-to-all-start.2 = ((bf16[16,128,128]{2,1,0:T(8,128)(2,1)}), bf16[16,128,128]{2,1,0:T(8,128)(2,1)S(1)}, u32[]{:S(2)}, u32[]{:S(2)}) async-start(bf16[16,128,128]{2,1,0:T(8,128)(2,1)} %get-tuple-element.31), calls=%async_computation.2 | async-start | bytes 1048576 | tf_op jit(solution)/shard_map/all_to_all | solution.py:388
  56.8 4.9 %collective-permute-start.11 = (f32[72,128]{1,0:T(8,128)S(1)}, f32[72,128]{1,0:T(8,128)S(1)}, u32[]{:S(2)}, u32[]{:S(2)}) collective-permute-start(f32[72,128]{1,0:T(8,128)S(1)} %add_add_fusion.2), channel_id=1, source_target_pairs={{0,96},{32,0},{64,32},{96,64},{1,97},{33,1},{65,33},{97,65},{2,98}... | collective-permute-start | bytes 110600 | tf_op jit(solution)/shard_map/ppermute | solution.py:378
  59.4 8.1 %collective-permute-start.10 = (f32[72,128]{1,0:T(8,128)S(1)}, f32[72,128]{1,0:T(8,128)S(1)}, u32[]{:S(2)}, u32[]{:S(2)}) collective-permute-start(f32[72,128]{1,0:T(8,128)S(1)} %add_add_fusion.2), channel_id=1, source_target_pairs={{0,64},{32,96},{64,0},{96,32},{1,65},{33,97},{65,1},{97,33},{2,66}... | collective-permute-start | bytes 110600 | tf_op jit(solution)/shard_map/ppermute | solution.py:378
  59.9 8.4 %collective-permute-start.9 = (f32[72,128]{1,0:T(8,128)S(1)}, f32[72,128]{1,0:T(8,128)S(1)}, u32[]{:S(2)}, u32[]{:S(2)}) collective-permute-start(f32[72,128]{1,0:T(8,128)S(1)} %add_add_fusion.2), channel_id=1, source_target_pairs={{0,32},{32,64},{64,96},{96,0},{1,33},{33,65},{65,97},{97,1},{2,34}... | collective-permute-start | bytes 110600 | tf_op jit(solution)/shard_map/ppermute | solution.py:378
  60.5 25.4 %collective-permute-start.1 = (bf16[32,6144]{1,0:T(8,128)(2,1)S(1)}, bf16[32,6144]{1,0:T(8,128)(2,1)S(1)}, u32[]{:S(2)}, u32[]{:S(2)}) collective-permute-start(bf16[32,6144]{1,0:T(8,128)(2,1)S(1)} %copy-done.8), channel_id=1, source_target_pairs={{0,1},{1,0},{2,3},{3,2},{4,5},{5,4},{6,7},{7,6},{8,9},{9,8},{10,11... | collective-permute-start | bytes 1179656 | tf_op jit(solution)/shard_map/ppermute | solution.py:370
  68.3 10.3 %collective-permute-start.14 = (f32[72,128]{1,0:T(8,128)S(1)}, f32[72,128]{1,0:T(8,128)S(1)}, u32[]{:S(2)}, u32[]{:S(2)}) collective-permute-start(f32[72,128]{1,0:T(8,128)S(1)} %add_add_fusion.1), channel_id=1, source_target_pairs={{0,24},{8,0},{16,8},{24,16},{1,25},{9,1},{17,9},{25,17},{2,26},{10... | collective-permute-start | bytes 110600 | tf_op jit(solution)/shard_map/ppermute | solution.py:378
  70.3 8.3 %collective-permute-start.13 = (f32[72,128]{1,0:T(8,128)S(1)}, f32[72,128]{1,0:T(8,128)S(1)}, u32[]{:S(2)}, u32[]{:S(2)}) collective-permute-start(f32[72,128]{1,0:T(8,128)S(1)} %add_add_fusion.1), channel_id=1, source_target_pairs={{0,16},{8,24},{16,0},{24,8},{1,17},{9,25},{17,1},{25,9},{2,18},{10... | collective-permute-start | bytes 110600 | tf_op jit(solution)/shard_map/ppermute | solution.py:378
  71.0 7.6 %collective-permute-start.12 = (f32[72,128]{1,0:T(8,128)S(1)}, f32[72,128]{1,0:T(8,128)S(1)}, u32[]{:S(2)}, u32[]{:S(2)}) collective-permute-start(f32[72,128]{1,0:T(8,128)S(1)} %add_add_fusion.1), channel_id=1, source_target_pairs={{0,8},{8,16},{16,24},{24,0},{1,9},{9,17},{17,25},{25,1},{2,10},{10... | collective-permute-start | bytes 110600 | tf_op jit(solution)/shard_map/ppermute | solution.py:378
  71.4 14.5 %copy-start.1 = (bf16[512,512]{1,0:T(8,128)(2,1)S(1)}, bf16[512,512]{1,0:T(8,128)(2,1)}, u32[]{:S(2)}) copy-start(bf16[512,512]{1,0:T(8,128)(2,1)} %constant.24.clone.perm) | copy-start | bytes 1572868
  71.4 14.5 %copy-start.2 = (bf16[32,6144]{1,0:T(8,128)(2,1)S(1)}, bf16[32,6144]{1,0:T(8,128)(2,1)}, u32[]{:S(2)}) copy-start(bf16[32,6144]{1,0:T(8,128)(2,1)} %get-tuple-element.32.keep) | copy-start | bytes 1179652
  73.5 12.4 %copy-start = (bf16[128,2048]{1,0:T(8,128)(2,1)S(1)}, bf16[128,2048]{1,0:T(8,128)(2,1)}, u32[]{:S(2)}) copy-start(bf16[128,2048]{1,0:T(8,128)(2,1)} %constant.25.clone.edge) | copy-start | bytes 1572868
  73.5 12.4 %all-to-all-start.3 = ((bf16[8,128,128]{2,1,0:T(8,128)(2,1)}), bf16[8,128,128]{2,1,0:T(8,128)(2,1)S(1)}, u32[]{:S(2)}, u32[]{:S(2)}) async-start(bf16[8,128,128]{2,1,0:T(8,128)(2,1)} %shard_map.133), calls=%async_computation.3 | async-start | bytes 524288 | tf_op jit(solution)/shard_map/all_to_all | solution.py:392
  78.6 7.3 %copy-start.3 = (bf16[128,128]{1,0:T(8,128)(2,1)S(1)}, bf16[128,128]{1,0:T(8,128)(2,1)}, u32[]{:S(2)}) copy-start(bf16[128,128]{1,0:T(8,128)(2,1)} %constant.28.clone.rev) | copy-start | bytes 98308
  78.7 6.5 %collective-permute-start.17 = (f32[72,128]{1,0:T(8,128)S(1)}, f32[72,128]{1,0:T(8,128)S(1)}, u32[]{:S(2)}, u32[]{:S(2)}) collective-permute-start(f32[72,128]{1,0:T(8,128)S(1)} %add_add_fusion.w0), channel_id=1, source_target_pairs={{0,6},{2,4},{4,2},{6,0},{1,7},{3,5},{5,3},{7,1},{8,14},{10,12},{12... | collective-permute-start | bytes 110600 | tf_op jit(solution)/shard_map/ppermute | solution.py:374
  80.4 4.8 %collective-permute-start.16 = (f32[72,128]{1,0:T(8,128)S(1)}, f32[72,128]{1,0:T(8,128)S(1)}, u32[]{:S(2)}, u32[]{:S(2)}) collective-permute-start(f32[72,128]{1,0:T(8,128)S(1)} %add_add_fusion.w0), channel_id=1, source_target_pairs={{0,4},{2,6},{4,0},{6,2},{1,5},{3,7},{5,1},{7,3},{8,12},{10,14},{12... | collective-permute-start | bytes 110600 | tf_op jit(solution)/shard_map/ppermute | solution.py:374
  80.4 4.8 %collective-permute-start.15 = (f32[72,128]{1,0:T(8,128)S(1)}, f32[72,128]{1,0:T(8,128)S(1)}, u32[]{:S(2)}, u32[]{:S(2)}) collective-permute-start(f32[72,128]{1,0:T(8,128)S(1)} %add_add_fusion.w0), channel_id=1, source_target_pairs={{0,2},{2,0},{4,6},{6,4},{1,3},{3,1},{5,7},{7,5},{8,10},{10,8},{12,... | collective-permute-start | bytes 110600 | tf_op jit(solution)/shard_map/ppermute | solution.py:374
  85.1 0.8 copy-start.4
